TPU v7x, 768 devices: a whole 4x8x12 slice. The times are simulated.
768 devices in a mesh: gx: 32 (over x, z_lo, core), gy: 3 (over z_hi), gz: 8 (over y).
Axes of the slice: x: 4, y: 8, z: 12 (z_hi: 3, z_lo: 4; z = z_hi * 4 + z_lo), core: 2. Of those that a mesh axis runs over, the one named last changes fastest.
Arguments:
- energy: float32 [192, 36, 1536], P('gx', 'gy', 'gz'), may hold values from 0.5 to 18, as said below
- density: float32 [64, 12, 512], P('gx', 'gy', 'gz'), may hold values from 0.125 to 1
- region: int32 [64, 12, 512], P('gx', 'gy', 'gz'), may hold values from 0 to 2
- gamma_table: float32 [3], replicated, may hold values from 1.3 to 1.9
Outputs:
- acceleration: float32 [3, 128, 24, 1024], P(None, 'gx', 'gy', 'gz')
- residual: float32 [3, 128, 24, 1024], P(None, 'gx', 'gy', 'gz')
Inputs may be any that keep to these rules, and one draw needn't show every extreme that they name: energy is positive.
All inputs are finite; a program needn't handle non-finite values.
Results may differ from a plain program's by a relative error of at most 0.0001.
Values sent between devices are 32-bit elements; how exact they have to be, the bound alone decides.
No kernel may reach another device: no remote copies, remote signals or barrier semaphores. Data moves between devices by JAX's collectives and lax.ppermute only.
A program may use at most 32 MiB of HBM per device.

v0:
```python
import math

import jax
import jax.numpy as jnp
from jax import lax
from jax.sharding import PartitionSpec as P

ITERS = 2


WEIGHTS = [5.0 / 18.0, 8.0 / 18.0, 5.0 / 18.0]


def shifted(value, axis, by):
    count = lax.axis_size(axis)
    pairs = [(i, i + by) for i in range(count) if 0 <= i + by < count]
    return lax.ppermute(value, axis, pairs)


def padded_2(block, sides, width):
    for axis, dim in sides:
        count = lax.axis_size(axis)
        forward = [(i, i + 1) for i in range(count - 1)]
        backward = [(target, source) for source, target in forward]
        low = lax.ppermute(
            lax.slice_in_dim(block, block.shape[dim] - width, None, axis=dim), axis, forward
        )
        high = lax.ppermute(lax.slice_in_dim(block, 0, width, axis=dim), axis, backward)
        block = jnp.concatenate([low, block, high], axis=dim)
    return block


def line_tables():
    root = math.sqrt(0.15)
    spots = [0.5 - root, 0.5, 0.5 + root]
    values = [
        [2.0 * (spot - 0.5) * (spot - 1.0), -4.0 * spot * (spot - 1.0), 2.0 * spot * (spot - 0.5)]
        for spot in spots
    ]
    slopes = [[4.0 * spot - 3.0, -8.0 * spot + 4.0, 4.0 * spot - 1.0] for spot in spots]
    return (values, slopes)


def to_points(field, axis, table):
    count = (field.shape[axis] - 1) // 2
    parts = [
        lax.slice_in_dim(field, offset, offset + 2 * count - 1, 2, axis) for offset in range(3)
    ]
    rows = [
        table[member][0] * parts[0] + table[member][1] * parts[1] + table[member][2] * parts[2]
        for member in range(3)
    ]
    joined = jnp.stack(rows, axis=axis + 1)
    shape_values = list(field.shape)
    shape_values[axis] = 3 * count
    return joined.reshape(shape_values)


def to_nodes(points, axis, table):
    count = points.shape[axis] // 3
    shape_values = list(points.shape)
    grouped = points.reshape(shape_values[:axis] + [count, 3] + shape_values[axis + 1 :])
    parts = [lax.index_in_dim(grouped, member, axis + 1, keepdims=False) for member in range(3)]
    terms = [
        table[0][offset] * parts[0] + table[1][offset] * parts[1] + table[2][offset] * parts[2]
        for offset in range(3)
    ]
    widths_end = [(0, 0)] * len(shape_values)
    widths_end[axis] = (0, 1)
    widths_front = [(0, 0)] * len(shape_values)
    widths_front[axis] = (1, 0)
    evens = jnp.pad(terms[0], widths_end) + jnp.pad(terms[2], widths_front)
    woven = jnp.stack([lax.slice_in_dim(evens, 0, count, 1, axis), terms[1]], axis=axis + 1)
    shape_two = list(terms[1].shape)
    shape_two[axis] = 2 * count
    woven = woven.reshape(shape_two)
    return jnp.concatenate([woven, lax.slice_in_dim(evens, count, count + 1, 1, axis)], axis=axis)


def mass_apply(nodes, coef):
    values, slopes = line_tables()
    points = to_points(to_points(to_points(nodes, 0, values), 1, values), 2, values)
    points = points * coef
    return to_nodes(to_nodes(to_nodes(points, 2, values), 1, values), 0, values)


def force_contributions(pressure_weighted):
    values, slopes = line_tables()
    force_x = to_nodes(to_nodes(to_nodes(pressure_weighted, 0, slopes), 1, values), 2, values)
    force_y = to_nodes(to_nodes(to_nodes(pressure_weighted, 0, values), 1, slopes), 2, values)
    force_z = to_nodes(to_nodes(to_nodes(pressure_weighted, 0, values), 1, values), 2, slopes)
    return jnp.stack([force_x, force_y, force_z])


def expand(values):
    return jnp.repeat(jnp.repeat(jnp.repeat(values, 3, 0), 3, 1), 3, 2)


def weight_grid(count_x, count_y, count_z):
    line_entries = jnp.array(WEIGHTS, jnp.float32)
    return (
        jnp.tile(line_entries, count_x)[:, None, None]
        * jnp.tile(line_entries, count_y)[None, :, None]
        * jnp.tile(line_entries, count_z)[None, None, :]
    )


def lookup(region, gamma_table):
    gamma_elem = jnp.zeros(region.shape, gamma_table.dtype)
    for index in range(gamma_table.shape[0]):
        gamma_elem = gamma_elem + jnp.where(region == index, gamma_table[index], 0.0)
    return gamma_elem


def wall_mask(count_x, count_y, count_z):
    mask_x = (lax.axis_index("gx") * (2 * count_x) + jnp.arange(2 * count_x) != 0).astype(
        jnp.float32
    )
    mask_y = (lax.axis_index("gy") * (2 * count_y) + jnp.arange(2 * count_y) != 0).astype(
        jnp.float32
    )
    depth_mask = (lax.axis_index("gz") * (2 * count_z) + jnp.arange(2 * count_z) != 0).astype(
        jnp.float32
    )
    return (mask_x[:, None, None] * mask_y[None, :, None] * depth_mask[None, None, :])[None]


def lower_rim(stacked):
    arrived = shifted(stacked[:, -3:], "gx", 1)
    stacked = jnp.concatenate([arrived, stacked], axis=1)
    arrived = shifted(stacked[:, :, -3:], "gy", 1)
    stacked = jnp.concatenate([arrived, stacked], axis=2)
    arrived = shifted(stacked[:, :, :, -3:], "gz", 1)
    return jnp.concatenate([arrived, stacked], axis=3)


def local_sum(left, right):
    return jnp.sum(left * right, axis=(1, 2, 3))


def residual_norms(residual):
    return lax.psum(local_sum(residual, residual), ("gx", "gy", "gz"))


def on_device(energy, density, region, gamma_table):
    count_x, count_y, count_z = density.shape
    quadrature_weights = weight_grid(count_x, count_y, count_z)
    gamma_elem = lookup(region, gamma_table)
    pressure_weighted = expand((gamma_elem - 1.0) * density) * energy * quadrature_weights
    boundary_mask = wall_mask(count_x, count_y, count_z)
    coef_own = expand(density) * quadrature_weights
    extended = lower_rim(jnp.stack([pressure_weighted, coef_own]))
    pressure_pad = extended[0]
    coef = extended[1]
    corner_force = (
        force_contributions(pressure_pad)[
            :, 2 : 2 * count_x + 2, 2 : 2 * count_y + 2, 2 : 2 * count_z + 2
        ]
        * boundary_mask
    )
    solution = jnp.zeros_like(corner_force)
    residual = corner_force
    direction = corner_force
    norm_now = residual_norms(residual)
    for step in range(ITERS):
        padded = padded_2(direction, (("gx", 1), ("gy", 2), ("gz", 3)), 2)
        padded = padded[:, : 2 * count_x + 3, : 2 * count_y + 3, : 2 * count_z + 3]
        outcome_field = jnp.stack([mass_apply(padded[member], coef) for member in range(3)])
        image = (
            outcome_field[:, 2 : 2 * count_x + 2, 2 : 2 * count_y + 2, 2 : 2 * count_z + 2]
            * boundary_mask
        )
        alpha = norm_now / lax.psum(local_sum(direction, image), ("gx", "gy", "gz"))
        solution = solution + alpha[:, None, None, None] * direction
        residual = residual - alpha[:, None, None, None] * image
        if step + 1 < ITERS:
            norm_next = residual_norms(residual)
            direction = residual + (norm_next / norm_now)[:, None, None, None] * direction
            norm_now = norm_next
    return (solution, residual)


def solution(mesh):
    in_specs = (P("gx", "gy", "gz"), P("gx", "gy", "gz"), P("gx", "gy", "gz"), P())
    out_specs = (P(None, "gx", "gy", "gz"), P(None, "gx", "gy", "gz"))
    return jax.shard_map(
        on_device, mesh=mesh, in_specs=in_specs, out_specs=out_specs, check_vma=False
    )
```

profile of v0, /device:TPU:35, one launch (start us, length us, event | category | flops | bytes accessed | tf_op | source)
XLA Modules:
  0.0 497.5 jit_solution(4007526236622933557)
XLA Ops:
  1.4 1.4 fusion.142
  3.5 2.6 add_multiply_fusion
  10.5 4.6 collective-permute-start
  15.2 1.3 collective-permute-done
  16.5 10.6 %collective-permute-start.1 = (f32[2,9,3,192]{3,0,2,1:T(2,128)S(1)}, f32[2,9,3,192]{3,0,2,1:T(2,128)S(1)}, u32[]{:S(2)}, u32[]{:S(2)}) collective-permute-start(f32[2,9,3,192]{3,0,2,1:T(2,128)S(1)} %pad_maximum_fusion.66), channel_id=1, source_target_pairs={{0,8},{8,16},{1,9},{9,17},{2,10},{10,18},{3,11},{11,19},{4,12},{12... | collective-permute-start | bytes 124424 | tf_op jit(solution)/shard_map/ppermute | solution.py:17
  27.1 1.2 collective-permute-done.1
  28.6 2.3 collective-permute-start.2
  31.0 4.6 collective-permute-done.2
  46.6 6.3 %collective-permute-start.3 = (f32[3,2,8,128]{3,1,2,0:T(2,128)S(1)}, f32[3,2,8,128]{3,1,2,0:T(2,128)S(1)}, u32[]{:S(2)}, u32[]{:S(2)}) collective-permute-start(f32[3,2,8,128]{3,1,2,0:T(2,128)S(1)} %get-tuple-element.205), channel_id=1, source_target_pairs={{0,24},{24,48},{48,72},{72,96},{96,120},{120,144},{144,168},{168,1... | collective-permute-start | bytes 73736 | tf_op jit(solution)/shard_map/ppermute | solution.py:25
  52.9 3.3 collective-permute-start.4
  56.2 1.8 collective-permute-done.4
  58.1 8.4 %collective-permute-start.5 = (f32[3,8,2,128]{3,1,2,0:T(8,128)S(1)}, f32[3,8,2,128]{3,1,2,0:T(8,128)S(1)}, u32[]{:S(2)}, u32[]{:S(2)}) collective-permute-start(f32[3,8,2,128]{3,1,2,0:T(8,128)S(1)} %get-tuple-element.199), channel_id=1, source_target_pairs={{0,8},{8,16},{1,9},{9,17},{2,10},{10,18},{3,11},{11,19},{4,12},{12... | collective-permute-start | bytes 73736 | tf_op jit(solution)/shard_map/ppermute | solution.py:25
  66.4 1.3 collective-permute-start.6
  67.8 9.5 %collective-permute-done.6 = f32[3,8,2,128]{3,1,2,0:T(8,128)S(1)} collective-permute-done((f32[3,8,2,128]{3,1,2,0:T(8,128)S(1)}, f32[3,8,2,128]{3,1,2,0:T(8,128)S(1)}, u32[]{:S(2)}, u32[]{:S(2)}) %collective-permute-start.6) | collective-permute-done | bytes 24608 | tf_op jit(solution)/shard_map/ppermute | solution.py:28
  78.0 1.9 collective-permute-start.7
  80.0 4.7 collective-permute-start.8
  87.3 1.2 slice.697
  88.5 1.2 slice.696
  89.8 1.2 slice.695
  91.7 1.2 slice.748
  92.9 1.2 slice.747
  94.2 1.2 slice.746
  95.9 1.2 slice.723
  97.1 1.2 slice.722
  98.4 1.4 slice.721
  101.0 1.1 copy.1487
  111.3 113.6 %all-reduce.52 = (f32[3]{0:T(128)S(1)}, f32[3]{0:T(128)S(1)}) all-reduce(f32[3]{0:T(128)S(1)} %get-tuple-element.23, f32[3]{0:T(128)S(1)} %get-tuple-element.22), channel_id=1, replica_groups=mesh['gx'=32,'gy'=3,'gz'=8] {'gx','gy','gz'}, use_global_device_ids=true, to_apply=%region_1.2 | all-reduce | flops 6 | bytes 48 | tf_op jit(solution)/shard_map/psum | solution.py:142
  225.1 103.9 %psum.30 = f32[3]{0:T(128)S(1)} all-reduce(f32[3]{0:T(128)S(1)} %multiply_reduce_fusion.1), channel_id=1, replica_groups=mesh['gx'=32,'gy'=3,'gz'=8] {'gx','gy','gz'}, use_global_device_ids=true, to_apply=%region_5.6 | all-reduce | flops 3 | bytes 24 | tf_op jit(solution)/shard_map/psum | solution.py:142
  329.2 4.2 collective-permute-start.9
  333.4 1.9 collective-permute-start.10
  335.3 3.2 collective-permute-done.10
  338.5 3.4 collective-permute-start.11
  341.9 1.3 collective-permute-start.12
  343.2 7.2 %collective-permute-done.12 = f32[3,8,2,128]{3,1,2,0:T(8,128)S(1)} collective-permute-done((f32[3,8,2,128]{3,1,2,0:T(8,128)S(1)}, f32[3,8,2,128]{3,1,2,0:T(8,128)S(1)}, u32[]{:S(2)}, u32[]{:S(2)}) %collective-permute-start.12) | collective-permute-done | bytes 24608 | tf_op jit(solution)/shard_map/ppermute | solution.py:28
  350.6 1.9 collective-permute-start.13
  352.5 5.0 %collective-permute-start.14 = (f32[3,8,12,2]{3,1,2,0:T(8,128)S(1)}, f32[3,8,12,2]{3,1,2,0:T(8,128)S(1)}, u32[]{:S(2)}, u32[]{:S(2)}) collective-permute-start(f32[3,8,12,2]{3,1,2,0:T(8,128)S(1)} %get-tuple-element.162), channel_id=1, source_target_pairs={{1,0},{2,1},{3,2},{4,3},{5,4},{6,5},{7,6},{9,8},{10,9},{11,10},{12... | collective-permute-start | bytes 6920 | tf_op jit(solution)/shard_map/ppermute | solution.py:28
  357.7 1.5 collective-permute-done.14
  359.8 1.2 slice.780
  361.1 1.2 slice.779
  362.3 1.2 slice.778
  364.2 1.2 slice.830
  365.5 1.2 slice.829
  366.7 1.2 slice.828
  368.4 1.2 slice.805
  369.7 1.2 slice.804
  370.9 1.4 slice.803
  373.5 1.1 copy.1532
  383.7 112.2 %psum.31 = f32[3]{0:T(128)S(1)} all-reduce(f32[3]{0:T(128)S(1)} %get-tuple-element.26), channel_id=1, replica_groups=mesh['gx'=32,'gy'=3,'gz'=8] {'gx','gy','gz'}, use_global_device_ids=true, to_apply=%region_7.8 | all-reduce | flops 3 | bytes 24 | tf_op jit(solution)/shard_map/psum | solution.py:173
  (355 shorter events, 44.6 us)
Async XLA Ops:
  8.8 0.9 copy-start
  10.5 6.0 %collective-permute-start = (f32[2,3,12,192]{3,0,2,1:T(2,128)S(1)}, f32[2,3,12,192]{3,0,2,1:T(2,128)S(1)}, u32[]{:S(2)}, u32[]{:S(2)}) collective-permute-start(f32[2,3,12,192]{3,0,2,1:T(2,128)S(1)} %pad_maximum_fusion.65), channel_id=1, source_target_pairs={{0,24},{24,48},{48,72},{72,96},{96,120},{120,144},{144,168},{168,1... | collective-permute-start | bytes 165896 | tf_op jit(solution)/shard_map/ppermute | solution.py:17
  16.5 11.9 %collective-permute-start.1 = (f32[2,9,3,192]{3,0,2,1:T(2,128)S(1)}, f32[2,9,3,192]{3,0,2,1:T(2,128)S(1)}, u32[]{:S(2)}, u32[]{:S(2)}) collective-permute-start(f32[2,9,3,192]{3,0,2,1:T(2,128)S(1)} %pad_maximum_fusion.66), channel_id=1, source_target_pairs={{0,8},{8,16},{1,9},{9,17},{2,10},{10,18},{3,11},{11,19},{4,12},{12... | collective-permute-start | bytes 124424 | tf_op jit(solution)/shard_map/ppermute | solution.py:17
  28.6 7.0 %collective-permute-start.2 = (f32[2,9,15,3]{3,0,2,1:T(2,128)S(1)}, f32[2,9,15,3]{3,0,2,1:T(2,128)S(1)}, u32[]{:S(2)}, u32[]{:S(2)}) collective-permute-start(f32[2,9,15,3]{3,0,2,1:T(2,128)S(1)} %pad_maximum_fusion.26), channel_id=1, source_target_pairs={{0,1},{1,2},{2,3},{3,4},{4,5},{5,6},{6,7},{8,9},{9,10},{10,11},{11... | collective-permute-start | bytes 9728 | tf_op jit(solution)/shard_map/ppermute | solution.py:17
  46.6 9.6 %collective-permute-start.3 = (f32[3,2,8,128]{3,1,2,0:T(2,128)S(1)}, f32[3,2,8,128]{3,1,2,0:T(2,128)S(1)}, u32[]{:S(2)}, u32[]{:S(2)}) collective-permute-start(f32[3,2,8,128]{3,1,2,0:T(2,128)S(1)} %get-tuple-element.205), channel_id=1, source_target_pairs={{0,24},{24,48},{48,72},{72,96},{96,120},{120,144},{144,168},{168,1... | collective-permute-start | bytes 73736 | tf_op jit(solution)/shard_map/ppermute | solution.py:25
  52.9 5.1 %collective-permute-start.4 = (f32[3,2,8,128]{3,1,2,0:T(2,128)S(1)}, f32[3,2,8,128]{3,1,2,0:T(2,128)S(1)}, u32[]{:S(2)}, u32[]{:S(2)}) collective-permute-start(f32[3,2,8,128]{3,1,2,0:T(2,128)S(1)} %get-tuple-element.206), channel_id=1, source_target_pairs={{24,0},{48,24},{72,48},{96,72},{120,96},{144,120},{168,144},{192,1... | collective-permute-start | bytes 73736 | tf_op jit(solution)/shard_map/ppermute | solution.py:28
  58.1 9.7 %collective-permute-start.5 = (f32[3,8,2,128]{3,1,2,0:T(8,128)S(1)}, f32[3,8,2,128]{3,1,2,0:T(8,128)S(1)}, u32[]{:S(2)}, u32[]{:S(2)}) collective-permute-start(f32[3,8,2,128]{3,1,2,0:T(8,128)S(1)} %get-tuple-element.199), channel_id=1, source_target_pairs={{0,8},{8,16},{1,9},{9,17},{2,10},{10,18},{3,11},{11,19},{4,12},{12... | collective-permute-start | bytes 73736 | tf_op jit(solution)/shard_map/ppermute | solution.py:25
  66.4 10.8 %collective-permute-start.6 = (f32[3,8,2,128]{3,1,2,0:T(8,128)S(1)}, f32[3,8,2,128]{3,1,2,0:T(8,128)S(1)}, u32[]{:S(2)}, u32[]{:S(2)}) collective-permute-start(f32[3,8,2,128]{3,1,2,0:T(8,128)S(1)} %get-tuple-element.200), channel_id=1, source_target_pairs={{8,0},{16,8},{9,1},{17,9},{10,2},{18,10},{11,3},{19,11},{12,4},{20... | collective-permute-start | bytes 73736 | tf_op jit(solution)/shard_map/ppermute | solution.py:28
  78.0 7.8 %collective-permute-start.7 = (f32[3,8,12,2]{3,1,2,0:T(8,128)}, f32[3,8,12,2]{3,1,2,0:T(8,128)S(1)}, u32[]{:S(2)}, u32[]{:S(2)}) collective-permute-start(f32[3,8,12,2]{3,1,2,0:T(8,128)} %get-tuple-element.163), channel_id=1, source_target_pairs={{0,1},{1,2},{2,3},{3,4},{4,5},{5,6},{6,7},{8,9},{9,10},{10,11},{11... | collective-permute-start | bytes 6920 | tf_op jit(solution)/shard_map/ppermute | solution.py:25
  80.0 6.7 %collective-permute-start.8 = (f32[3,8,12,2]{3,1,2,0:T(8,128)S(1)}, f32[3,8,12,2]{3,1,2,0:T(8,128)S(1)}, u32[]{:S(2)}, u32[]{:S(2)}) collective-permute-start(f32[3,8,12,2]{3,1,2,0:T(8,128)S(1)} %get-tuple-element.164), channel_id=1, source_target_pairs={{1,0},{2,1},{3,2},{4,3},{5,4},{6,5},{7,6},{9,8},{10,9},{11,10},{12... | collective-permute-start | bytes 6920 | tf_op jit(solution)/shard_map/ppermute | solution.py:28
  329.2 6.2 %collective-permute-start.9 = (f32[3,2,8,128]{3,1,2,0:T(2,128)S(1)}, f32[3,2,8,128]{3,1,2,0:T(2,128)S(1)}, u32[]{:S(2)}, u32[]{:S(2)}) collective-permute-start(f32[3,2,8,128]{3,1,2,0:T(2,128)S(1)} %get-tuple-element.203), channel_id=1, source_target_pairs={{0,24},{24,48},{48,72},{72,96},{96,120},{120,144},{144,168},{168,1... | collective-permute-start | bytes 73736 | tf_op jit(solution)/shard_map/ppermute | solution.py:25
  333.4 5.1 %collective-permute-start.10 = (f32[3,2,8,128]{3,1,2,0:T(2,128)S(1)}, f32[3,2,8,128]{3,1,2,0:T(2,128)S(1)}, u32[]{:S(2)}, u32[]{:S(2)}) collective-permute-start(f32[3,2,8,128]{3,1,2,0:T(2,128)S(1)} %get-tuple-element.204), channel_id=1, source_target_pairs={{24,0},{48,24},{72,48},{96,72},{120,96},{144,120},{168,144},{192,1... | collective-permute-start | bytes 73736 | tf_op jit(solution)/shard_map/ppermute | solution.py:28
  338.5 4.7 collective-permute-start.11
  341.9 8.5 %collective-permute-start.12 = (f32[3,8,2,128]{3,1,2,0:T(8,128)S(1)}, f32[3,8,2,128]{3,1,2,0:T(8,128)S(1)}, u32[]{:S(2)}, u32[]{:S(2)}) collective-permute-start(f32[3,8,2,128]{3,1,2,0:T(8,128)S(1)} %get-tuple-element.198), channel_id=1, source_target_pairs={{8,0},{16,8},{9,1},{17,9},{10,2},{18,10},{11,3},{19,11},{12,4},{20... | collective-permute-start | bytes 73736 | tf_op jit(solution)/shard_map/ppermute | solution.py:28
  350.6 7.1 %collective-permute-start.13 = (f32[3,8,12,2]{3,1,2,0:T(8,128)S(1)}, f32[3,8,12,2]{3,1,2,0:T(8,128)S(1)}, u32[]{:S(2)}, u32[]{:S(2)}) collective-permute-start(f32[3,8,12,2]{3,1,2,0:T(8,128)S(1)} %get-tuple-element.161), channel_id=1, source_target_pairs={{0,1},{1,2},{2,3},{3,4},{4,5},{5,6},{6,7},{8,9},{9,10},{10,11},{11... | collective-permute-start | bytes 6920 | tf_op jit(solution)/shard_map/ppermute | solution.py:25
  352.5 6.7 %collective-permute-start.14 = (f32[3,8,12,2]{3,1,2,0:T(8,128)S(1)}, f32[3,8,12,2]{3,1,2,0:T(8,128)S(1)}, u32[]{:S(2)}, u32[]{:S(2)}) collective-permute-start(f32[3,8,12,2]{3,1,2,0:T(8,128)S(1)} %get-tuple-element.162), channel_id=1, source_target_pairs={{1,0},{2,1},{3,2},{4,3},{5,4},{6,5},{7,6},{9,8},{10,9},{11,10},{12... | collective-permute-start | bytes 6920 | tf_op jit(solution)/shard_map/ppermute | solution.py:28
where the time goes:
time: 506 us; the launch traced here: 497 us
  blocking collectives  330 us (65%)
  starting transfers between devices  61.1 us (12%)
  local copies, waits for them, and re-layouts  59.1 us (12%)
  waiting for transfers between devices  31.2 us (6%)
  other arithmetic  13.5 us (3%)
    psum x2, blocking collectives, residual_norms(): return lax.psum(local_sum(residual, residual), ('gx', 'gy', 'gz'))  218 us
    psum x1, blocking collectives, on_device(): alpha = norm_now / lax.psum(local_sum(direction, image), ('gx', 'gy', 'gz'))  112 us
    ppermute x6, starting transfers between devices, padded_2(): lax.ppermute(lax.slice_in_dim(block, block.shape[dim] - width, None, axis...  26.1 us
    ppermute x6, waiting for transfers between devices, padded_2(): lax.ppermute(lax.slice_in_dim(block, 0, width, axis=dim), axis, backward)  23.9 us
    slice x36, local copies, waits for them, and re-layouts, to_points(): lax.slice_in_dim(field, offset, offset + 2 * count - 1, 2, axis)  23.4 us
    ppermute x6, starting transfers between devices, padded_2(): lax.ppermute(lax.slice_in_dim(block, 0, width, axis=dim), axis, backward)  17.5 us
    ppermute x3, starting transfers between devices, shifted(): return lax.ppermute(value, axis, pairs)  17.5 us
  transfers between devices with their start and end apart: 15, of which 10 were waited for; matrix products, arithmetic and copies ran while one was open for 0% of the time, Pallas kernels for 0%

commit v1 on v0

v1 whole, which is shorter than its diff:
```python
import functools
import math

import jax
import jax.numpy as jnp
from jax import lax
from jax.experimental import pallas as pl
from jax.experimental.pallas import tpu as pltpu
from jax.sharding import Mesh
from jax.sharding import PartitionSpec as P

LOW, HIGH = 3, 2
PAIRS = 14
ROOT = math.sqrt(0.15)
EDGE_W, MID_W = 5.0 / 18.0, 8.0 / 18.0
EXACT = lax.Precision.HIGHEST
GX = ("gx0", "gx1", "gx2")


def vmem(count):
    return [pl.BlockSpec(memory_space=pltpu.VMEM)] * count


def iota(shape, dim):
    return lax.broadcasted_iota(jnp.int32, shape, dim)


def class_of(q, qz):
    if qz < 2:
        return q, qz
    return (q + 9, 0) if q < 5 else (q + 4, 1)


def prepare(energy, density, region, gamma, rows_out, message_out, spread, lines):
    for point in range(6):
        spread[16 * point : 16 * point + 12, :] = energy[point]
    row, col = iota((192, 256), 0), iota((192, 256), 1)
    pick = (row == 3 * (col % 64) + jnp.minimum(col // 64, 2)).astype(jnp.float32)
    lines[...] = jnp.dot(
        spread[...], pick, precision=EXACT, preferred_element_type=jnp.float32
    )
    rho = density[...]
    zone = region[...]
    table = jnp.zeros_like(rho)
    for index in range(3):
        table = table + jnp.where(zone == index, gamma[index], 0.0)
    scale = (table - 1.0) * rho
    scale = jnp.concatenate([scale, scale], axis=-1)
    rho = jnp.concatenate([rho, rho], axis=-1)
    low_half = iota((1, 128), 1) < 64
    pair, lane = iota((16, 128), 0), iota((16, 128), 1)
    real = pair < PAIRS
    start = (lane + 128 - 3 * pair) % 128
    keep_one = real & ((start >= 125) | ((start >= 64) & (start <= 65)))
    keep_zero = real & (((start >= 61) & (start <= 63)) | (start < 2))
    for x in range(2):
        for y in range(4):
            factor = scale[x, y : y + 1]
            parts = []
            tails = []
            for qx in range(3):
                at = (3 * x + qx) * 16 + 3 * y
                parts.append(lines[at : at + 3, 0:128] * factor)
                tails.append(lines[at : at + 3, 128:256] * factor)
            tail = [tails[q // 3][q % 3 : q % 3 + 1] for q in range(9)] + [rho[x, y : y + 1]]
            for i in range(5):
                parts.append(jnp.where(low_half, tail[i], tail[i + 5]))
            parts.append(jnp.zeros((2, 128), jnp.float32))
            base = 16 * x
            block = jnp.concatenate(parts, axis=0)
            rows_out[y, base : base + 16, :] = block
            turned = pltpu.roll(block, 0, 1, stride=3, stride_axis=0)
            zero = jnp.sum(jnp.where(keep_zero, turned, 0.0), axis=0, keepdims=True)
            one = jnp.sum(jnp.where(keep_one, turned, 0.0), axis=0, keepdims=True)
            place = y * 4 + x * 2
            message_out[place : place + 1, :] = pltpu.roll(zero, 64, 1)
            message_out[place + 1 : place + 2, :] = one


def fill_z(rows, from_low, from_high, rows_out, up_out, down_out):
    lane = iota((16, 128), 1)
    halo = jnp.where((lane < 50) | (lane >= 110), from_low[...], from_high[...])
    for y in range(4):
        for x in range(2):
            base = 16 * x
            place = y * 4 + x * 2
            block = rows[y, base : base + 16, :]
            block = jnp.concatenate([block[:PAIRS], halo[place : place + 2]], axis=0)
            rows_out[y, base : base + 16, :] = block
            if y >= 1:
                up_out[y - 1, base : base + 16, :] = block
            if y < HIGH:
                down_out[y, base : base + 16, :] = block


def fill_y(rows, from_low, from_high, rows_out, last_out):
    for y in range(9):
        if y < LOW:
            block = from_low[y]
        elif y < LOW + 4:
            block = rows[y - LOW]
        else:
            block = from_high[y - LOW - 4]
        rows_out[y] = block
        last_out[y] = block[16:32]


def element_op(v, m, w):
    total, gap = v + w, v - w
    outer = 0.75 * total + m
    inner = 1.25 * gap
    return outer + inner, total + 8.0 * m, outer - inner


def by_values(q0, q1, q2):
    total, gap = q0 + q2, q0 - q2
    outer = (0.3 * EDGE_W) * total
    inner = (ROOT * EDGE_W) * gap
    return outer + inner, (0.4 * EDGE_W) * total + MID_W * q1, outer - inner


def by_slopes(q0, q1, q2):
    total, gap = q0 + q2, q0 - q2
    outer = EDGE_W * total + MID_W * q1
    inner = (4.0 * ROOT * EDGE_W) * gap
    return -outer - inner, 2.0 * inner, outer - inner


def up_z(value):
    return pltpu.roll(value, 1, 1)


def down_z(value):
    return pltpu.roll(value, 127, 1)


def up_x(value):
    return pltpu.roll(value, 1, 0)


def down_x(value):
    return pltpu.roll(value, 7, 0)


def krylov(sizes, own, far, near, above, fields_out, sums_out, points, base, image, second, flat):
    size_x, size_y, size_z = sizes
    index_x = (lax.axis_index(GX[0]) * lax.axis_size(GX[1]) + lax.axis_index(GX[1])) * (
        lax.axis_size(GX[2])
    ) + lax.axis_index(GX[2])
    zeros = jnp.zeros((16, 128), jnp.float32)
    for y in range(9):
        sources = [
            far[y],
            near[y, 0:16],
            near[y, 16:32],
            own[y, 0:16],
            own[y, 16:32],
            above[y, 0:16],
            above[y, 16:32],
            zeros,
        ]
        for s in range(8):
            points[pl.ds(y * 128 + s, 16, stride=8), :] = sources[s]

    sub, lane = iota((8, 128), 0), iota((8, 128), 1)
    at_x = 2 * index_x + sub - LOW
    at_z = 64 * lax.axis_index("gz") + jnp.where(lane < 96, lane, lane - 128)
    inside_x = (at_x > 0) & (at_x < size_x)
    inside_z = (at_z > 0) & (at_z < size_z)
    inside = {
        (0, 0): (inside_x & inside_z).astype(jnp.float32),
        (0, 1): inside_x.astype(jnp.float32),
        (1, 0): inside_z.astype(jnp.float32),
    }
    first_y = 4 * lax.axis_index("gy") - LOW
    mine = lane < 64

    def inside_y(y):
        at = first_y + y
        return ((at > 0) & (at < size_y)).astype(jnp.float32)

    def tile(ref, d, yc, xc, zc, y):
        row = (((d * 2 + yc) * 4 + xc * 2 + zc) * 9 + y) * 8
        return ref.at[pl.ds(pl.multiple_of(row, 8), 8), :]

    def point(y, p, h):
        main = points[pl.ds(pl.multiple_of(y * 128 + p * 8, 8), 8), :]
        side = points[pl.ds(pl.multiple_of(y * 128 + (PAIRS + h) * 8, 8), 8), :]
        if h:
            main = pltpu.roll(main, 64, 1)
        if p:
            side = pltpu.roll(side, 128 - 3 * p, 1)
        return jnp.where(mine, main, side)

    def put(ref, d, xc, zc, y, vertex, middle, wall):
        if (xc, zc) in inside:
            vertex = vertex * inside[xc, zc]
            middle = middle * inside[xc, zc]
        tile(ref, d, 0, xc, zc, y)[...] = vertex * wall
        tile(ref, d, 1, xc, zc, y)[...] = middle

    def force_row(y, carry):
        wall = inside_y(y)
        value_z, slope_z = {}, {}
        for q in range(9):
            q0, q1, q2 = (point(y, *class_of(q, qz)) for qz in range(3))
            n0, n1, n2 = by_values(q0, q1, q2)
            value_z[q, 0], value_z[q, 1] = n0 + up_z(n2), n1
            n0, n1, n2 = by_slopes(q0, q1, q2)
            slope_z[q, 0], slope_z[q, 1] = n0 + up_z(n2), n1
        kept = []
        for d in range(3):
            source = slope_z if d == 2 else value_z
            op_x = by_slopes if d == 0 else by_values
            op_y = by_slopes if d == 1 else by_values
            lines = {}
            for qy in range(3):
                for zc in range(2):
                    n0, n1, n2 = op_x(*(source[3 * qx + qy, zc] for qx in range(3)))
                    lines[qy, 0, zc], lines[qy, 1, zc] = n0 + up_x(n2), n1
            for xc in range(2):
                for zc in range(2):
                    n0, n1, n2 = op_y(*(lines[qy, xc, zc] for qy in range(3)))
                    put(base, d, xc, zc, y, n0 + carry[len(kept)], n1, wall)
                    kept.append(n2)
        return tuple(kept)

    blank = jnp.zeros((8, 128), jnp.float32)
    lax.fori_loop(0, 9, force_row, (blank,) * 12)

    def mass_row(d, y, source, target, carry, rho):
        wall = inside_y(y)
        locals_y = {}
        for xc in range(2):
            for zc in range(2):
                got = element_op(
                    tile(source, d, 0, xc, zc, y)[...],
                    tile(source, d, 1, xc, zc, y)[...],
                    tile(source, d, 0, xc, zc, y + 1)[...],
                )
                for k in range(3):
                    locals_y[k, xc, zc] = got[k]
        kept = [None] * 4
        out = {}
        for k in range(3):
            lines = {}
            for xc in range(2):
                v, m = locals_y[k, xc, 0], locals_y[k, xc, 1]
                got = element_op(v, m, down_z(v))
                for j in range(3):
                    lines[j, xc] = got[j]
            joined = {}
            for j in range(3):
                v, m = lines[j, 0], lines[j, 1]
                n0, n1, n2 = (rho * n for n in element_op(v, m, down_x(v)))
                joined[j, 0], joined[j, 1] = n0 + up_x(n2), n1
            for xc in range(2):
                out[k, xc, 0] = joined[0, xc] + up_z(joined[2, xc])
                out[k, xc, 1] = joined[1, xc]
        for xc in range(2):
            for zc in range(2):
                slot = 2 * xc + zc
                put(target, d, xc, zc, y, out[0, xc, zc] + carry[slot], out[1, xc, zc], wall)
                kept[slot] = out[2, xc, zc]
        return tuple(kept)

    def mass(source, target, start, stop):
        def step(y, carry):
            rho = point(y, 13, 1) * (1.0 / 3375.0)
            kept = ()
            for d in range(3):
                kept += mass_row(d, y, source, target, carry[4 * d : 4 * d + 4], rho)
            return kept

        lax.fori_loop(start, stop, step, (blank,) * 12)

    mass(base, image, 1, 8)
    mass(image, second, 2, 7)

    owned = mine & (sub >= LOW) & (sub < LOW + 2)
    row, col = iota((8, 128), 0), iota((8, 128), 1)
    sums = jnp.zeros((8, 128), jnp.float32)
    for d in range(3):
        totals = [blank] * 4
        for yc in range(2):
            for xc in range(2):
                for zc in range(2):
                    for y in range(LOW, LOW + 4):
                        v0 = tile(base, d, yc, xc, zc, y)[...]
                        v1 = tile(image, d, yc, xc, zc, y)[...]
                        v2 = tile(second, d, yc, xc, zc, y)[...]
                        totals[0] = totals[0] + v0 * v0
                        totals[1] = totals[1] + v0 * v1
                        totals[2] = totals[2] + v1 * v1
                        totals[3] = totals[3] + v1 * v2
        for k in range(4):
            total = jnp.sum(jnp.where(owned, totals[k], 0.0), keepdims=True)
            sums = sums + jnp.where((row == k) & (col == d), total, 0.0)
    sums_out[...] = sums

    mine_row = iota((4, 128), 1) < 64
    for f, ref in enumerate((base, image, second)):
        for d in range(3):
            for yc in range(2):
                for xc in range(2):
                    for x in range(2):
                        got = []
                        for zc in range(2):
                            at = (((d * 2 + yc) * 4 + xc * 2 + zc) * 9 + LOW) * 8 + LOW + x
                            got.append(ref[pl.ds(at, 4, stride=8), :])
                        line = jnp.where(mine_row, got[0], pltpu.roll(got[1], 64, 1))
                        place = ((f * 3 + d) * 4 + 2 * x + xc) * 8 + yc
                        flat[pl.ds(place, 4, stride=2), :] = line
    row, col = iota((128, 128), 0), iota((128, 128), 1)
    weave = (row == (col % 2) * 64 + col // 2).astype(jnp.float32)
    fields_out[...] = jnp.dot(
        flat[...], weave, precision=EXACT, preferred_element_type=jnp.float32
    )


def combine(fields, sums, acceleration_out, residual_out):
    for d in range(3):
        c0, c1, c2, c3 = (sums[k : k + 1, d : d + 1] for k in range(4))
        alpha = c0 / c1
        norm = c0 - 2.0 * alpha * c1 + alpha * alpha * c2
        beta = norm / c0
        grow = 1.0 + beta
        alpha_2 = norm / (grow * grow * c1 - 2.0 * alpha * grow * c2 + alpha * alpha * c3)
        v0, v1, v2 = (fields[96 * f + 32 * d : 96 * f + 32 * d + 32, :] for f in range(3))
        direction = (v0 - alpha * v1) + beta * v0
        image = grow * v1 - alpha * v2
        acceleration_out[32 * d : 32 * d + 32, :] = alpha * v0 + alpha_2 * direction
        residual_out[32 * d : 32 * d + 32, :] = (v0 - alpha * v1) - alpha_2 * image


def moved(value, axis, by):
    count = lax.axis_size(axis)
    pairs = [(i, i + by) for i in range(count) if 0 <= i + by < count]
    return lax.ppermute(value, axis, pairs)


def shape(*dims):
    return jax.ShapeDtypeStruct(dims, jnp.float32)


def call(body, outs, count, scratch=(), specs=None):
    return pl.pallas_call(
        body,
        out_shape=outs,
        in_specs=specs or vmem(count),
        out_specs=tuple(vmem(len(outs))),
        scratch_shapes=[pltpu.VMEM(dims, jnp.float32) for dims in scratch],
    )


def total_over(value):
    for axis in (("gx2",), ("gx1",), ("gx0",), ("gy",), ("gz",)):
        value = lax.psum(value, axis)
    return value


def on_device(sizes, energy, density, region, gamma_table):
    rows, message = call(
        prepare,
        (shape(4, 32, 128), shape(16, 128)),
        4,
        ((96, 192), (96, 256)),
        vmem(3) + [pl.BlockSpec(memory_space=pltpu.SMEM)],
    )(energy, density, region, gamma_table)
    rows, up, down = call(fill_z, (shape(4, 32, 128), shape(3, 32, 128), shape(2, 32, 128)), 3)(
        rows, moved(message, "gz", 1), moved(message, "gz", -1)
    )
    own, last = call(fill_y, (shape(9, 32, 128), shape(9, 16, 128)), 3)(
        rows, moved(up, "gy", 1), moved(down, "gy", -1)
    )
    near, above, far = moved(own, GX, 1), moved(own, GX, -1), moved(last, GX, 2)
    grid = (3 * 2 * 4 * 9 * 8, 128)
    fields, sums = call(
        functools.partial(krylov, sizes),
        (shape(288, 128), shape(8, 128)),
        4,
        ((9 * 128, 128), grid, grid, grid, (288, 128)),
    )(own, far, near, above)
    acceleration, residual = call(combine, (shape(96, 128), shape(96, 128)), 2)(
        fields, total_over(sums)
    )
    return acceleration.reshape(3, 4, 8, 128), residual.reshape(3, 4, 8, 128)


def split(count):
    inner = 2
    middle = math.gcd(4, count // inner)
    return count // (inner * middle), middle, inner


def solution(mesh):
    count = mesh.shape["gx"]
    devices = mesh.devices.reshape(*split(count), mesh.shape["gy"], mesh.shape["gz"])
    finer = Mesh(devices, (*GX, "gy", "gz"))
    sizes = (2 * count, 4 * mesh.shape["gy"], 64 * mesh.shape["gz"])
    place = P(GX, "gy", "gz")
    out = P(None, GX, "gy", "gz")
    return jax.shard_map(
        functools.partial(on_device, sizes),
        mesh=finer,
        in_specs=(place, place, place, P()),
        out_specs=(out, out),
        check_vma=False,
    )
```

time: 506 us -> 113 us (0.22)
  the two profiles are of different devices: /device:TPU:35 before, /device:TPU:64 now
where the time goes in v1:
time: 113 us; the launch traced here: 112 us
  blocking collectives  56.6 us (50%)
  starting transfers between devices  26.8 us (24%)
  Pallas kernels  13.2 us (12%)
  waiting for transfers between devices  12.5 us (11%)
  local copies, waits for them, and re-layouts  2.57 us (2%)
    psum x5, blocking collectives, total_over(): value = lax.psum(value, axis)  56.6 us
    ppermute x7, starting transfers between devices, moved(): return lax.ppermute(value, axis, pairs)  26.8 us
    ppermute x7, waiting for transfers between devices, moved(): return lax.ppermute(value, axis, pairs)  12.5 us
    pallas_call x1, Pallas kernels, on_device(): call(functools.partial(krylov, sizes), (shape(288, 128), shape(8, 128)),...  6.54 us
    unnamed x14, local copies, waits for them, and re-layouts  2.57 us
  transfers between devices with their start and end apart: 7, of which 3 were waited for; matrix products, arithmetic and copies ran while one was open for 0% of the time, Pallas kernels for 0%

profile of v1, /device:TPU:64, one launch (start us, length us, event | category | flops | bytes accessed | tf_op | source)
XLA Modules:
  0.0 112.4 jit_solution(4082322386164264141)
XLA Ops:
  0.6 1.9 %shard_map.59 = (f32[4,32,128]{2,1,0:T(8,128)}, f32[16,128]{1,0:T(8,128)}) custom-call(f32[6,12,192]{2,1,0:T(8,128)} %energy.1, f32[2,4,64]{2,1,0:T(4,128)} %density.1, s32[2,4,64]{2,1,0:T(4,128)} %region.1, f32[3]{0:T(128)} %gamma.1), custom_call_target="tpu_custom_call" | custom-call | tf_op jit(solution)/shard_map/pallas_call | solution.py:363
  2.6 1.3 %collective-permute-start.1 = (f32[16,128]{1,0:T(8,128)}, f32[16,128]{1,0:T(8,128)S(1)}, u32[]{:S(2)}, u32[]{:S(2)}) collective-permute-start(f32[16,128]{1,0:T(8,128)} %get-tuple-element.14), channel_id=1, source_target_pairs={{1,0},{2,1},{3,2},{4,3},{5,4},{6,5},{7,6},{9,8},{10,9},{11,10},{12... | collective-permute-start | bytes 24584 | tf_op jit(solution)/shard_map/ppermute | solution.py:339
  3.9 4.5 %collective-permute-start = (f32[16,128]{1,0:T(8,128)}, f32[16,128]{1,0:T(8,128)S(1)}, u32[]{:S(2)}, u32[]{:S(2)}) collective-permute-start(f32[16,128]{1,0:T(8,128)} %get-tuple-element.14), channel_id=1, source_target_pairs={{0,1},{1,2},{2,3},{3,4},{4,5},{5,6},{6,7},{8,9},{9,10},{10,11},{11... | collective-permute-start | bytes 24584 | tf_op jit(solution)/shard_map/ppermute | solution.py:339
  8.4 0.0 collective-permute-done.1.from_high
  8.4 0.0 copy-start.5
  8.4 1.5 %collective-permute-done.from_low = f32[16,128]{1,0:T(8,128)S(1)} collective-permute-done((f32[16,128]{1,0:T(8,128)}, f32[16,128]{1,0:T(8,128)S(1)}, u32[]{:S(2)}, u32[]{:S(2)}) %collective-permute-start) | collective-permute-done | bytes 8224 | tf_op jit(solution)/shard_map/ppermute | solution.py:339
  10.0 0.0 copy-start.6
  10.0 0.0 copy-done.5
  10.0 0.6 copy-done.6
  10.6 1.5 %shard_map.60 = (f32[4,32,128]{2,1,0:T(8,128)}, f32[3,32,128]{2,1,0:T(8,128)}, f32[2,32,128]{2,1,0:T(8,128)}) custom-call(f32[4,32,128]{2,1,0:T(8,128)} %get-tuple-element.13.rows, f32[16,128]{1,0:T(8,128)} %copy-done.6, f32[16,128]{1,0:T(8,128)} %copy-done.5), custom_call_target="tpu_custom_call" | custom-call | tf_op jit(solution)/shard_map/pallas_call | solution.py:370
  12.1 10.9 %collective-permute-start.2 = (f32[3,32,128]{2,1,0:T(8,128)}, f32[3,32,128]{2,1,0:T(8,128)S(1)}, u32[]{:S(2)}, u32[]{:S(2)}) collective-permute-start(f32[3,32,128]{2,1,0:T(8,128)} %get-tuple-element.16), channel_id=1, source_target_pairs={{0,8},{8,16},{1,9},{9,17},{2,10},{10,18},{3,11},{11,19},{4,12},{12... | collective-permute-start | bytes 147464 | tf_op jit(solution)/shard_map/ppermute | solution.py:339
  23.0 1.3 %collective-permute-start.3 = (f32[2,32,128]{2,1,0:T(8,128)}, f32[2,32,128]{2,1,0:T(8,128)S(1)}, u32[]{:S(2)}, u32[]{:S(2)}) collective-permute-start(f32[2,32,128]{2,1,0:T(8,128)} %get-tuple-element.17), channel_id=1, source_target_pairs={{8,0},{16,8},{9,1},{17,9},{10,2},{18,10},{11,3},{19,11},{12,4},{20... | collective-permute-start | bytes 98312 | tf_op jit(solution)/shard_map/ppermute | solution.py:339
  24.3 8.6 %collective-permute-done.3.from_high = f32[2,32,128]{2,1,0:T(8,128)S(1)} collective-permute-done((f32[2,32,128]{2,1,0:T(8,128)}, f32[2,32,128]{2,1,0:T(8,128)S(1)}, u32[]{:S(2)}, u32[]{:S(2)}) %collective-permute-start.3) | collective-permute-done | bytes 32800 | tf_op jit(solution)/shard_map/ppermute | solution.py:339
  32.9 0.0 copy-start.4
  32.9 0.0 collective-permute-done.2.from_low
  32.9 0.0 copy-start.3
  32.9 0.6 copy-done.4
  33.5 0.0 copy-done.3
  33.6 1.6 %shard_map.61 = (f32[9,32,128]{2,1,0:T(8,128)}, f32[9,16,128]{2,1,0:T(8,128)}) custom-call(f32[4,32,128]{2,1,0:T(8,128)} %get-tuple-element.15.rows, f32[3,32,128]{2,1,0:T(8,128)} %copy-done.3, f32[2,32,128]{2,1,0:T(8,128)} %copy-done.4), custom_call_target="tpu_custom_call" | custom-call | tf_op jit(solution)/shard_map/pallas_call | solution.py:373
  35.1 1.9 %collective-permute-start.6 = (f32[9,32,128]{2,1,0:T(8,128)}, f32[9,32,128]{2,1,0:T(8,128)S(1)}, u32[]{:S(2)}, u32[]{:S(2)}) collective-permute-start(f32[9,32,128]{2,1,0:T(8,128)} %get-tuple-element.18.own), channel_id=1, source_target_pairs={{24,0},{48,24},{72,48},{96,72},{120,96},{144,120},{168,144},{192,1... | collective-permute-start | bytes 442376 | tf_op jit(solution)/shard_map/ppermute | solution.py:339
  37.0 2.4 %collective-permute-start.5 = (f32[9,32,128]{2,1,0:T(8,128)}, f32[9,32,128]{2,1,0:T(8,128)S(1)}, u32[]{:S(2)}, u32[]{:S(2)}) collective-permute-start(f32[9,32,128]{2,1,0:T(8,128)} %get-tuple-element.18.own), channel_id=1, source_target_pairs={{0,24},{24,48},{48,72},{72,96},{96,120},{120,144},{144,168},{168,1... | collective-permute-start | bytes 442376 | tf_op jit(solution)/shard_map/ppermute | solution.py:339
  39.4 4.5 %collective-permute-start.4 = (f32[9,16,128]{2,1,0:T(8,128)}, f32[9,16,128]{2,1,0:T(8,128)S(1)}, u32[]{:S(2)}, u32[]{:S(2)}) collective-permute-start(f32[9,16,128]{2,1,0:T(8,128)} %get-tuple-element.19), channel_id=1, source_target_pairs={{0,48},{24,72},{48,96},{72,120},{96,144},{120,168},{144,192},{168,... | collective-permute-start | bytes 221192 | tf_op jit(solution)/shard_map/ppermute | solution.py:339
  44.0 2.3 %collective-permute-done.4.far = f32[9,16,128]{2,1,0:T(8,128)S(1)} collective-permute-done((f32[9,16,128]{2,1,0:T(8,128)}, f32[9,16,128]{2,1,0:T(8,128)S(1)}, u32[]{:S(2)}, u32[]{:S(2)}) %collective-permute-start.4) | collective-permute-done | bytes 73760 | tf_op jit(solution)/shard_map/ppermute | solution.py:339
  46.2 0.0 copy-start.2
  46.2 0.0 collective-permute-done.6.above
  46.2 0.0 copy-start
  46.2 0.0 collective-permute-done.5.near
  46.2 0.6 copy-done.2
  46.9 0.1 copy-done
  46.9 0.0 copy-start.1
  46.9 0.7 copy-done.1
  47.6 6.5 %shard_map.62 = (f32[288,128]{1,0:T(8,128)}, f32[8,128]{1,0:T(8,128)}) custom-call(f32[9,32,128]{2,1,0:T(8,128)} %get-tuple-element.18.own, f32[9,16,128]{2,1,0:T(8,128)} %copy-done.2, f32[9,32,128]{2,1,0:T(8,128)} %copy-done.1, f32[9,32,128]{2,1,0:T(8,128)} %copy-done), custom_call_target="tpu_custom_call" | custom-call | tf_op jit(solution)/shard_map/pallas_call | solution.py:378
  54.1 3.2 %psum.35 = f32[8,128]{1,0:T(8,128)S(1)} all-reduce(f32[8,128]{1,0:T(8,128)} %get-tuple-element.21), channel_id=1, replica_groups=mesh['gx0'=4,'gx1'=4,'gx2'=2,'gy'=3,'gz'=8] {'gx2'}, use_global_device_ids=true, to_apply=%region_0.0 | all-reduce | flops 1024 | bytes 8192 | tf_op jit(solution)/shard_map/psum | solution.py:358
  57.4 9.9 %psum.36 = f32[8,128]{1,0:T(8,128)S(1)} all-reduce(f32[8,128]{1,0:T(8,128)S(1)} %psum.35), channel_id=1, replica_groups=mesh['gx0'=4,'gx1'=4,'gx2'=2,'gy'=3,'gz'=8] {'gx1'}, use_global_device_ids=true, to_apply=%region_1.0 | all-reduce | flops 1024 | bytes 8192 | tf_op jit(solution)/shard_map/psum | solution.py:358
  67.2 12.8 %psum.37 = f32[8,128]{1,0:T(8,128)S(1)} all-reduce(f32[8,128]{1,0:T(8,128)S(1)} %psum.36), channel_id=1, replica_groups=mesh['gx0'=4,'gx1'=4,'gx2'=2,'gy'=3,'gz'=8] {'gx0'}, use_global_device_ids=true, to_apply=%region_2.0 | all-reduce | flops 1024 | bytes 8192 | tf_op jit(solution)/shard_map/psum | solution.py:358
  80.1 10.8 %psum.38 = f32[8,128]{1,0:T(8,128)S(1)} all-reduce(f32[8,128]{1,0:T(8,128)S(1)} %psum.37), channel_id=1, replica_groups=mesh['gx0'=4,'gx1'=4,'gx2'=2,'gy'=3,'gz'=8] {'gy'}, use_global_device_ids=true, to_apply=%region_3.0 | all-reduce | flops 1024 | bytes 8192 | tf_op jit(solution)/shard_map/psum | solution.py:358
  90.9 19.8 %psum.39.sums = f32[8,128]{1,0:T(8,128)} all-reduce(f32[8,128]{1,0:T(8,128)S(1)} %psum.38), channel_id=1, replica_groups=mesh['gx0'=4,'gx1'=4,'gx2'=2,'gy'=3,'gz'=8] {'gz'}, use_global_device_ids=true, to_apply=%region_4.0 | all-reduce | flops 1024 | bytes 8192 | tf_op jit(solution)/shard_map/psum | solution.py:358
  110.7 1.7 %shard_map.63 = (f32[96,128]{1,0:T(8,128)}, f32[96,128]{1,0:T(8,128)}) custom-call(f32[288,128]{1,0:T(8,128)} %get-tuple-element.20.fields, f32[8,128]{1,0:T(8,128)} %psum.39.sums), custom_call_target="tpu_custom_call" | custom-call | tf_op jit(solution)/shard_map/pallas_call | solution.py:384
Async XLA Ops:
  2.6 5.8 %collective-permute-start.1 = (f32[16,128]{1,0:T(8,128)}, f32[16,128]{1,0:T(8,128)S(1)}, u32[]{:S(2)}, u32[]{:S(2)}) collective-permute-start(f32[16,128]{1,0:T(8,128)} %get-tuple-element.14), channel_id=1, source_target_pairs={{1,0},{2,1},{3,2},{4,3},{5,4},{6,5},{7,6},{9,8},{10,9},{11,10},{12... | collective-permute-start | bytes 24584 | tf_op jit(solution)/shard_map/ppermute | solution.py:339
  3.9 6.1 %collective-permute-start = (f32[16,128]{1,0:T(8,128)}, f32[16,128]{1,0:T(8,128)S(1)}, u32[]{:S(2)}, u32[]{:S(2)}) collective-permute-start(f32[16,128]{1,0:T(8,128)} %get-tuple-element.14), channel_id=1, source_target_pairs={{0,1},{1,2},{2,3},{3,4},{4,5},{5,6},{6,7},{8,9},{9,10},{10,11},{11... | collective-permute-start | bytes 24584 | tf_op jit(solution)/shard_map/ppermute | solution.py:339
  8.4 1.6 %copy-start.5 = (f32[16,128]{1,0:T(8,128)}, f32[16,128]{1,0:T(8,128)S(1)}, u32[]{:S(2)}) copy-start(f32[16,128]{1,0:T(8,128)S(1)} %collective-permute-done.1.from_high) | copy-start | bytes 24580
  10.0 0.6 copy-start.6
  12.1 20.8 %collective-permute-start.2 = (f32[3,32,128]{2,1,0:T(8,128)}, f32[3,32,128]{2,1,0:T(8,128)S(1)}, u32[]{:S(2)}, u32[]{:S(2)}) collective-permute-start(f32[3,32,128]{2,1,0:T(8,128)} %get-tuple-element.16), channel_id=1, source_target_pairs={{0,8},{8,16},{1,9},{9,17},{2,10},{10,18},{3,11},{11,19},{4,12},{12... | collective-permute-start | bytes 147464 | tf_op jit(solution)/shard_map/ppermute | solution.py:339
  23.0 9.9 %collective-permute-start.3 = (f32[2,32,128]{2,1,0:T(8,128)}, f32[2,32,128]{2,1,0:T(8,128)S(1)}, u32[]{:S(2)}, u32[]{:S(2)}) collective-permute-start(f32[2,32,128]{2,1,0:T(8,128)} %get-tuple-element.17), channel_id=1, source_target_pairs={{8,0},{16,8},{9,1},{17,9},{10,2},{18,10},{11,3},{19,11},{12,4},{20... | collective-permute-start | bytes 98312 | tf_op jit(solution)/shard_map/ppermute | solution.py:339
  32.9 0.6 copy-start.4
  32.9 0.6 copy-start.3
  35.1 11.1 %collective-permute-start.6 = (f32[9,32,128]{2,1,0:T(8,128)}, f32[9,32,128]{2,1,0:T(8,128)S(1)}, u32[]{:S(2)}, u32[]{:S(2)}) collective-permute-start(f32[9,32,128]{2,1,0:T(8,128)} %get-tuple-element.18.own), channel_id=1, source_target_pairs={{24,0},{48,24},{72,48},{96,72},{120,96},{144,120},{168,144},{192,1... | collective-permute-start | bytes 442376 | tf_op jit(solution)/shard_map/ppermute | solution.py:339
  37.0 9.2 %collective-permute-start.5 = (f32[9,32,128]{2,1,0:T(8,128)}, f32[9,32,128]{2,1,0:T(8,128)S(1)}, u32[]{:S(2)}, u32[]{:S(2)}) collective-permute-start(f32[9,32,128]{2,1,0:T(8,128)} %get-tuple-element.18.own), channel_id=1, source_target_pairs={{0,24},{24,48},{48,72},{72,96},{96,120},{120,144},{144,168},{168,1... | collective-permute-start | bytes 442376 | tf_op jit(solution)/shard_map/ppermute | solution.py:339
  39.4 6.8 %collective-permute-start.4 = (f32[9,16,128]{2,1,0:T(8,128)}, f32[9,16,128]{2,1,0:T(8,128)S(1)}, u32[]{:S(2)}, u32[]{:S(2)}) collective-permute-start(f32[9,16,128]{2,1,0:T(8,128)} %get-tuple-element.19), channel_id=1, source_target_pairs={{0,48},{24,72},{48,96},{72,120},{96,144},{120,168},{144,192},{168,... | collective-permute-start | bytes 221192 | tf_op jit(solution)/shard_map/ppermute | solution.py:339
  46.2 0.6 copy-start.2
  46.2 0.7 copy-start
  46.9 0.7 copy-start.1

commit v2 on v1

--- a/solution.py
+++ b/solution.py
@@ -343,14 +343,16 @@
     return jax.ShapeDtypeStruct(dims, jnp.float32)
 
 
-def call(body, outs, count, scratch=(), specs=None):
+def call(body, outs, *operands, scratch=(), last=False, specs=None):
+    kept = [pltpu.with_memory_space_constraint(o, pltpu.VMEM) for o in operands]
+    place = (lambda o: o) if last else (lambda o: pltpu.VMEM(o.shape, o.dtype))
     return pl.pallas_call(
         body,
-        out_shape=outs,
-        in_specs=specs or vmem(count),
+        out_shape=tuple(place(o) for o in outs),
+        in_specs=vmem(len(operands)),
         out_specs=tuple(vmem(len(outs))),
         scratch_shapes=[pltpu.VMEM(dims, jnp.float32) for dims in scratch],
-    )
+    )(*kept)
 
 
 def total_over(value):
@@ -360,29 +362,40 @@
 
 
 def on_device(sizes, energy, density, region, gamma_table):
-    rows, message = call(
+    rows, message = pl.pallas_call(
         prepare,
-        (shape(4, 32, 128), shape(16, 128)),
-        4,
-        ((96, 192), (96, 256)),
-        vmem(3) + [pl.BlockSpec(memory_space=pltpu.SMEM)],
+        out_shape=(pltpu.VMEM((4, 32, 128), jnp.float32), pltpu.VMEM((16, 128), jnp.float32)),
+        in_specs=vmem(3) + [pl.BlockSpec(memory_space=pltpu.SMEM)],
+        out_specs=tuple(vmem(2)),
+        scratch_shapes=[pltpu.VMEM((96, 192), jnp.float32), pltpu.VMEM((96, 256), jnp.float32)],
     )(energy, density, region, gamma_table)
-    rows, up, down = call(fill_z, (shape(4, 32, 128), shape(3, 32, 128), shape(2, 32, 128)), 3)(
-        rows, moved(message, "gz", 1), moved(message, "gz", -1)
-    )
-    own, last = call(fill_y, (shape(9, 32, 128), shape(9, 16, 128)), 3)(
-        rows, moved(up, "gy", 1), moved(down, "gy", -1)
+    rows, up, down = call(
+        fill_z,
+        (shape(4, 32, 128), shape(3, 32, 128), shape(2, 32, 128)),
+        rows,
+        moved(message, "gz", 1),
+        moved(message, "gz", -1),
+    )
+    own, last = call(
+        fill_y,
+        (shape(9, 32, 128), shape(9, 16, 128)),
+        rows,
+        moved(up, "gy", 1),
+        moved(down, "gy", -1),
     )
     near, above, far = moved(own, GX, 1), moved(own, GX, -1), moved(last, GX, 2)
     grid = (3 * 2 * 4 * 9 * 8, 128)
     fields, sums = call(
         functools.partial(krylov, sizes),
         (shape(288, 128), shape(8, 128)),
-        4,
-        ((9 * 128, 128), grid, grid, grid, (288, 128)),
-    )(own, far, near, above)
-    acceleration, residual = call(combine, (shape(96, 128), shape(96, 128)), 2)(
-        fields, total_over(sums)
+        own,
+        far,
+        near,
+        above,
+        scratch=((9 * 128, 128), grid, grid, grid, (288, 128)),
+    )
+    acceleration, residual = call(
+        combine, (shape(96, 128), shape(96, 128)), fields, total_over(sums), last=True
     )
     return acceleration.reshape(3, 4, 8, 128), residual.reshape(3, 4, 8, 128)
 

time: 113 us -> 103 us (0.912)
  Pallas kernels: 13.2 us -> 6.98 us
  local copies, waits for them, and re-layouts: 2.57 us -> 0 us
    pallas_call x5, Pallas kernels: 13.2 us -> 6.98 us  [the longest x4 5.64 us: call(): pl.pallas_call(body, out_shape=tuple((place(o) for o in outs)), in_specs=...]
    unnamed x14 -> x0, local copies, waits for them, and re-layouts: 2.57 us -> none
where the time goes in v2:
time: 103 us; the launch traced here: 102 us
  blocking collectives  56 us (54%)
  starting transfers between devices  26.9 us (26%)
  waiting for transfers between devices  11.7 us (11%)
  Pallas kernels  6.98 us (7%)
    psum x5, blocking collectives, total_over(): value = lax.psum(value, axis)  56 us
    ppermute x7, starting transfers between devices, moved(): return lax.ppermute(value, axis, pairs)  26.9 us
    ppermute x7, waiting for transfers between devices, moved(): return lax.ppermute(value, axis, pairs)  11.7 us
    pallas_call x4, Pallas kernels, call(): pl.pallas_call(body, out_shape=tuple((place(o) for o in outs)), in_specs=...  5.64 us
  transfers between devices with their start and end apart: 7, of which 3 were waited for; matrix products, arithmetic and copies ran while one was open for 0% of the time, Pallas kernels for 0%

profile of v2, /device:TPU:64, one launch (start us, length us, event | category | flops | bytes accessed | tf_op | source)
XLA Modules:
  0.0 102.3 jit_solution(10286782658707596962)
XLA Ops:
  0.6 1.3 %shard_map.59 = (f32[4,32,128]{2,1,0:T(8,128)S(1)}, f32[16,128]{1,0:T(8,128)S(1)}) custom-call(f32[6,12,192]{2,1,0:T(8,128)} %energy.1, f32[2,4,64]{2,1,0:T(4,128)} %density.1, s32[2,4,64]{2,1,0:T(4,128)} %region.1, f32[3]{0:T(128)} %gamma.1), custom_call_target="tpu_custom_call" | custom-call | tf_op jit(solution)/shard_map/pallas_call | solution.py:365
  2.0 1.3 %collective-permute-start.1 = (f32[16,128]{1,0:T(8,128)S(1)}, f32[16,128]{1,0:T(8,128)S(1)}, u32[]{:S(2)}, u32[]{:S(2)}) collective-permute-start(f32[16,128]{1,0:T(8,128)S(1)} %get-tuple-element.14), channel_id=1, source_target_pairs={{1,0},{2,1},{3,2},{4,3},{5,4},{6,5},{7,6},{9,8},{10,9},{11,10},{12... | collective-permute-start | bytes 24584 | tf_op jit(solution)/shard_map/ppermute | solution.py:339
  3.3 4.5 %collective-permute-start = (f32[16,128]{1,0:T(8,128)S(1)}, f32[16,128]{1,0:T(8,128)S(1)}, u32[]{:S(2)}, u32[]{:S(2)}) collective-permute-start(f32[16,128]{1,0:T(8,128)S(1)} %get-tuple-element.14), channel_id=1, source_target_pairs={{0,1},{1,2},{2,3},{3,4},{4,5},{5,6},{6,7},{8,9},{9,10},{10,11},{11... | collective-permute-start | bytes 24584 | tf_op jit(solution)/shard_map/ppermute | solution.py:339
  7.8 0.0 collective-permute-done.1.from_high
  7.8 1.3 %collective-permute-done.from_low = f32[16,128]{1,0:T(8,128)S(1)} collective-permute-done((f32[16,128]{1,0:T(8,128)S(1)}, f32[16,128]{1,0:T(8,128)S(1)}, u32[]{:S(2)}, u32[]{:S(2)}) %collective-permute-start) | collective-permute-done | bytes 8224 | tf_op jit(solution)/shard_map/ppermute | solution.py:339
  9.2 10.9 %collective-permute-start.2 = (f32[3,32,128]{2,1,0:T(8,128)S(1)}, f32[3,32,128]{2,1,0:T(8,128)S(1)}, u32[]{:S(2)}, u32[]{:S(2)}) collective-permute-start(f32[3,32,128]{2,1,0:T(8,128)S(1)} %get-tuple-element.16), channel_id=1, source_target_pairs={{0,8},{8,16},{1,9},{9,17},{2,10},{10,18},{3,11},{11,19},{4,12},{12... | collective-permute-start | bytes 147464 | tf_op jit(solution)/shard_map/ppermute | solution.py:339
  20.1 1.3 %collective-permute-start.3 = (f32[2,32,128]{2,1,0:T(8,128)S(1)}, f32[2,32,128]{2,1,0:T(8,128)S(1)}, u32[]{:S(2)}, u32[]{:S(2)}) collective-permute-start(f32[2,32,128]{2,1,0:T(8,128)S(1)} %get-tuple-element.17), channel_id=1, source_target_pairs={{8,0},{16,8},{9,1},{17,9},{10,2},{18,10},{11,3},{19,11},{12,4},{20... | collective-permute-start | bytes 98312 | tf_op jit(solution)/shard_map/ppermute | solution.py:339
  21.4 8.4 %collective-permute-done.3.from_high = f32[2,32,128]{2,1,0:T(8,128)S(1)} collective-permute-done((f32[2,32,128]{2,1,0:T(8,128)S(1)}, f32[2,32,128]{2,1,0:T(8,128)S(1)}, u32[]{:S(2)}, u32[]{:S(2)}) %collective-permute-start.3) | collective-permute-done | bytes 32800 | tf_op jit(solution)/shard_map/ppermute | solution.py:339
  29.8 0.0 collective-permute-done.2.from_low
  29.8 1.9 %collective-permute-start.6 = (f32[9,32,128]{2,1,0:T(8,128)S(1)}, f32[9,32,128]{2,1,0:T(8,128)S(1)}, u32[]{:S(2)}, u32[]{:S(2)}) collective-permute-start(f32[9,32,128]{2,1,0:T(8,128)S(1)} %get-tuple-element.18.own), channel_id=1, source_target_pairs={{24,0},{48,24},{72,48},{96,72},{120,96},{144,120},{168,144},{192,1... | collective-permute-start | bytes 442376 | tf_op jit(solution)/shard_map/ppermute | solution.py:339
  31.8 2.4 %collective-permute-start.5 = (f32[9,32,128]{2,1,0:T(8,128)S(1)}, f32[9,32,128]{2,1,0:T(8,128)S(1)}, u32[]{:S(2)}, u32[]{:S(2)}) collective-permute-start(f32[9,32,128]{2,1,0:T(8,128)S(1)} %get-tuple-element.18.own), channel_id=1, source_target_pairs={{0,24},{24,48},{48,72},{72,96},{96,120},{120,144},{144,168},{168,1... | collective-permute-start | bytes 442376 | tf_op jit(solution)/shard_map/ppermute | solution.py:339
  34.2 4.5 %collective-permute-start.4 = (f32[9,16,128]{2,1,0:T(8,128)S(1)}, f32[9,16,128]{2,1,0:T(8,128)S(1)}, u32[]{:S(2)}, u32[]{:S(2)}) collective-permute-start(f32[9,16,128]{2,1,0:T(8,128)S(1)} %get-tuple-element.19), channel_id=1, source_target_pairs={{0,48},{24,72},{48,96},{72,120},{96,144},{120,168},{144,192},{168,... | collective-permute-start | bytes 221192 | tf_op jit(solution)/shard_map/ppermute | solution.py:339
  38.7 2.0 %collective-permute-done.4.far = f32[9,16,128]{2,1,0:T(8,128)S(1)} collective-permute-done((f32[9,16,128]{2,1,0:T(8,128)S(1)}, f32[9,16,128]{2,1,0:T(8,128)S(1)}, u32[]{:S(2)}, u32[]{:S(2)}) %collective-permute-start.4) | collective-permute-done | bytes 73760 | tf_op jit(solution)/shard_map/ppermute | solution.py:339
  40.7 0.0 collective-permute-done.6.above
  40.7 0.0 collective-permute-done.5.near
  40.7 4.8 %shard_map.62 = (f32[288,128]{1,0:T(8,128)S(1)}, f32[8,128]{1,0:T(8,128)S(1)}) custom-call(f32[9,32,128]{2,1,0:T(8,128)S(1)} %get-tuple-element.18.own, f32[9,16,128]{2,1,0:T(8,128)S(1)} %collective-permute-done.4.far, f32[9,32,128]{2,1,0:T(8,128)S(1)} %collective-permute-done.5.near, f32[9,32,128]{2,1,0:T(8,128)S(1)} %collective-permute-done.6.above), custom_call_target="tpu_custom_call" | custom-call | tf_op jit(solution)/shard_map/pallas_call | solution.py:349
  45.5 3.1 %psum.35 = f32[8,128]{1,0:T(8,128)S(1)} all-reduce(f32[8,128]{1,0:T(8,128)S(1)} %get-tuple-element.21), channel_id=1, replica_groups=mesh['gx0'=4,'gx1'=4,'gx2'=2,'gy'=3,'gz'=8] {'gx2'}, use_global_device_ids=true, to_apply=%region_0.0 | all-reduce | flops 1024 | bytes 8192 | tf_op jit(solution)/shard_map/psum | solution.py:360
  48.6 10.0 %psum.36 = f32[8,128]{1,0:T(8,128)S(1)} all-reduce(f32[8,128]{1,0:T(8,128)S(1)} %psum.35), channel_id=1, replica_groups=mesh['gx0'=4,'gx1'=4,'gx2'=2,'gy'=3,'gz'=8] {'gx1'}, use_global_device_ids=true, to_apply=%region_1.0 | all-reduce | flops 1024 | bytes 8192 | tf_op jit(solution)/shard_map/psum | solution.py:360
  58.6 12.8 %psum.37 = f32[8,128]{1,0:T(8,128)S(1)} all-reduce(f32[8,128]{1,0:T(8,128)S(1)} %psum.36), channel_id=1, replica_groups=mesh['gx0'=4,'gx1'=4,'gx2'=2,'gy'=3,'gz'=8] {'gx0'}, use_global_device_ids=true, to_apply=%region_2.0 | all-reduce | flops 1024 | bytes 8192 | tf_op jit(solution)/shard_map/psum | solution.py:360
  71.5 10.8 %psum.38 = f32[8,128]{1,0:T(8,128)S(1)} all-reduce(f32[8,128]{1,0:T(8,128)S(1)} %psum.37), channel_id=1, replica_groups=mesh['gx0'=4,'gx1'=4,'gx2'=2,'gy'=3,'gz'=8] {'gy'}, use_global_device_ids=true, to_apply=%region_3.0 | all-reduce | flops 1024 | bytes 8192 | tf_op jit(solution)/shard_map/psum | solution.py:360
  82.3 19.2 %psum.39.sums = f32[8,128]{1,0:T(8,128)S(1)} all-reduce(f32[8,128]{1,0:T(8,128)S(1)} %psum.38), channel_id=1, replica_groups=mesh['gx0'=4,'gx1'=4,'gx2'=2,'gy'=3,'gz'=8] {'gz'}, use_global_device_ids=true, to_apply=%region_4.0 | all-reduce | flops 1024 | bytes 8192 | tf_op jit(solution)/shard_map/psum | solution.py:360
  101.5 0.8 shard_map.63
  (2 shorter events, 0.0 us)
Async XLA Ops:
  2.0 5.8 %collective-permute-start.1 = (f32[16,128]{1,0:T(8,128)S(1)}, f32[16,128]{1,0:T(8,128)S(1)}, u32[]{:S(2)}, u32[]{:S(2)}) collective-permute-start(f32[16,128]{1,0:T(8,128)S(1)} %get-tuple-element.14), channel_id=1, source_target_pairs={{1,0},{2,1},{3,2},{4,3},{5,4},{6,5},{7,6},{9,8},{10,9},{11,10},{12... | collective-permute-start | bytes 24584 | tf_op jit(solution)/shard_map/ppermute | solution.py:339
  3.3 5.9 %collective-permute-start = (f32[16,128]{1,0:T(8,128)S(1)}, f32[16,128]{1,0:T(8,128)S(1)}, u32[]{:S(2)}, u32[]{:S(2)}) collective-permute-start(f32[16,128]{1,0:T(8,128)S(1)} %get-tuple-element.14), channel_id=1, source_target_pairs={{0,1},{1,2},{2,3},{3,4},{4,5},{5,6},{6,7},{8,9},{9,10},{10,11},{11... | collective-permute-start | bytes 24584 | tf_op jit(solution)/shard_map/ppermute | solution.py:339
  9.2 20.6 %collective-permute-start.2 = (f32[3,32,128]{2,1,0:T(8,128)S(1)}, f32[3,32,128]{2,1,0:T(8,128)S(1)}, u32[]{:S(2)}, u32[]{:S(2)}) collective-permute-start(f32[3,32,128]{2,1,0:T(8,128)S(1)} %get-tuple-element.16), channel_id=1, source_target_pairs={{0,8},{8,16},{1,9},{9,17},{2,10},{10,18},{3,11},{11,19},{4,12},{12... | collective-permute-start | bytes 147464 | tf_op jit(solution)/shard_map/ppermute | solution.py:339
  20.1 9.7 %collective-permute-start.3 = (f32[2,32,128]{2,1,0:T(8,128)S(1)}, f32[2,32,128]{2,1,0:T(8,128)S(1)}, u32[]{:S(2)}, u32[]{:S(2)}) collective-permute-start(f32[2,32,128]{2,1,0:T(8,128)S(1)} %get-tuple-element.17), channel_id=1, source_target_pairs={{8,0},{16,8},{9,1},{17,9},{10,2},{18,10},{11,3},{19,11},{12,4},{20... | collective-permute-start | bytes 98312 | tf_op jit(solution)/shard_map/ppermute | solution.py:339
  29.8 10.8 %collective-permute-start.6 = (f32[9,32,128]{2,1,0:T(8,128)S(1)}, f32[9,32,128]{2,1,0:T(8,128)S(1)}, u32[]{:S(2)}, u32[]{:S(2)}) collective-permute-start(f32[9,32,128]{2,1,0:T(8,128)S(1)} %get-tuple-element.18.own), channel_id=1, source_target_pairs={{24,0},{48,24},{72,48},{96,72},{120,96},{144,120},{168,144},{192,1... | collective-permute-start | bytes 442376 | tf_op jit(solution)/shard_map/ppermute | solution.py:339
  31.8 8.9 %collective-permute-start.5 = (f32[9,32,128]{2,1,0:T(8,128)S(1)}, f32[9,32,128]{2,1,0:T(8,128)S(1)}, u32[]{:S(2)}, u32[]{:S(2)}) collective-permute-start(f32[9,32,128]{2,1,0:T(8,128)S(1)} %get-tuple-element.18.own), channel_id=1, source_target_pairs={{0,24},{24,48},{48,72},{72,96},{96,120},{120,144},{144,168},{168,1... | collective-permute-start | bytes 442376 | tf_op jit(solution)/shard_map/ppermute | solution.py:339
  34.2 6.5 %collective-permute-start.4 = (f32[9,16,128]{2,1,0:T(8,128)S(1)}, f32[9,16,128]{2,1,0:T(8,128)S(1)}, u32[]{:S(2)}, u32[]{:S(2)}) collective-permute-start(f32[9,16,128]{2,1,0:T(8,128)S(1)} %get-tuple-element.19), channel_id=1, source_target_pairs={{0,48},{24,72},{48,96},{72,120},{96,144},{120,168},{144,192},{168,... | collective-permute-start | bytes 221192 | tf_op jit(solution)/shard_map/ppermute | solution.py:339

commit v3 on v2

--- a/solution.py
+++ b/solution.py
@@ -278,8 +278,8 @@
     mass(image, second, 2, 7)
 
     owned = mine & (sub >= LOW) & (sub < LOW + 2)
-    row, col = iota((8, 128), 0), iota((8, 128), 1)
-    sums = jnp.zeros((8, 128), jnp.float32)
+    col = iota((1, 128), 1)
+    sums = jnp.zeros((1, 128), jnp.float32)
     for d in range(3):
         totals = [blank] * 4
         for yc in range(2):
@@ -295,8 +295,8 @@
                         totals[3] = totals[3] + v1 * v2
         for k in range(4):
             total = jnp.sum(jnp.where(owned, totals[k], 0.0), keepdims=True)
-            sums = sums + jnp.where((row == k) & (col == d), total, 0.0)
-    sums_out[...] = sums
+            sums = sums + jnp.where(col == 4 * d + k, total, 0.0)
+    sums_out[...] = jnp.broadcast_to(sums[None], sums_out.shape)
 
     mine_row = iota((4, 128), 1) < 64
     for f, ref in enumerate((base, image, second)):
@@ -318,9 +318,21 @@
     )
 
 
-def combine(fields, sums, acceleration_out, residual_out):
+def add_parts(parts):
+    total = parts[0]
+    for k in range(1, parts.shape[0]):
+        total = total + parts[k]
+    return total
+
+
+def relay(parts, sums_out):
+    sums_out[...] = jnp.broadcast_to(add_parts(parts)[None], sums_out.shape)
+
+
+def combine(fields, parts, acceleration_out, residual_out):
+    sums = add_parts(parts)
     for d in range(3):
-        c0, c1, c2, c3 = (sums[k : k + 1, d : d + 1] for k in range(4))
+        c0, c1, c2, c3 = (sums[:, 4 * d + k : 4 * d + k + 1] for k in range(4))
         alpha = c0 / c1
         norm = c0 - 2.0 * alpha * c1 + alpha * alpha * c2
         beta = norm / c0
@@ -355,10 +367,15 @@
     )(*kept)
 
 
-def total_over(value):
-    for axis in (("gx2",), ("gx1",), ("gx0",), ("gy",), ("gz",)):
-        value = lax.psum(value, axis)
-    return value
+FIRST, SECOND = ("gx0", "gz", "gx2"), ("gy", "gx1")
+
+
+def members(axes):
+    return math.prod(lax.axis_size(axis) for axis in axes)
+
+
+def exchange(value, axes):
+    return lax.all_to_all(value, axes, 0, 0)
 
 
 def on_device(sizes, energy, density, region, gamma_table):
@@ -387,15 +404,20 @@
     grid = (3 * 2 * 4 * 9 * 8, 128)
     fields, sums = call(
         functools.partial(krylov, sizes),
-        (shape(288, 128), shape(8, 128)),
+        (shape(288, 128), shape(members(FIRST), 1, 128)),
         own,
         far,
         near,
         above,
         scratch=((9 * 128, 128), grid, grid, grid, (288, 128)),
     )
+    (sums,) = call(relay, (shape(members(SECOND), 1, 128),), exchange(sums, FIRST))
     acceleration, residual = call(
-        combine, (shape(96, 128), shape(96, 128)), fields, total_over(sums), last=True
+        combine,
+        (shape(96, 128), shape(96, 128)),
+        fields,
+        exchange(sums, SECOND),
+        last=True,
     )
     return acceleration.reshape(3, 4, 8, 128), residual.reshape(3, 4, 8, 128)
 

time: 103 us -> 89.2 us (0.87)
  the two profiles are of different devices: /device:TPU:64 before, /device:TPU:1 now
where the time goes in v3:
time: 89.2 us; the launch traced here: 88.8 us
  blocking collectives  40.3 us (45%)
  starting transfers between devices  30.3 us (34%)
  waiting for transfers between devices  10.4 us (12%)
  Pallas kernels  7.11 us (8%)
    all_to_all x2, blocking collectives, exchange(): return lax.all_to_all(value, axes, 0, 0)  40.3 us
    ppermute x7, starting transfers between devices, moved(): return lax.ppermute(value, axis, pairs)  30.3 us
    ppermute x7, waiting for transfers between devices, moved(): return lax.ppermute(value, axis, pairs)  10.4 us
    pallas_call x5, Pallas kernels, call(): pl.pallas_call(body, out_shape=tuple((place(o) for o in outs)), in_specs=...  5.77 us
  transfers between devices with their start and end apart: 7, of which 3 were waited for; matrix products, arithmetic and copies ran while one was open for 0% of the time, Pallas kernels for 0%

profile of v3, /device:TPU:1, one launch (start us, length us, event | category | flops | bytes accessed | tf_op | source)
XLA Modules:
  0.0 88.8 jit_solution(7197104949055483492)
XLA Ops:
  0.6 1.3 %shard_map.59 = (f32[4,32,128]{2,1,0:T(8,128)S(1)}, f32[16,128]{1,0:T(8,128)S(1)}) custom-call(f32[6,12,192]{2,1,0:T(8,128)} %energy.1, f32[2,4,64]{2,1,0:T(4,128)} %density.1, s32[2,4,64]{2,1,0:T(4,128)} %region.1, f32[3]{0:T(128)} %gamma.1), custom_call_target="tpu_custom_call" | custom-call | tf_op jit(solution)/shard_map/pallas_call | solution.py:382
  2.0 1.3 %collective-permute-start.1 = (f32[16,128]{1,0:T(8,128)S(1)}, f32[16,128]{1,0:T(8,128)S(1)}, u32[]{:S(2)}, u32[]{:S(2)}) collective-permute-start(f32[16,128]{1,0:T(8,128)S(1)} %get-tuple-element.14), channel_id=1, source_target_pairs={{1,0},{2,1},{3,2},{4,3},{5,4},{6,5},{7,6},{9,8},{10,9},{11,10},{12... | collective-permute-start | bytes 24584 | tf_op jit(solution)/shard_map/ppermute | solution.py:351
  3.3 4.6 %collective-permute-start = (f32[16,128]{1,0:T(8,128)S(1)}, f32[16,128]{1,0:T(8,128)S(1)}, u32[]{:S(2)}, u32[]{:S(2)}) collective-permute-start(f32[16,128]{1,0:T(8,128)S(1)} %get-tuple-element.14), channel_id=1, source_target_pairs={{0,1},{1,2},{2,3},{3,4},{4,5},{5,6},{6,7},{8,9},{9,10},{10,11},{11... | collective-permute-start | bytes 24584 | tf_op jit(solution)/shard_map/ppermute | solution.py:351
  7.9 0.0 collective-permute-done.1.from_high
  7.9 0.8 collective-permute-done.from_low
  8.7 10.8 %collective-permute-start.2 = (f32[3,32,128]{2,1,0:T(8,128)S(1)}, f32[3,32,128]{2,1,0:T(8,128)S(1)}, u32[]{:S(2)}, u32[]{:S(2)}) collective-permute-start(f32[3,32,128]{2,1,0:T(8,128)S(1)} %get-tuple-element.16), channel_id=1, source_target_pairs={{0,8},{8,16},{1,9},{9,17},{2,10},{10,18},{3,11},{11,19},{4,12},{12... | collective-permute-start | bytes 147464 | tf_op jit(solution)/shard_map/ppermute | solution.py:351
  19.5 1.3 %collective-permute-start.3 = (f32[2,32,128]{2,1,0:T(8,128)S(1)}, f32[2,32,128]{2,1,0:T(8,128)S(1)}, u32[]{:S(2)}, u32[]{:S(2)}) collective-permute-start(f32[2,32,128]{2,1,0:T(8,128)S(1)} %get-tuple-element.17), channel_id=1, source_target_pairs={{8,0},{16,8},{9,1},{17,9},{10,2},{18,10},{11,3},{19,11},{12,4},{20... | collective-permute-start | bytes 98312 | tf_op jit(solution)/shard_map/ppermute | solution.py:351
  20.8 8.2 %collective-permute-done.3.from_high = f32[2,32,128]{2,1,0:T(8,128)S(1)} collective-permute-done((f32[2,32,128]{2,1,0:T(8,128)S(1)}, f32[2,32,128]{2,1,0:T(8,128)S(1)}, u32[]{:S(2)}, u32[]{:S(2)}) %collective-permute-start.3) | collective-permute-done | bytes 32800 | tf_op jit(solution)/shard_map/ppermute | solution.py:351
  29.0 0.0 collective-permute-done.2.from_low
  29.1 4.9 %collective-permute-start.6 = (f32[9,32,128]{2,1,0:T(8,128)S(1)}, f32[9,32,128]{2,1,0:T(8,128)S(1)}, u32[]{:S(2)}, u32[]{:S(2)}) collective-permute-start(f32[9,32,128]{2,1,0:T(8,128)S(1)} %get-tuple-element.18.own), channel_id=1, source_target_pairs={{24,0},{48,24},{72,48},{96,72},{120,96},{144,120},{168,144},{192,1... | collective-permute-start | bytes 442376 | tf_op jit(solution)/shard_map/ppermute | solution.py:351
  33.9 3.2 %collective-permute-start.5 = (f32[9,32,128]{2,1,0:T(8,128)S(1)}, f32[9,32,128]{2,1,0:T(8,128)S(1)}, u32[]{:S(2)}, u32[]{:S(2)}) collective-permute-start(f32[9,32,128]{2,1,0:T(8,128)S(1)} %get-tuple-element.18.own), channel_id=1, source_target_pairs={{0,24},{24,48},{48,72},{72,96},{96,120},{120,144},{144,168},{168,1... | collective-permute-start | bytes 442376 | tf_op jit(solution)/shard_map/ppermute | solution.py:351
  37.2 4.2 %collective-permute-start.4 = (f32[9,16,128]{2,1,0:T(8,128)S(1)}, f32[9,16,128]{2,1,0:T(8,128)S(1)}, u32[]{:S(2)}, u32[]{:S(2)}) collective-permute-start(f32[9,16,128]{2,1,0:T(8,128)S(1)} %get-tuple-element.19), channel_id=1, source_target_pairs={{0,48},{24,72},{48,96},{72,120},{96,144},{120,168},{144,192},{168,... | collective-permute-start | bytes 221192 | tf_op jit(solution)/shard_map/ppermute | solution.py:351
  41.4 1.4 %collective-permute-done.4.far = f32[9,16,128]{2,1,0:T(8,128)S(1)} collective-permute-done((f32[9,16,128]{2,1,0:T(8,128)S(1)}, f32[9,16,128]{2,1,0:T(8,128)S(1)}, u32[]{:S(2)}, u32[]{:S(2)}) %collective-permute-start.4) | collective-permute-done | bytes 73760 | tf_op jit(solution)/shard_map/ppermute | solution.py:351
  42.8 0.0 collective-permute-done.6.above
  42.8 0.0 collective-permute-done.5.near
  42.8 4.9 %shard_map.62 = (f32[288,128]{1,0:T(8,128)S(1)}, f32[64,1,128]{2,1,0:T(1,128)S(1)}) custom-call(f32[9,32,128]{2,1,0:T(8,128)S(1)} %get-tuple-element.18.own, f32[9,16,128]{2,1,0:T(8,128)S(1)} %collective-permute-done.4.far, f32[9,32,128]{2,1,0:T(8,128)S(1)} %collective-permute-done.5.near, f32[9,32,128]{2,1,0:T(8,128)S(1)} %collective-permute-done.6.above), custom_call_target="tpu_custom_call" | custom-call | tf_op jit(solution)/shard_map/pallas_call | solution.py:361
  47.7 25.0 %all_to_all.10.parts = f32[64,1,128]{2,1,0:T(1,128)S(1)} all-to-all(f32[64,1,128]{2,1,0:T(1,128)S(1)} %get-tuple-element.21), channel_id=1, replica_groups=mesh['gx0'=4,'gx1'=4,'gx2'=2,'gy'=3,'gz'=8] {'gx0','gz','gx2'}, dimensions={0} | all-to-all | bytes 65536 | tf_op jit(solution)/shard_map/all_to_all | solution.py:378
  72.6 0.1 shard_map.63
  72.7 15.3 %all_to_all.11.parts = f32[12,1,128]{2,1,0:T(1,128)S(1)} all-to-all(f32[12,1,128]{2,1,0:T(1,128)S(1)} %shard_map.63), channel_id=1, replica_groups=mesh['gx0'=4,'gx1'=4,'gx2'=2,'gy'=3,'gz'=8] {'gy','gx1'}, dimensions={0} | all-to-all | bytes 12288 | tf_op jit(solution)/shard_map/all_to_all | solution.py:378
  88.0 0.8 shard_map.64
  (2 shorter events, 0.0 us)
Async XLA Ops:
  2.0 6.0 %collective-permute-start.1 = (f32[16,128]{1,0:T(8,128)S(1)}, f32[16,128]{1,0:T(8,128)S(1)}, u32[]{:S(2)}, u32[]{:S(2)}) collective-permute-start(f32[16,128]{1,0:T(8,128)S(1)} %get-tuple-element.14), channel_id=1, source_target_pairs={{1,0},{2,1},{3,2},{4,3},{5,4},{6,5},{7,6},{9,8},{10,9},{11,10},{12... | collective-permute-start | bytes 24584 | tf_op jit(solution)/shard_map/ppermute | solution.py:351
  3.3 5.4 %collective-permute-start = (f32[16,128]{1,0:T(8,128)S(1)}, f32[16,128]{1,0:T(8,128)S(1)}, u32[]{:S(2)}, u32[]{:S(2)}) collective-permute-start(f32[16,128]{1,0:T(8,128)S(1)} %get-tuple-element.14), channel_id=1, source_target_pairs={{0,1},{1,2},{2,3},{3,4},{4,5},{5,6},{6,7},{8,9},{9,10},{10,11},{11... | collective-permute-start | bytes 24584 | tf_op jit(solution)/shard_map/ppermute | solution.py:351
  8.7 20.3 %collective-permute-start.2 = (f32[3,32,128]{2,1,0:T(8,128)S(1)}, f32[3,32,128]{2,1,0:T(8,128)S(1)}, u32[]{:S(2)}, u32[]{:S(2)}) collective-permute-start(f32[3,32,128]{2,1,0:T(8,128)S(1)} %get-tuple-element.16), channel_id=1, source_target_pairs={{0,8},{8,16},{1,9},{9,17},{2,10},{10,18},{3,11},{11,19},{4,12},{12... | collective-permute-start | bytes 147464 | tf_op jit(solution)/shard_map/ppermute | solution.py:351
  19.5 9.5 %collective-permute-start.3 = (f32[2,32,128]{2,1,0:T(8,128)S(1)}, f32[2,32,128]{2,1,0:T(8,128)S(1)}, u32[]{:S(2)}, u32[]{:S(2)}) collective-permute-start(f32[2,32,128]{2,1,0:T(8,128)S(1)} %get-tuple-element.17), channel_id=1, source_target_pairs={{8,0},{16,8},{9,1},{17,9},{10,2},{18,10},{11,3},{19,11},{12,4},{20... | collective-permute-start | bytes 98312 | tf_op jit(solution)/shard_map/ppermute | solution.py:351
  29.1 13.7 %collective-permute-start.6 = (f32[9,32,128]{2,1,0:T(8,128)S(1)}, f32[9,32,128]{2,1,0:T(8,128)S(1)}, u32[]{:S(2)}, u32[]{:S(2)}) collective-permute-start(f32[9,32,128]{2,1,0:T(8,128)S(1)} %get-tuple-element.18.own), channel_id=1, source_target_pairs={{24,0},{48,24},{72,48},{96,72},{120,96},{144,120},{168,144},{192,1... | collective-permute-start | bytes 442376 | tf_op jit(solution)/shard_map/ppermute | solution.py:351
  33.9 8.8 %collective-permute-start.5 = (f32[9,32,128]{2,1,0:T(8,128)S(1)}, f32[9,32,128]{2,1,0:T(8,128)S(1)}, u32[]{:S(2)}, u32[]{:S(2)}) collective-permute-start(f32[9,32,128]{2,1,0:T(8,128)S(1)} %get-tuple-element.18.own), channel_id=1, source_target_pairs={{0,24},{24,48},{48,72},{72,96},{96,120},{120,144},{144,168},{168,1... | collective-permute-start | bytes 442376 | tf_op jit(solution)/shard_map/ppermute | solution.py:351
  37.2 5.6 %collective-permute-start.4 = (f32[9,16,128]{2,1,0:T(8,128)S(1)}, f32[9,16,128]{2,1,0:T(8,128)S(1)}, u32[]{:S(2)}, u32[]{:S(2)}) collective-permute-start(f32[9,16,128]{2,1,0:T(8,128)S(1)} %get-tuple-element.19), channel_id=1, source_target_pairs={{0,48},{24,72},{48,96},{72,120},{96,144},{120,168},{144,192},{168,... | collective-permute-start | bytes 221192 | tf_op jit(solution)/shard_map/ppermute | solution.py:351

commit v4 on v3

--- a/solution.py
+++ b/solution.py
@@ -13,12 +13,23 @@
 PAIRS = 14
 ROOT = math.sqrt(0.15)
 EDGE_W, MID_W = 5.0 / 18.0, 8.0 / 18.0
-EXACT = lax.Precision.HIGHEST
+UNROLL = (3, 5, 3)
 GX = ("gx0", "gx1", "gx2")
 
 
 def vmem(count):
     return [pl.BlockSpec(memory_space=pltpu.VMEM)] * count
+
+
+def selected(value, pick):
+    pick = pick.astype(jnp.bfloat16)
+    total = None
+    for part in range(3):
+        piece = value.astype(jnp.bfloat16)
+        value = value - piece.astype(jnp.float32)
+        got = jnp.dot(piece, pick, preferred_element_type=jnp.float32)
+        total = got if total is None else total + got
+    return total
 
 
 def iota(shape, dim):
@@ -35,10 +46,8 @@
     for point in range(6):
         spread[16 * point : 16 * point + 12, :] = energy[point]
     row, col = iota((192, 256), 0), iota((192, 256), 1)
-    pick = (row == 3 * (col % 64) + jnp.minimum(col // 64, 2)).astype(jnp.float32)
-    lines[...] = jnp.dot(
-        spread[...], pick, precision=EXACT, preferred_element_type=jnp.float32
-    )
+    pick = row == 3 * (col % 64) + jnp.minimum(col // 64, 2)
+    lines[...] = selected(spread[...], pick)
     rho = density[...]
     zone = region[...]
     table = jnp.zeros_like(rho)
@@ -53,6 +62,11 @@
     start = (lane + 128 - 3 * pair) % 128
     keep_one = real & ((start >= 125) | ((start >= 64) & (start <= 65)))
     keep_zero = real & (((start >= 61) & (start <= 63)) | (start < 2))
+    middle = iota((3, 128), 0) == 1
+    line_w = jnp.where(middle, MID_W, EDGE_W)
+    half_w = jnp.where(iota((3, 128), 1) < 64, EDGE_W, MID_W)
+    weights = [line_w * half_w * w for w in (EDGE_W, MID_W, EDGE_W)]
+    tail_weights = [line_w * EDGE_W * w for w in (EDGE_W, MID_W, EDGE_W)]
     for x in range(2):
         for y in range(4):
             factor = scale[x, y : y + 1]
@@ -60,8 +74,8 @@
             tails = []
             for qx in range(3):
                 at = (3 * x + qx) * 16 + 3 * y
-                parts.append(lines[at : at + 3, 0:128] * factor)
-                tails.append(lines[at : at + 3, 128:256] * factor)
+                parts.append(lines[at : at + 3, 0:128] * (factor * weights[qx]))
+                tails.append(lines[at : at + 3, 128:256] * (factor * tail_weights[qx]))
             tail = [tails[q // 3][q % 3 : q % 3 + 1] for q in range(9)] + [rho[x, y : y + 1]]
             for i in range(5):
                 parts.append(jnp.where(low_half, tail[i], tail[i + 5]))
@@ -114,15 +128,13 @@
 
 def by_values(q0, q1, q2):
     total, gap = q0 + q2, q0 - q2
-    outer = (0.3 * EDGE_W) * total
-    inner = (ROOT * EDGE_W) * gap
-    return outer + inner, (0.4 * EDGE_W) * total + MID_W * q1, outer - inner
+    outer, inner = 0.3 * total, ROOT * gap
+    return outer + inner, 0.4 * total + q1, outer - inner
 
 
 def by_slopes(q0, q1, q2):
-    total, gap = q0 + q2, q0 - q2
-    outer = EDGE_W * total + MID_W * q1
-    inner = (4.0 * ROOT * EDGE_W) * gap
+    outer = (q0 + q2) + q1
+    inner = (4.0 * ROOT) * (q0 - q2)
     return -outer - inner, 2.0 * inner, outer - inner
 
 
@@ -142,21 +154,25 @@
     return pltpu.roll(value, 7, 0)
 
 
-def krylov(sizes, own, far, near, above, fields_out, sums_out, points, base, image, second, flat):
+def krylov(sizes, own, pair, cross, far, fields_out, sums_out, points, base, image, second, flat):
     size_x, size_y, size_z = sizes
     index_x = (lax.axis_index(GX[0]) * lax.axis_size(GX[1]) + lax.axis_index(GX[1])) * (
         lax.axis_size(GX[2])
     ) + lax.axis_index(GX[2])
     zeros = jnp.zeros((16, 128), jnp.float32)
+    core = lax.axis_index(GX[2])
     for y in range(9):
+        partner, distant = pair[1 - core, y], cross[y]
+        near = jnp.where(core == 1, partner, distant)
+        above = jnp.where(core == 1, distant, partner)
         sources = [
             far[y],
-            near[y, 0:16],
-            near[y, 16:32],
+            near[0:16],
+            near[16:32],
             own[y, 0:16],
             own[y, 16:32],
-            above[y, 0:16],
-            above[y, 16:32],
+            above[0:16],
+            above[16:32],
             zeros,
         ]
         for s in range(8):
@@ -195,40 +211,42 @@
     def put(ref, d, xc, zc, y, vertex, middle, wall):
         if (xc, zc) in inside:
             vertex = vertex * inside[xc, zc]
-            middle = middle * inside[xc, zc]
+            middle = None if middle is None else middle * inside[xc, zc]
         tile(ref, d, 0, xc, zc, y)[...] = vertex * wall
-        tile(ref, d, 1, xc, zc, y)[...] = middle
+        if middle is not None:
+            tile(ref, d, 1, xc, zc, y)[...] = middle
 
     def force_row(y, carry):
         wall = inside_y(y)
-        value_z, slope_z = {}, {}
-        for q in range(9):
-            q0, q1, q2 = (point(y, *class_of(q, qz)) for qz in range(3))
-            n0, n1, n2 = by_values(q0, q1, q2)
-            value_z[q, 0], value_z[q, 1] = n0 + up_z(n2), n1
-            n0, n1, n2 = by_slopes(q0, q1, q2)
-            slope_z[q, 0], slope_z[q, 1] = n0 + up_z(n2), n1
+        lines = {}
+        for qy in range(3):
+            value_z, slope_z = {}, {}
+            for qx in range(3):
+                q0, q1, q2 = (point(y, *class_of(3 * qx + qy, qz)) for qz in range(3))
+                n0, n1, n2 = by_values(q0, q1, q2)
+                value_z[qx, 0], value_z[qx, 1] = n0 + up_z(n2), n1
+                n0, n1, n2 = by_slopes(q0, q1, q2)
+                slope_z[qx, 0], slope_z[qx, 1] = n0 + up_z(n2), n1
+            for d in range(3):
+                source = slope_z if d == 2 else value_z
+                op_x = by_slopes if d == 0 else by_values
+                for zc in range(2):
+                    n0, n1, n2 = op_x(*(source[qx, zc] for qx in range(3)))
+                    lines[d, qy, 0, zc], lines[d, qy, 1, zc] = n0 + up_x(n2), n1
         kept = []
         for d in range(3):
-            source = slope_z if d == 2 else value_z
-            op_x = by_slopes if d == 0 else by_values
             op_y = by_slopes if d == 1 else by_values
-            lines = {}
-            for qy in range(3):
-                for zc in range(2):
-                    n0, n1, n2 = op_x(*(source[3 * qx + qy, zc] for qx in range(3)))
-                    lines[qy, 0, zc], lines[qy, 1, zc] = n0 + up_x(n2), n1
             for xc in range(2):
                 for zc in range(2):
-                    n0, n1, n2 = op_y(*(lines[qy, xc, zc] for qy in range(3)))
+                    n0, n1, n2 = op_y(*(lines[d, qy, xc, zc] for qy in range(3)))
                     put(base, d, xc, zc, y, n0 + carry[len(kept)], n1, wall)
                     kept.append(n2)
         return tuple(kept)
 
     blank = jnp.zeros((8, 128), jnp.float32)
-    lax.fori_loop(0, 9, force_row, (blank,) * 12)
-
-    def mass_row(d, y, source, target, carry, rho):
+    lax.fori_loop(0, 9, force_row, (blank,) * 12, unroll=UNROLL[0])
+
+    def mass_row(d, y, source, target, carry, rho, wanted):
         wall = inside_y(y)
         locals_y = {}
         for xc in range(2):
@@ -242,7 +260,7 @@
                     locals_y[k, xc, zc] = got[k]
         kept = [None] * 4
         out = {}
-        for k in range(3):
+        for k in wanted:
             lines = {}
             for xc in range(2):
                 v, m = locals_y[k, xc, 0], locals_y[k, xc, 1]
@@ -260,43 +278,26 @@
         for xc in range(2):
             for zc in range(2):
                 slot = 2 * xc + zc
-                put(target, d, xc, zc, y, out[0, xc, zc] + carry[slot], out[1, xc, zc], wall)
-                kept[slot] = out[2, xc, zc]
+                if 0 in wanted:
+                    middle = out.get((1, xc, zc))
+                    put(target, d, xc, zc, y, out[0, xc, zc] + carry[slot], middle, wall)
+                kept[slot] = out.get((2, xc, zc), blank)
         return tuple(kept)
 
-    def mass(source, target, start, stop):
-        def step(y, carry):
+    def mass(source, target, start, stop, last, unroll):
+        def step(y, carry, wanted=(0, 1, 2)):
             rho = point(y, 13, 1) * (1.0 / 3375.0)
             kept = ()
             for d in range(3):
-                kept += mass_row(d, y, source, target, carry[4 * d : 4 * d + 4], rho)
+                kept += mass_row(d, y, source, target, carry[4 * d : 4 * d + 4], rho, wanted)
             return kept
 
-        lax.fori_loop(start, stop, step, (blank,) * 12)
-
-    mass(base, image, 1, 8)
-    mass(image, second, 2, 7)
-
-    owned = mine & (sub >= LOW) & (sub < LOW + 2)
-    col = iota((1, 128), 1)
-    sums = jnp.zeros((1, 128), jnp.float32)
-    for d in range(3):
-        totals = [blank] * 4
-        for yc in range(2):
-            for xc in range(2):
-                for zc in range(2):
-                    for y in range(LOW, LOW + 4):
-                        v0 = tile(base, d, yc, xc, zc, y)[...]
-                        v1 = tile(image, d, yc, xc, zc, y)[...]
-                        v2 = tile(second, d, yc, xc, zc, y)[...]
-                        totals[0] = totals[0] + v0 * v0
-                        totals[1] = totals[1] + v0 * v1
-                        totals[2] = totals[2] + v1 * v1
-                        totals[3] = totals[3] + v1 * v2
-        for k in range(4):
-            total = jnp.sum(jnp.where(owned, totals[k], 0.0), keepdims=True)
-            sums = sums + jnp.where(col == 4 * d + k, total, 0.0)
-    sums_out[...] = jnp.broadcast_to(sums[None], sums_out.shape)
+        carry = step(start, (blank,) * 12, (2,))
+        carry = lax.fori_loop(start + 1, stop - 1, step, carry, unroll=unroll)
+        step(stop - 1, carry, last)
+
+    mass(base, image, 1, 8, (0,), UNROLL[1])
+    mass(image, second, 2, 7, (0, 1), UNROLL[2])
 
     mine_row = iota((4, 128), 1) < 64
     for f, ref in enumerate((base, image, second)):
@@ -311,26 +312,47 @@
                         line = jnp.where(mine_row, got[0], pltpu.roll(got[1], 64, 1))
                         place = ((f * 3 + d) * 4 + 2 * x + xc) * 8 + yc
                         flat[pl.ds(place, 4, stride=2), :] = line
+
+    lines = []
+    for d in range(3):
+        v0, v1, v2 = (flat[96 * f + 32 * d : 96 * f + 32 * d + 32, :] for f in range(3))
+        for product in (v0 * v0, v0 * v1, v1 * v1, v1 * v2):
+            lines.append(jnp.sum(product, axis=0, keepdims=True))
+    lines = jnp.sum(jnp.concatenate(lines, axis=0), axis=1, keepdims=True)
+    row, col = iota((12, 128), 0), iota((12, 128), 1)
+    sums = jnp.sum(jnp.where(row == col, lines, 0.0), axis=0, keepdims=True)
+    if sums_out.ndim == 3:
+        sums = sums[None]
+    sums_out[...] = jnp.broadcast_to(sums, sums_out.shape)
+
     row, col = iota((128, 128), 0), iota((128, 128), 1)
-    weave = (row == (col % 2) * 64 + col // 2).astype(jnp.float32)
+    weave = row == (col % 2) * 64 + col // 2
     fields_out[...] = jnp.dot(
-        flat[...], weave, precision=EXACT, preferred_element_type=jnp.float32
-    )
-
-
-def add_parts(parts):
-    total = parts[0]
-    for k in range(1, parts.shape[0]):
-        total = total + parts[k]
-    return total
+        flat[...],
+        weave.astype(jnp.float32),
+        precision=lax.Precision.HIGHEST,
+        preferred_element_type=jnp.float32,
+    )
+
+
+def total_of(parts):
+    if parts.ndim == 2:
+        return jnp.sum(parts[...], axis=0, keepdims=True)
+    rows = [parts[k] for k in range(parts.shape[0])]
+    while len(rows) > 1:
+        rows = [sum(rows[k : k + 2][1:], rows[k]) for k in range(0, len(rows), 2)]
+    return rows[0]
 
 
 def relay(parts, sums_out):
-    sums_out[...] = jnp.broadcast_to(add_parts(parts)[None], sums_out.shape)
+    sums = total_of(parts)
+    if sums_out.ndim == 3:
+        sums = sums[None]
+    sums_out[...] = jnp.broadcast_to(sums, sums_out.shape)
 
 
 def combine(fields, parts, acceleration_out, residual_out):
-    sums = add_parts(parts)
+    sums = total_of(parts)
     for d in range(3):
         c0, c1, c2, c3 = (sums[:, 4 * d + k : 4 * d + k + 1] for k in range(4))
         alpha = c0 / c1
@@ -374,8 +396,14 @@
     return math.prod(lax.axis_size(axis) for axis in axes)
 
 
+def parts_shape(axes):
+    count = members(axes)
+    return shape(count, 128) if count % 8 == 0 else shape(count, 1, 128)
+
+
 def exchange(value, axes):
-    return lax.all_to_all(value, axes, 0, 0)
+    parts = lax.all_to_all(value.reshape(-1, 1, 128), axes, 0, 0)
+    return parts.reshape(value.shape)
 
 
 def on_device(sizes, energy, density, region, gamma_table):
@@ -400,18 +428,22 @@
         moved(up, "gy", 1),
         moved(down, "gy", -1),
     )
-    near, above, far = moved(own, GX, 1), moved(own, GX, -1), moved(last, GX, 2)
+    chips = members(GX) // 2
+    links = [(2 * i + 1, 2 * i + 2) for i in range(chips - 1)]
+    cross = lax.ppermute(own, GX, links + [(b, a) for a, b in links])
+    far = moved(last, GX, 2)
+    pair = lax.all_gather(own, GX[2])
     grid = (3 * 2 * 4 * 9 * 8, 128)
     fields, sums = call(
         functools.partial(krylov, sizes),
-        (shape(288, 128), shape(members(FIRST), 1, 128)),
+        (shape(288, 128), parts_shape(FIRST)),
         own,
+        pair,
+        cross,
         far,
-        near,
-        above,
         scratch=((9 * 128, 128), grid, grid, grid, (288, 128)),
     )
-    (sums,) = call(relay, (shape(members(SECOND), 1, 128),), exchange(sums, FIRST))
+    (sums,) = call(relay, (parts_shape(SECOND),), exchange(sums, FIRST))
     acceleration, residual = call(
         combine,
         (shape(96, 128), shape(96, 128)),

time: 89.2 us -> 84.6 us (0.948)
  Pallas kernels: 7.11 us -> 5.18 us
  starting transfers between devices: 30.3 us -> 28.4 us
  waiting for transfers between devices: 10.4 us -> 9.01 us
    ppermute x7 -> x5, starting transfers between devices: 30.3 us -> 22.2 us  [moved(): return lax.ppermute(value, axis, pairs)]
    ppermute x0 -> x1, starting transfers between devices: none -> 6.16 us  [on_device(): cross = lax.ppermute(own, GX, links + [(b, a) for a, b in links])]
    all_gather x0 -> x1, blocking collectives: none -> 2.02 us  [on_device(): pair = lax.all_gather(own, GX[2])]
    pallas_call x5, Pallas kernels: 5.77 us -> 3.88 us  [call(): pl.pallas_call(body, out_shape=tuple((place(o) for o in outs)), in_specs=...]
    ppermute x7 -> x5, waiting for transfers between devices: 10.4 us -> 9 us  [moved(): return lax.ppermute(value, axis, pairs)]
    all_to_all x2, blocking collectives: 40.3 us -> 38.9 us  [exchange(): parts = lax.all_to_all(value.reshape(-1, 1, 128), axes, 0, 0)]
  transfers between devices with their start and end apart: 7 -> 6, of which waited for: 3 -> 2; matrix products, arithmetic and copies ran while one was open for 0% -> 0% of each run, Pallas kernels for 0% -> 0%
where the time goes in v4:
time: 84.6 us; the launch traced here: 84.2 us
  blocking collectives  40.9 us (48%)
  starting transfers between devices  28.4 us (34%)
  waiting for transfers between devices  9.01 us (11%)
  Pallas kernels  5.18 us (6%)
    all_to_all x2, blocking collectives, exchange(): parts = lax.all_to_all(value.reshape(-1, 1, 128), axes, 0, 0)  38.9 us
    ppermute x5, starting transfers between devices, moved(): return lax.ppermute(value, axis, pairs)  22.2 us
    ppermute x5, waiting for transfers between devices, moved(): return lax.ppermute(value, axis, pairs)  9 us
    ppermute x1, starting transfers between devices, on_device(): cross = lax.ppermute(own, GX, links + [(b, a) for a, b in links])  6.16 us
    pallas_call x5, Pallas kernels, call(): pl.pallas_call(body, out_shape=tuple((place(o) for o in outs)), in_specs=...  3.88 us
    all_gather x1, blocking collectives, on_device(): pair = lax.all_gather(own, GX[2])  2.02 us
  transfers between devices with their start and end apart: 6, of which 2 were waited for; matrix products, arithmetic and copies ran while one was open for 0% of the time, Pallas kernels for 0%

profile of v4, /device:TPU:1, one launch (start us, length us, event | category | flops | bytes accessed | tf_op | source)
XLA Modules:
  0.0 84.2 jit_solution(6913097818936955452)
XLA Ops:
  0.6 1.3 %shard_map.59 = (f32[4,32,128]{2,1,0:T(8,128)S(1)}, f32[16,128]{1,0:T(8,128)S(1)}) custom-call(f32[6,12,192]{2,1,0:T(8,128)} %energy.1, f32[2,4,64]{2,1,0:T(4,128)} %density.1, s32[2,4,64]{2,1,0:T(4,128)} %region.1, f32[3]{0:T(128)} %gamma.1), custom_call_target="tpu_custom_call" | custom-call | tf_op jit(solution)/shard_map/pallas_call | solution.py:410
  1.9 1.3 %collective-permute-start.1 = (f32[16,128]{1,0:T(8,128)S(1)}, f32[16,128]{1,0:T(8,128)S(1)}, u32[]{:S(2)}, u32[]{:S(2)}) collective-permute-start(f32[16,128]{1,0:T(8,128)S(1)} %get-tuple-element.14), channel_id=1, source_target_pairs={{1,0},{2,1},{3,2},{4,3},{5,4},{6,5},{7,6},{9,8},{10,9},{11,10},{12... | collective-permute-start | bytes 24584 | tf_op jit(solution)/shard_map/ppermute | solution.py:373
  3.2 4.6 %collective-permute-start = (f32[16,128]{1,0:T(8,128)S(1)}, f32[16,128]{1,0:T(8,128)S(1)}, u32[]{:S(2)}, u32[]{:S(2)}) collective-permute-start(f32[16,128]{1,0:T(8,128)S(1)} %get-tuple-element.14), channel_id=1, source_target_pairs={{0,1},{1,2},{2,3},{3,4},{4,5},{5,6},{6,7},{8,9},{9,10},{10,11},{11... | collective-permute-start | bytes 24584 | tf_op jit(solution)/shard_map/ppermute | solution.py:373
  7.9 0.0 collective-permute-done.1.from_high
  7.9 0.8 collective-permute-done.from_low
  8.7 10.8 %collective-permute-start.2 = (f32[3,32,128]{2,1,0:T(8,128)S(1)}, f32[3,32,128]{2,1,0:T(8,128)S(1)}, u32[]{:S(2)}, u32[]{:S(2)}) collective-permute-start(f32[3,32,128]{2,1,0:T(8,128)S(1)} %get-tuple-element.16), channel_id=1, source_target_pairs={{0,8},{8,16},{1,9},{9,17},{2,10},{10,18},{3,11},{11,19},{4,12},{12... | collective-permute-start | bytes 147464 | tf_op jit(solution)/shard_map/ppermute | solution.py:373
  19.5 1.3 %collective-permute-start.3 = (f32[2,32,128]{2,1,0:T(8,128)S(1)}, f32[2,32,128]{2,1,0:T(8,128)S(1)}, u32[]{:S(2)}, u32[]{:S(2)}) collective-permute-start(f32[2,32,128]{2,1,0:T(8,128)S(1)} %get-tuple-element.17), channel_id=1, source_target_pairs={{8,0},{16,8},{9,1},{17,9},{10,2},{18,10},{11,3},{19,11},{12,4},{20... | collective-permute-start | bytes 98312 | tf_op jit(solution)/shard_map/ppermute | solution.py:373
  20.8 8.2 %collective-permute-done.3.from_high = f32[2,32,128]{2,1,0:T(8,128)S(1)} collective-permute-done((f32[2,32,128]{2,1,0:T(8,128)S(1)}, f32[2,32,128]{2,1,0:T(8,128)S(1)}, u32[]{:S(2)}, u32[]{:S(2)}) %collective-permute-start.3) | collective-permute-done | bytes 32800 | tf_op jit(solution)/shard_map/ppermute | solution.py:373
  29.0 0.0 collective-permute-done.2.from_low
  29.0 6.2 %collective-permute-start.4 = (f32[9,32,128]{2,1,0:T(8,128)S(1)}, f32[9,32,128]{2,1,0:T(8,128)S(1)}, u32[]{:S(2)}, u32[]{:S(2)}) collective-permute-start(f32[9,32,128]{2,1,0:T(8,128)S(1)} %get-tuple-element.18.own), channel_id=1, source_target_pairs={{24,48},{72,96},{120,144},{168,192},{216,240},{264,288},{312,336},... | collective-permute-start | bytes 442376 | tf_op jit(solution)/shard_map/ppermute | solution.py:433
  35.2 4.2 %collective-permute-start.5 = (f32[9,16,128]{2,1,0:T(8,128)S(1)}, f32[9,16,128]{2,1,0:T(8,128)S(1)}, u32[]{:S(2)}, u32[]{:S(2)}) collective-permute-start(f32[9,16,128]{2,1,0:T(8,128)S(1)} %get-tuple-element.19), channel_id=1, source_target_pairs={{0,48},{24,72},{48,96},{72,120},{96,144},{120,168},{144,192},{168,... | collective-permute-start | bytes 221192 | tf_op jit(solution)/shard_map/ppermute | solution.py:373
  39.4 2.0 %all-gather = f32[18,32,128]{2,1,0:T(8,128)S(1)} all-gather(f32[9,32,128]{2,1,0:T(8,128)S(1)} %get-tuple-element.18.own), channel_id=2, replica_groups=mesh['gx0'=4,'gx1'=4,'gx2'=2,'gy'=3,'gz'=8] {'gx2'}, dimensions={0}, use_global_device_ids=true | all-gather | bytes 442368 | tf_op jit(solution)/shard_map/all_gather | solution.py:435
  41.4 0.0 collective-permute-done.5.far
  41.4 0.0 collective-permute-done.4.cross
  41.4 3.0 %shard_map.62 = (f32[288,128]{1,0:T(8,128)S(1)}, f32[64,128]{1,0:T(8,128)S(1)}) custom-call(f32[9,32,128]{2,1,0:T(8,128)S(1)} %get-tuple-element.18.own, f32[2,9,32,128]{3,2,1,0:T(8,128)S(1)} %bitcast.7, f32[9,32,128]{2,1,0:T(8,128)S(1)} %collective-permute-done.4.cross, f32[9,16,128]{2,1,0:T(8,128)S(1)} %collective-permute-done.5.far), custom_call_target="tpu_custom_call" | custom-call | tf_op jit(solution)/shard_map/pallas_call | solution.py:383
  44.5 24.4 %all_to_all.10 = f32[64,1,128]{2,1,0:T(1,128)S(1)} all-to-all(f32[64,1,128]{2,1,0:T(1,128)S(1)} %bitcast.9), channel_id=1, replica_groups=mesh['gx0'=4,'gx1'=4,'gx2'=2,'gy'=3,'gz'=8] {'gx0','gz','gx2'}, dimensions={0} | all-to-all | bytes 65536 | tf_op jit(solution)/shard_map/all_to_all | solution.py:405
  68.9 14.6 %all_to_all.11.parts = f32[12,1,128]{2,1,0:T(1,128)S(1)} all-to-all(f32[12,1,128]{2,1,0:T(1,128)S(1)} %shard_map.63), channel_id=1, replica_groups=mesh['gx0'=4,'gx1'=4,'gx2'=2,'gy'=3,'gz'=8] {'gy','gx1'}, dimensions={0} | all-to-all | bytes 12288 | tf_op jit(solution)/shard_map/all_to_all | solution.py:405
  83.4 0.8 shard_map.64
  (3 shorter events, 0.0 us)
Async XLA Ops:
  1.9 6.0 %collective-permute-start.1 = (f32[16,128]{1,0:T(8,128)S(1)}, f32[16,128]{1,0:T(8,128)S(1)}, u32[]{:S(2)}, u32[]{:S(2)}) collective-permute-start(f32[16,128]{1,0:T(8,128)S(1)} %get-tuple-element.14), channel_id=1, source_target_pairs={{1,0},{2,1},{3,2},{4,3},{5,4},{6,5},{7,6},{9,8},{10,9},{11,10},{12... | collective-permute-start | bytes 24584 | tf_op jit(solution)/shard_map/ppermute | solution.py:373
  3.2 5.4 %collective-permute-start = (f32[16,128]{1,0:T(8,128)S(1)}, f32[16,128]{1,0:T(8,128)S(1)}, u32[]{:S(2)}, u32[]{:S(2)}) collective-permute-start(f32[16,128]{1,0:T(8,128)S(1)} %get-tuple-element.14), channel_id=1, source_target_pairs={{0,1},{1,2},{2,3},{3,4},{4,5},{5,6},{6,7},{8,9},{9,10},{10,11},{11... | collective-permute-start | bytes 24584 | tf_op jit(solution)/shard_map/ppermute | solution.py:373
  8.7 20.3 %collective-permute-start.2 = (f32[3,32,128]{2,1,0:T(8,128)S(1)}, f32[3,32,128]{2,1,0:T(8,128)S(1)}, u32[]{:S(2)}, u32[]{:S(2)}) collective-permute-start(f32[3,32,128]{2,1,0:T(8,128)S(1)} %get-tuple-element.16), channel_id=1, source_target_pairs={{0,8},{8,16},{1,9},{9,17},{2,10},{10,18},{3,11},{11,19},{4,12},{12... | collective-permute-start | bytes 147464 | tf_op jit(solution)/shard_map/ppermute | solution.py:373
  19.5 9.5 %collective-permute-start.3 = (f32[2,32,128]{2,1,0:T(8,128)S(1)}, f32[2,32,128]{2,1,0:T(8,128)S(1)}, u32[]{:S(2)}, u32[]{:S(2)}) collective-permute-start(f32[2,32,128]{2,1,0:T(8,128)S(1)} %get-tuple-element.17), channel_id=1, source_target_pairs={{8,0},{16,8},{9,1},{17,9},{10,2},{18,10},{11,3},{19,11},{12,4},{20... | collective-permute-start | bytes 98312 | tf_op jit(solution)/shard_map/ppermute | solution.py:373
  29.0 12.4 %collective-permute-start.4 = (f32[9,32,128]{2,1,0:T(8,128)S(1)}, f32[9,32,128]{2,1,0:T(8,128)S(1)}, u32[]{:S(2)}, u32[]{:S(2)}) collective-permute-start(f32[9,32,128]{2,1,0:T(8,128)S(1)} %get-tuple-element.18.own), channel_id=1, source_target_pairs={{24,48},{72,96},{120,144},{168,192},{216,240},{264,288},{312,336},... | collective-permute-start | bytes 442376 | tf_op jit(solution)/shard_map/ppermute | solution.py:433
  35.2 6.3 %collective-permute-start.5 = (f32[9,16,128]{2,1,0:T(8,128)S(1)}, f32[9,16,128]{2,1,0:T(8,128)S(1)}, u32[]{:S(2)}, u32[]{:S(2)}) collective-permute-start(f32[9,16,128]{2,1,0:T(8,128)S(1)} %get-tuple-element.19), channel_id=1, source_target_pairs={{0,48},{24,72},{48,96},{72,120},{96,144},{120,168},{144,192},{168,... | collective-permute-start | bytes 221192 | tf_op jit(solution)/shard_map/ppermute | solution.py:373

commit v5 on v4

--- a/solution.py
+++ b/solution.py
@@ -91,30 +91,43 @@
             message_out[place + 1 : place + 2, :] = one
 
 
-def fill_z(rows, from_low, from_high, rows_out, up_out, down_out):
+def fill_z(rows, even, odd, rows_out, slots_out):
     lane = iota((16, 128), 1)
-    halo = jnp.where((lane < 50) | (lane >= 110), from_low[...], from_high[...])
+    place_z = lax.axis_index("gz")
+    swapped = place_z % 2 == 1
+    from_low = jnp.where(swapped, even[...], odd[...])
+    from_high = jnp.where(swapped, odd[...], even[...])
+    halo = jnp.where((lane < 50) | (lane >= 110), from_low, from_high)
+    me = lax.axis_index("gy")
     for y in range(4):
+        blocks = []
         for x in range(2):
             base = 16 * x
             place = y * 4 + x * 2
             block = rows[y, base : base + 16, :]
-            block = jnp.concatenate([block[:PAIRS], halo[place : place + 2]], axis=0)
-            rows_out[y, base : base + 16, :] = block
-            if y >= 1:
-                up_out[y - 1, base : base + 16, :] = block
-            if y < HIGH:
-                down_out[y, base : base + 16, :] = block
-
-
-def fill_y(rows, from_low, from_high, rows_out, last_out):
-    for y in range(9):
+            blocks.append(jnp.concatenate([block[:PAIRS], halo[place : place + 2]], axis=0))
+        rows_out[y] = jnp.concatenate(blocks, axis=0)
+    for to in range(slots_out.shape[0]):
+        first = jnp.where(to > me, 1, 0)
+        for k in range(LOW):
+            slots_out[to, 32 * k : 32 * k + 32, :] = rows_out[first + k]
+
+
+def fill_y(rows, slots, rows_out, last_out):
+    me = lax.axis_index("gy")
+    count = slots.shape[0]
+    below = jnp.maximum(me - 1, 0)
+    above = jnp.minimum(me + 1, count - 1)
+    for y in range(LOW + 4 + HIGH):
         if y < LOW:
-            block = from_low[y]
+            block = slots[below, 32 * y : 32 * y + 32, :]
+            block = jnp.where(me > 0, block, 0.0)
         elif y < LOW + 4:
             block = rows[y - LOW]
         else:
-            block = from_high[y - LOW - 4]
+            at = 32 * (y - LOW - 4)
+            block = slots[above, at : at + 32, :]
+            block = jnp.where(me < count - 1, block, 0.0)
         rows_out[y] = block
         last_out[y] = block[16:32]
 
@@ -373,6 +386,11 @@
     return lax.ppermute(value, axis, pairs)
 
 
+def swapped(value, axis, first):
+    links = [(i, i + 1) for i in range(first, lax.axis_size(axis) - 1, 2)]
+    return lax.ppermute(value, axis, links + [(b, a) for a, b in links])
+
+
 def shape(*dims):
     return jax.ShapeDtypeStruct(dims, jnp.float32)
 
@@ -414,19 +432,18 @@
         out_specs=tuple(vmem(2)),
         scratch_shapes=[pltpu.VMEM((96, 192), jnp.float32), pltpu.VMEM((96, 256), jnp.float32)],
     )(energy, density, region, gamma_table)
-    rows, up, down = call(
+    rows, slots = call(
         fill_z,
-        (shape(4, 32, 128), shape(3, 32, 128), shape(2, 32, 128)),
+        (shape(4, 32, 128), shape(lax.axis_size("gy"), 32 * LOW, 128)),
         rows,
-        moved(message, "gz", 1),
-        moved(message, "gz", -1),
+        swapped(message, "gz", 0),
+        swapped(message, "gz", 1),
     )
     own, last = call(
         fill_y,
         (shape(9, 32, 128), shape(9, 16, 128)),
         rows,
-        moved(up, "gy", 1),
-        moved(down, "gy", -1),
+        lax.all_to_all(slots, "gy", 0, 0),
     )
     chips = members(GX) // 2
     links = [(2 * i + 1, 2 * i + 2) for i in range(chips - 1)]

time: 84.6 us -> 82.7 us (0.978)
  blocking collectives: 40.9 us -> 57.6 us
  starting transfers between devices: 28.4 us -> 17.8 us
  waiting for transfers between devices: 9.01 us -> 1.02 us
    all_to_all x0 -> x1, blocking collectives: none -> 20.7 us  [on_device(): lax.all_to_all(slots, 'gy', 0, 0)]
    ppermute x5 -> x1, starting transfers between devices: 22.2 us -> 3.1 us  [moved(): return lax.ppermute(value, axis, pairs)]
    ppermute x5 -> x1, waiting for transfers between devices: 9 us -> 0.01 us  [moved(): return lax.ppermute(value, axis, pairs)]
    ppermute x0 -> x2, starting transfers between devices: none -> 7.22 us  [swapped(): return lax.ppermute(value, axis, links + [(b, a) for a, b in links])]
    all_to_all x2, blocking collectives: 38.9 us -> 34.9 us  [exchange(): parts = lax.all_to_all(value.reshape(-1, 1, 128), axes, 0, 0)]
    ppermute x1, starting transfers between devices: 6.16 us -> 7.52 us  [on_device(): cross = lax.ppermute(own, GX, links + [(b, a) for a, b in links])]
    ppermute x0 -> x2, waiting for transfers between devices: none -> 1.02 us  [swapped(): return lax.ppermute(value, axis, links + [(b, a) for a, b in links])]
  transfers between devices with their start and end apart: 6 -> 4, of which waited for: 2 -> 1; matrix products, arithmetic and copies ran while one was open for 0% -> 0% of each run, Pallas kernels for 0% -> 0%
where the time goes in v5:
time: 82.7 us; the launch traced here: 82.4 us
  blocking collectives  57.6 us (70%)
  starting transfers between devices  17.8 us (22%)
  Pallas kernels  5.19 us (6%)
  waiting for transfers between devices  1.02 us (1%)
    all_to_all x2, blocking collectives, exchange(): parts = lax.all_to_all(value.reshape(-1, 1, 128), axes, 0, 0)  34.9 us
    all_to_all x1, blocking collectives, on_device(): lax.all_to_all(slots, 'gy', 0, 0)  20.7 us
    ppermute x1, starting transfers between devices, on_device(): cross = lax.ppermute(own, GX, links + [(b, a) for a, b in links])  7.52 us
    ppermute x2, starting transfers between devices, swapped(): return lax.ppermute(value, axis, links + [(b, a) for a, b in links])  7.22 us
    pallas_call x5, Pallas kernels, call(): pl.pallas_call(body, out_shape=tuple((place(o) for o in outs)), in_specs=...  3.9 us
    ppermute x1, starting transfers between devices, moved(): return lax.ppermute(value, axis, pairs)  3.1 us
    all_gather x1, blocking collectives, on_device(): pair = lax.all_gather(own, GX[2])  2.02 us
  transfers between devices with their start and end apart: 4, of which 1 were waited for; matrix products, arithmetic and copies ran while one was open for 0% of the time, Pallas kernels for 0%

profile of v5, /device:TPU:1, one launch (start us, length us, event | category | flops | bytes accessed | tf_op | source)
XLA Modules:
  0.0 82.4 jit_solution(5838205220058068350)
XLA Ops:
  0.6 1.3 %shard_map.59 = (f32[4,32,128]{2,1,0:T(8,128)S(1)}, f32[16,128]{1,0:T(8,128)S(1)}) custom-call(f32[6,12,192]{2,1,0:T(8,128)} %energy.1, f32[2,4,64]{2,1,0:T(4,128)} %density.1, s32[2,4,64]{2,1,0:T(4,128)} %region.1, f32[3]{0:T(128)} %gamma.1), custom_call_target="tpu_custom_call" | custom-call | tf_op jit(solution)/shard_map/pallas_call | solution.py:428
  1.9 0.7 collective-permute-start.1
  2.6 6.6 %collective-permute-start = (f32[16,128]{1,0:T(8,128)S(1)}, f32[16,128]{1,0:T(8,128)S(1)}, u32[]{:S(2)}, u32[]{:S(2)}) collective-permute-start(f32[16,128]{1,0:T(8,128)S(1)} %get-tuple-element.13), channel_id=1, source_target_pairs={{0,1},{2,3},{4,5},{6,7},{1,0},{3,2},{5,4},{7,6},{8,9},{10,11},{12,... | collective-permute-start | bytes 24584 | tf_op jit(solution)/shard_map/ppermute | solution.py:391
  9.2 0.0 collective-permute-done.1.odd
  9.2 1.0 %collective-permute-done.even = f32[16,128]{1,0:T(8,128)S(1)} collective-permute-done((f32[16,128]{1,0:T(8,128)S(1)}, f32[16,128]{1,0:T(8,128)S(1)}, u32[]{:S(2)}, u32[]{:S(2)}) %collective-permute-start) | collective-permute-done | bytes 8224 | tf_op jit(solution)/shard_map/ppermute | solution.py:391
  10.2 20.7 %all_to_all.15.slots = f32[3,96,128]{2,1,0:T(8,128)S(1)} all-to-all(f32[3,96,128]{2,1,0:T(8,128)S(1)} %get-tuple-element.15), channel_id=1, replica_groups=mesh['gx0'=4,'gx1'=4,'gx2'=2,'gy'=3,'gz'=8] {'gy'}, dimensions={0} | all-to-all | bytes 294912 | tf_op jit(solution)/shard_map/all_to_all | solution.py:446
  30.9 7.5 %collective-permute-start.2 = (f32[9,32,128]{2,1,0:T(8,128)S(1)}, f32[9,32,128]{2,1,0:T(8,128)S(1)}, u32[]{:S(2)}, u32[]{:S(2)}) collective-permute-start(f32[9,32,128]{2,1,0:T(8,128)S(1)} %get-tuple-element.16.own), channel_id=1, source_target_pairs={{24,48},{72,96},{120,144},{168,192},{216,240},{264,288},{312,336},... | collective-permute-start | bytes 442376 | tf_op jit(solution)/shard_map/ppermute | solution.py:450
  38.4 3.1 %collective-permute-start.3 = (f32[9,16,128]{2,1,0:T(8,128)S(1)}, f32[9,16,128]{2,1,0:T(8,128)S(1)}, u32[]{:S(2)}, u32[]{:S(2)}) collective-permute-start(f32[9,16,128]{2,1,0:T(8,128)S(1)} %get-tuple-element.17), channel_id=1, source_target_pairs={{0,48},{24,72},{48,96},{72,120},{96,144},{120,168},{144,192},{168,... | collective-permute-start | bytes 221192 | tf_op jit(solution)/shard_map/ppermute | solution.py:386
  41.5 2.0 %all-gather = f32[18,32,128]{2,1,0:T(8,128)S(1)} all-gather(f32[9,32,128]{2,1,0:T(8,128)S(1)} %get-tuple-element.16.own), channel_id=2, replica_groups=mesh['gx0'=4,'gx1'=4,'gx2'=2,'gy'=3,'gz'=8] {'gx2'}, dimensions={0}, use_global_device_ids=true | all-gather | bytes 442368 | tf_op jit(solution)/shard_map/all_gather | solution.py:452
  43.6 0.0 collective-permute-done.3.far
  43.6 0.0 collective-permute-done.2.cross
  43.6 3.0 %shard_map.62 = (f32[288,128]{1,0:T(8,128)S(1)}, f32[64,128]{1,0:T(8,128)S(1)}) custom-call(f32[9,32,128]{2,1,0:T(8,128)S(1)} %get-tuple-element.16.own, f32[2,9,32,128]{3,2,1,0:T(8,128)S(1)} %bitcast.7, f32[9,32,128]{2,1,0:T(8,128)S(1)} %collective-permute-done.2.cross, f32[9,16,128]{2,1,0:T(8,128)S(1)} %collective-permute-done.3.far), custom_call_target="tpu_custom_call" | custom-call | tf_op jit(solution)/shard_map/pallas_call | solution.py:401
  46.6 22.3 %all_to_all.16 = f32[64,1,128]{2,1,0:T(1,128)S(1)} all-to-all(f32[64,1,128]{2,1,0:T(1,128)S(1)} %bitcast.9), channel_id=1, replica_groups=mesh['gx0'=4,'gx1'=4,'gx2'=2,'gy'=3,'gz'=8] {'gx0','gz','gx2'}, dimensions={0} | all-to-all | bytes 65536 | tf_op jit(solution)/shard_map/all_to_all | solution.py:423
  68.9 12.6 %all_to_all.17.parts = f32[12,1,128]{2,1,0:T(1,128)S(1)} all-to-all(f32[12,1,128]{2,1,0:T(1,128)S(1)} %shard_map.63), channel_id=1, replica_groups=mesh['gx0'=4,'gx1'=4,'gx2'=2,'gy'=3,'gz'=8] {'gy','gx1'}, dimensions={0} | all-to-all | bytes 12288 | tf_op jit(solution)/shard_map/all_to_all | solution.py:423
  81.6 0.8 shard_map.64
  (3 shorter events, 0.1 us)
Async XLA Ops:
  1.9 7.2 %collective-permute-start.1 = (f32[16,128]{1,0:T(8,128)S(1)}, f32[16,128]{1,0:T(8,128)S(1)}, u32[]{:S(2)}, u32[]{:S(2)}) collective-permute-start(f32[16,128]{1,0:T(8,128)S(1)} %get-tuple-element.13), channel_id=1, source_target_pairs={{1,2},{3,4},{5,6},{2,1},{4,3},{6,5},{9,10},{11,12},{13,14},{10,9},... | collective-permute-start | bytes 24584 | tf_op jit(solution)/shard_map/ppermute | solution.py:391
  2.6 7.6 %collective-permute-start = (f32[16,128]{1,0:T(8,128)S(1)}, f32[16,128]{1,0:T(8,128)S(1)}, u32[]{:S(2)}, u32[]{:S(2)}) collective-permute-start(f32[16,128]{1,0:T(8,128)S(1)} %get-tuple-element.13), channel_id=1, source_target_pairs={{0,1},{2,3},{4,5},{6,7},{1,0},{3,2},{5,4},{7,6},{8,9},{10,11},{12,... | collective-permute-start | bytes 24584 | tf_op jit(solution)/shard_map/ppermute | solution.py:391
  30.9 12.7 %collective-permute-start.2 = (f32[9,32,128]{2,1,0:T(8,128)S(1)}, f32[9,32,128]{2,1,0:T(8,128)S(1)}, u32[]{:S(2)}, u32[]{:S(2)}) collective-permute-start(f32[9,32,128]{2,1,0:T(8,128)S(1)} %get-tuple-element.16.own), channel_id=1, source_target_pairs={{24,48},{72,96},{120,144},{168,192},{216,240},{264,288},{312,336},... | collective-permute-start | bytes 442376 | tf_op jit(solution)/shard_map/ppermute | solution.py:450
  38.4 5.1 %collective-permute-start.3 = (f32[9,16,128]{2,1,0:T(8,128)S(1)}, f32[9,16,128]{2,1,0:T(8,128)S(1)}, u32[]{:S(2)}, u32[]{:S(2)}) collective-permute-start(f32[9,16,128]{2,1,0:T(8,128)S(1)} %get-tuple-element.17), channel_id=1, source_target_pairs={{0,48},{24,72},{48,96},{72,120},{96,144},{120,168},{144,192},{168,... | collective-permute-start | bytes 221192 | tf_op jit(solution)/shard_map/ppermute | solution.py:386

commit v6 on v5

--- a/solution.py
+++ b/solution.py
@@ -15,6 +15,7 @@
 EDGE_W, MID_W = 5.0 / 18.0, 8.0 / 18.0
 UNROLL = (3, 5, 3)
 GX = ("gx0", "gx1", "gx2")
+GZ = ("gz0", "gz1")
 
 
 def vmem(count):
@@ -93,10 +94,10 @@
 
 def fill_z(rows, even, odd, rows_out, slots_out):
     lane = iota((16, 128), 1)
-    place_z = lax.axis_index("gz")
-    swapped = place_z % 2 == 1
-    from_low = jnp.where(swapped, even[...], odd[...])
-    from_high = jnp.where(swapped, odd[...], even[...])
+    second = lax.axis_index(GZ[1]) == 1
+    partner = even[1 - lax.axis_index(GZ[1])]
+    from_low = jnp.where(second, partner, odd[...])
+    from_high = jnp.where(second, odd[...], partner)
     halo = jnp.where((lane < 50) | (lane >= 110), from_low, from_high)
     me = lax.axis_index("gy")
     for y in range(4):
@@ -193,7 +194,8 @@
 
     sub, lane = iota((8, 128), 0), iota((8, 128), 1)
     at_x = 2 * index_x + sub - LOW
-    at_z = 64 * lax.axis_index("gz") + jnp.where(lane < 96, lane, lane - 128)
+    index_z = lax.axis_index(GZ[0]) * lax.axis_size(GZ[1]) + lax.axis_index(GZ[1])
+    at_z = 64 * index_z + jnp.where(lane < 96, lane, lane - 128)
     inside_x = (at_x > 0) & (at_x < size_x)
     inside_z = (at_z > 0) & (at_z < size_z)
     inside = {
@@ -380,15 +382,14 @@
         residual_out[32 * d : 32 * d + 32, :] = (v0 - alpha * v1) - alpha_2 * image
 
 
-def moved(value, axis, by):
-    count = lax.axis_size(axis)
-    pairs = [(i, i + by) for i in range(count) if 0 <= i + by < count]
-    return lax.ppermute(value, axis, pairs)
-
-
-def swapped(value, axis, first):
-    links = [(i, i + 1) for i in range(first, lax.axis_size(axis) - 1, 2)]
-    return lax.ppermute(value, axis, links + [(b, a) for a, b in links])
+def moved(value, axes, by):
+    pairs = [(i, i + by) for i in range(members(axes) - by)]
+    return lax.ppermute(value, axes, pairs)
+
+
+def swapped(value, axes):
+    links = [(i, i + 1) for i in range(1, members(axes) - 1, 2)]
+    return lax.ppermute(value, axes, links + [(b, a) for a, b in links])
 
 
 def shape(*dims):
@@ -407,7 +408,7 @@
     )(*kept)
 
 
-FIRST, SECOND = ("gx0", "gz", "gx2"), ("gy", "gx1")
+FIRST, SECOND = ("gx0", *GZ, "gx2"), ("gy", "gx1")
 
 
 def members(axes):
@@ -436,8 +437,8 @@
         fill_z,
         (shape(4, 32, 128), shape(lax.axis_size("gy"), 32 * LOW, 128)),
         rows,
-        swapped(message, "gz", 0),
-        swapped(message, "gz", 1),
+        lax.all_gather(message, GZ[1]),
+        swapped(message, GZ),
     )
     own, last = call(
         fill_y,
@@ -445,9 +446,7 @@
         rows,
         lax.all_to_all(slots, "gy", 0, 0),
     )
-    chips = members(GX) // 2
-    links = [(2 * i + 1, 2 * i + 2) for i in range(chips - 1)]
-    cross = lax.ppermute(own, GX, links + [(b, a) for a, b in links])
+    cross = swapped(own, GX)
     far = moved(last, GX, 2)
     pair = lax.all_gather(own, GX[2])
     grid = (3 * 2 * 4 * 9 * 8, 128)
@@ -479,11 +478,12 @@
 
 def solution(mesh):
     count = mesh.shape["gx"]
-    devices = mesh.devices.reshape(*split(count), mesh.shape["gy"], mesh.shape["gz"])
-    finer = Mesh(devices, (*GX, "gy", "gz"))
-    sizes = (2 * count, 4 * mesh.shape["gy"], 64 * mesh.shape["gz"])
-    place = P(GX, "gy", "gz")
-    out = P(None, GX, "gy", "gz")
+    depth = mesh.shape["gz"]
+    devices = mesh.devices.reshape(*split(count), mesh.shape["gy"], depth // 2, 2)
+    finer = Mesh(devices, (*GX, "gy", *GZ))
+    sizes = (2 * count, 4 * mesh.shape["gy"], 64 * depth)
+    place = P(GX, "gy", GZ)
+    out = P(None, GX, "gy", GZ)
     return jax.shard_map(
         functools.partial(on_device, sizes),
         mesh=finer,

time: 82.7 us -> 81.5 us (0.985)
  starting transfers between devices: 17.8 us -> 11.3 us
  blocking collectives: 57.6 us -> 64 us
  waiting for transfers between devices: 1.02 us -> 0.01 us
    ppermute x4 -> x3, starting transfers between devices: 17.8 us -> 11.3 us  [the longest x2 8.18 us: swapped(): return lax.ppermute(value, axes, links + [(b, a) for a, b in links])]
    all_gather x0 -> x1, blocking collectives: none -> 6.39 us  [on_device(): lax.all_gather(message, GZ[1])]
    ppermute x4 -> x3, waiting for transfers between devices: 1.02 us -> 0.01 us  [the longest x2 0.01 us: swapped(): return lax.ppermute(value, axes, links + [(b, a) for a, b in links])]
  transfers between devices with their start and end apart: 4 -> 3, of which waited for: 1 -> 0; matrix products, arithmetic and copies ran while one was open for 0% -> 0% of each run, Pallas kernels for 0% -> 0%
where the time goes in v6:
time: 81.5 us; the launch traced here: 81.2 us
  blocking collectives  64 us (79%)
  starting transfers between devices  11.3 us (14%)
  Pallas kernels  5.2 us (6%)
    all_to_all x2, blocking collectives, exchange(): parts = lax.all_to_all(value.reshape(-1, 1, 128), axes, 0, 0)  34.9 us
    all_to_all x1, blocking collectives, on_device(): lax.all_to_all(slots, 'gy', 0, 0)  20.7 us
    ppermute x2, starting transfers between devices, swapped(): return lax.ppermute(value, axes, links + [(b, a) for a, b in links])  8.18 us
    all_gather x1, blocking collectives, on_device(): lax.all_gather(message, GZ[1])  6.39 us
    pallas_call x5, Pallas kernels, call(): pl.pallas_call(body, out_shape=tuple((place(o) for o in outs)), in_specs=...  3.9 us
    ppermute x1, starting transfers between devices, moved(): return lax.ppermute(value, axes, pairs)  3.1 us
    all_gather x1, blocking collectives, on_device(): pair = lax.all_gather(own, GX[2])  2.02 us
  transfers between devices with their start and end apart: 3, of which 0 were waited for; matrix products, arithmetic and copies ran while one was open for 0% of the time, Pallas kernels for 0%

profile of v6, /device:TPU:1, one launch (start us, length us, event | category | flops | bytes accessed | tf_op | source)
XLA Modules:
  0.0 81.2 jit_solution(14401887597701864063)
XLA Ops:
  0.6 1.3 %shard_map.59 = (f32[4,32,128]{2,1,0:T(8,128)S(1)}, f32[16,128]{1,0:T(8,128)S(1)}) custom-call(f32[6,12,192]{2,1,0:T(8,128)} %energy.1, f32[2,4,64]{2,1,0:T(4,128)} %density.1, s32[2,4,64]{2,1,0:T(4,128)} %region.1, f32[3]{0:T(128)} %gamma.1), custom_call_target="tpu_custom_call" | custom-call | tf_op jit(solution)/shard_map/pallas_call | solution.py:429
  1.9 0.7 collective-permute-start
  2.6 6.4 %all-gather = f32[32,128]{1,0:T(8,128)S(1)} all-gather(f32[16,128]{1,0:T(8,128)S(1)} %get-tuple-element.13), channel_id=2, replica_groups=mesh['gx0'=4,'gx1'=4,'gx2'=2,'gy'=3,'gz0'=4,'gz1'=2] {'gz1'}, dimensions={0}, use_global_device_ids=true | all-gather | bytes 24576 | tf_op jit(solution)/shard_map/all_gather | solution.py:440
  9.0 0.0 collective-permute-done.odd
  9.0 20.7 %all_to_all.15.slots = f32[3,96,128]{2,1,0:T(8,128)S(1)} all-to-all(f32[3,96,128]{2,1,0:T(8,128)S(1)} %get-tuple-element.15), channel_id=1, replica_groups=mesh['gx0'=4,'gx1'=4,'gx2'=2,'gy'=3,'gz0'=4,'gz1'=2] {'gy'}, dimensions={0} | all-to-all | bytes 294912 | tf_op jit(solution)/shard_map/all_to_all | solution.py:447
  29.7 7.5 %collective-permute-start.1 = (f32[9,32,128]{2,1,0:T(8,128)S(1)}, f32[9,32,128]{2,1,0:T(8,128)S(1)}, u32[]{:S(2)}, u32[]{:S(2)}) collective-permute-start(f32[9,32,128]{2,1,0:T(8,128)S(1)} %get-tuple-element.16.own), channel_id=1, source_target_pairs={{24,48},{72,96},{120,144},{168,192},{216,240},{264,288},{312,336},... | collective-permute-start | bytes 442376 | tf_op jit(solution)/shard_map/ppermute | solution.py:392
  37.2 3.1 %collective-permute-start.2 = (f32[9,16,128]{2,1,0:T(8,128)S(1)}, f32[9,16,128]{2,1,0:T(8,128)S(1)}, u32[]{:S(2)}, u32[]{:S(2)}) collective-permute-start(f32[9,16,128]{2,1,0:T(8,128)S(1)} %get-tuple-element.17), channel_id=1, source_target_pairs={{0,48},{24,72},{48,96},{72,120},{96,144},{120,168},{144,192},{168,... | collective-permute-start | bytes 221192 | tf_op jit(solution)/shard_map/ppermute | solution.py:387
  40.3 2.0 %all-gather.1 = f32[18,32,128]{2,1,0:T(8,128)S(1)} all-gather(f32[9,32,128]{2,1,0:T(8,128)S(1)} %get-tuple-element.16.own), channel_id=3, replica_groups=mesh['gx0'=4,'gx1'=4,'gx2'=2,'gy'=3,'gz0'=4,'gz1'=2] {'gx2'}, dimensions={0}, use_global_device_ids=true | all-gather | bytes 442368 | tf_op jit(solution)/shard_map/all_gather | solution.py:451
  42.4 0.0 collective-permute-done.2.far
  42.4 0.0 collective-permute-done.1.cross
  42.4 3.0 %shard_map.62 = (f32[288,128]{1,0:T(8,128)S(1)}, f32[64,128]{1,0:T(8,128)S(1)}) custom-call(f32[9,32,128]{2,1,0:T(8,128)S(1)} %get-tuple-element.16.own, f32[2,9,32,128]{3,2,1,0:T(8,128)S(1)} %bitcast.8, f32[9,32,128]{2,1,0:T(8,128)S(1)} %collective-permute-done.1.cross, f32[9,16,128]{2,1,0:T(8,128)S(1)} %collective-permute-done.2.far), custom_call_target="tpu_custom_call" | custom-call | tf_op jit(solution)/shard_map/pallas_call | solution.py:402
  45.4 22.2 %all_to_all.16 = f32[64,1,128]{2,1,0:T(1,128)S(1)} all-to-all(f32[64,1,128]{2,1,0:T(1,128)S(1)} %bitcast.11), channel_id=1, replica_groups=mesh['gx0'=4,'gx1'=4,'gx2'=2,'gy'=3,'gz0'=4,'gz1'=2] {'gx0','gz0','gz1',..., dimensions={0} | all-to-all | bytes 65536 | tf_op jit(solution)/shard_map/all_to_all | solution.py:424
  67.6 12.8 %all_to_all.17.parts = f32[12,1,128]{2,1,0:T(1,128)S(1)} all-to-all(f32[12,1,128]{2,1,0:T(1,128)S(1)} %shard_map.63), channel_id=1, replica_groups=mesh['gx0'=4,'gx1'=4,'gx2'=2,'gy'=3,'gz0'=4,'gz1'=2] {'gy','gx1'}, dimensions={0} | all-to-all | bytes 12288 | tf_op jit(solution)/shard_map/all_to_all | solution.py:424
  80.4 0.8 shard_map.64
  (3 shorter events, 0.1 us)
Async XLA Ops:
  1.9 7.1 %collective-permute-start = (f32[16,128]{1,0:T(8,128)S(1)}, f32[16,128]{1,0:T(8,128)S(1)}, u32[]{:S(2)}, u32[]{:S(2)}) collective-permute-start(f32[16,128]{1,0:T(8,128)S(1)} %get-tuple-element.13), channel_id=1, source_target_pairs={{1,2},{3,4},{5,6},{2,1},{4,3},{6,5},{9,10},{11,12},{13,14},{10,9},... | collective-permute-start | bytes 24584 | tf_op jit(solution)/shard_map/ppermute | solution.py:392
  29.7 12.7 %collective-permute-start.1 = (f32[9,32,128]{2,1,0:T(8,128)S(1)}, f32[9,32,128]{2,1,0:T(8,128)S(1)}, u32[]{:S(2)}, u32[]{:S(2)}) collective-permute-start(f32[9,32,128]{2,1,0:T(8,128)S(1)} %get-tuple-element.16.own), channel_id=1, source_target_pairs={{24,48},{72,96},{120,144},{168,192},{216,240},{264,288},{312,336},... | collective-permute-start | bytes 442376 | tf_op jit(solution)/shard_map/ppermute | solution.py:392
  37.2 5.1 %collective-permute-start.2 = (f32[9,16,128]{2,1,0:T(8,128)S(1)}, f32[9,16,128]{2,1,0:T(8,128)S(1)}, u32[]{:S(2)}, u32[]{:S(2)}) collective-permute-start(f32[9,16,128]{2,1,0:T(8,128)S(1)} %get-tuple-element.17), channel_id=1, source_target_pairs={{0,48},{24,72},{48,96},{72,120},{96,144},{120,168},{144,192},{168,... | collective-permute-start | bytes 221192 | tf_op jit(solution)/shard_map/ppermute | solution.py:387

commit v7 on v6

--- a/solution.py
+++ b/solution.py
@@ -11,9 +11,10 @@
 
 LOW, HIGH = 3, 2
 PAIRS = 14
+CORNERS = ((0, 0), (0, 1), (1, 0), (1, 1))
 ROOT = math.sqrt(0.15)
 EDGE_W, MID_W = 5.0 / 18.0, 8.0 / 18.0
-UNROLL = (3, 5, 3)
+UNROLL = (9, 5, 3, 9)
 GX = ("gx0", "gx1", "gx2")
 GZ = ("gz0", "gz1")
 
@@ -140,6 +141,13 @@
     return outer + inner, total + 8.0 * m, outer - inner
 
 
+def weighted_op(v, m, w, rhos):
+    total, gap = v + w, v - w
+    outer = rhos[1] * total + rhos[0] * m
+    inner = rhos[2] * gap
+    return outer + inner, rhos[0] * total + rhos[3] * m, outer - inner
+
+
 def by_values(q0, q1, q2):
     total, gap = q0 + q2, q0 - q2
     outer, inner = 0.3 * total, ROOT * gap
@@ -168,7 +176,7 @@
     return pltpu.roll(value, 7, 0)
 
 
-def krylov(sizes, own, pair, cross, far, fields_out, sums_out, points, base, image, second, flat):
+def krylov(sizes, own, pair, cross, far, fields_out, sums_out, points, ready, base, image, second, flat):
     size_x, size_y, size_z = sizes
     index_x = (lax.axis_index(GX[0]) * lax.axis_size(GX[1]) + lax.axis_index(GX[1])) * (
         lax.axis_size(GX[2])
@@ -223,21 +231,35 @@
             side = pltpu.roll(side, 128 - 3 * p, 1)
         return jnp.where(mine, main, side)
 
+    def walls(y):
+        wall = inside_y(y)
+        return {at: inside[at] * wall if at in inside else wall for at in CORNERS}
+
     def put(ref, d, xc, zc, y, vertex, middle, wall):
         if (xc, zc) in inside:
-            vertex = vertex * inside[xc, zc]
             middle = None if middle is None else middle * inside[xc, zc]
-        tile(ref, d, 0, xc, zc, y)[...] = vertex * wall
+        tile(ref, d, 0, xc, zc, y)[...] = vertex * wall[xc, zc]
         if middle is not None:
             tile(ref, d, 1, xc, zc, y)[...] = middle
 
+    def ready_tile(y, q, qz):
+        return ready.at[pl.ds(pl.multiple_of(y * 216 + (3 * q + qz) * 8, 8), 8), :]
+
+    def unpack_row(y, carry):
+        for q in range(9):
+            for qz in range(3):
+                ready_tile(y, q, qz)[...] = point(y, *class_of(q, qz))
+        return carry
+
+    lax.fori_loop(0, 9, unpack_row, 0, unroll=UNROLL[3])
+
     def force_row(y, carry):
-        wall = inside_y(y)
+        wall = walls(y)
         lines = {}
         for qy in range(3):
             value_z, slope_z = {}, {}
             for qx in range(3):
-                q0, q1, q2 = (point(y, *class_of(3 * qx + qy, qz)) for qz in range(3))
+                q0, q1, q2 = (ready_tile(y, 3 * qx + qy, qz)[...] for qz in range(3))
                 n0, n1, n2 = by_values(q0, q1, q2)
                 value_z[qx, 0], value_z[qx, 1] = n0 + up_z(n2), n1
                 n0, n1, n2 = by_slopes(q0, q1, q2)
@@ -261,8 +283,7 @@
     blank = jnp.zeros((8, 128), jnp.float32)
     lax.fori_loop(0, 9, force_row, (blank,) * 12, unroll=UNROLL[0])
 
-    def mass_row(d, y, source, target, carry, rho, wanted):
-        wall = inside_y(y)
+    def mass_row(d, y, source, target, carry, rhos, wall, wanted):
         locals_y = {}
         for xc in range(2):
             for zc in range(2):
@@ -285,7 +306,7 @@
             joined = {}
             for j in range(3):
                 v, m = lines[j, 0], lines[j, 1]
-                n0, n1, n2 = (rho * n for n in element_op(v, m, down_x(v)))
+                n0, n1, n2 = weighted_op(v, m, down_x(v), rhos)
                 joined[j, 0], joined[j, 1] = n0 + up_x(n2), n1
             for xc in range(2):
                 out[k, xc, 0] = joined[0, xc] + up_z(joined[2, xc])
@@ -301,10 +322,12 @@
 
     def mass(source, target, start, stop, last, unroll):
         def step(y, carry, wanted=(0, 1, 2)):
-            rho = point(y, 13, 1) * (1.0 / 3375.0)
+            rho = point(y, 13, 1)
+            rhos = [rho * (k / 3375.0) for k in (1.0, 0.75, 1.25, 8.0)]
+            wall = walls(y)
             kept = ()
             for d in range(3):
-                kept += mass_row(d, y, source, target, carry[4 * d : 4 * d + 4], rho, wanted)
+                kept += mass_row(d, y, source, target, carry[4 * d : 4 * d + 4], rhos, wall, wanted)
             return kept
 
         carry = step(start, (blank,) * 12, (2,))
@@ -457,7 +480,7 @@
         pair,
         cross,
         far,
-        scratch=((9 * 128, 128), grid, grid, grid, (288, 128)),
+        scratch=((9 * 128, 128), (9 * 216, 128), grid, grid, grid, (288, 128)),
     )
     (sums,) = call(relay, (parts_shape(SECOND),), exchange(sums, FIRST))
     acceleration, residual = call(

time: 81.5 us -> 81.9 us (level)
  no operation moved by 1% of the time
where the time goes in v7:
time: 81.9 us; the launch traced here: 81.6 us
  blocking collectives  64 us (78%)
  starting transfers between devices  11.3 us (14%)
  Pallas kernels  5.58 us (7%)
    all_to_all x2, blocking collectives, exchange(): parts = lax.all_to_all(value.reshape(-1, 1, 128), axes, 0, 0)  34.9 us
    all_to_all x1, blocking collectives, on_device(): lax.all_to_all(slots, 'gy', 0, 0)  20.7 us
    ppermute x2, starting transfers between devices, swapped(): return lax.ppermute(value, axes, links + [(b, a) for a, b in links])  8.18 us
    all_gather x1, blocking collectives, on_device(): lax.all_gather(message, GZ[1])  6.39 us
    pallas_call x5, Pallas kernels, call(): pl.pallas_call(body, out_shape=tuple((place(o) for o in outs)), in_specs=...  4.28 us
    ppermute x1, starting transfers between devices, moved(): return lax.ppermute(value, axes, pairs)  3.1 us
    all_gather x1, blocking collectives, on_device(): pair = lax.all_gather(own, GX[2])  2.02 us
  transfers between devices with their start and end apart: 3, of which 0 were waited for; matrix products, arithmetic and copies ran while one was open for 0% of the time, Pallas kernels for 0%

profile of v7, /device:TPU:1, one launch (start us, length us, event | category | flops | bytes accessed | tf_op | source)
XLA Modules:
  0.0 81.6 jit_solution(979518446591954436)
XLA Ops:
  0.6 1.3 %shard_map.59 = (f32[4,32,128]{2,1,0:T(8,128)S(1)}, f32[16,128]{1,0:T(8,128)S(1)}) custom-call(f32[6,12,192]{2,1,0:T(8,128)} %energy.1, f32[2,4,64]{2,1,0:T(4,128)} %density.1, s32[2,4,64]{2,1,0:T(4,128)} %region.1, f32[3]{0:T(128)} %gamma.1), custom_call_target="tpu_custom_call" | custom-call | tf_op jit(solution)/shard_map/pallas_call | solution.py:452
  1.9 0.7 collective-permute-start
  2.6 6.4 %all-gather = f32[32,128]{1,0:T(8,128)S(1)} all-gather(f32[16,128]{1,0:T(8,128)S(1)} %get-tuple-element.13), channel_id=2, replica_groups=mesh['gx0'=4,'gx1'=4,'gx2'=2,'gy'=3,'gz0'=4,'gz1'=2] {'gz1'}, dimensions={0}, use_global_device_ids=true | all-gather | bytes 24576 | tf_op jit(solution)/shard_map/all_gather | solution.py:463
  9.0 0.0 collective-permute-done.odd
  9.0 20.7 %all_to_all.15.slots = f32[3,96,128]{2,1,0:T(8,128)S(1)} all-to-all(f32[3,96,128]{2,1,0:T(8,128)S(1)} %get-tuple-element.15), channel_id=1, replica_groups=mesh['gx0'=4,'gx1'=4,'gx2'=2,'gy'=3,'gz0'=4,'gz1'=2] {'gy'}, dimensions={0} | all-to-all | bytes 294912 | tf_op jit(solution)/shard_map/all_to_all | solution.py:470
  29.7 7.5 %collective-permute-start.1 = (f32[9,32,128]{2,1,0:T(8,128)S(1)}, f32[9,32,128]{2,1,0:T(8,128)S(1)}, u32[]{:S(2)}, u32[]{:S(2)}) collective-permute-start(f32[9,32,128]{2,1,0:T(8,128)S(1)} %get-tuple-element.16.own), channel_id=1, source_target_pairs={{24,48},{72,96},{120,144},{168,192},{216,240},{264,288},{312,336},... | collective-permute-start | bytes 442376 | tf_op jit(solution)/shard_map/ppermute | solution.py:415
  37.2 3.1 %collective-permute-start.2 = (f32[9,16,128]{2,1,0:T(8,128)S(1)}, f32[9,16,128]{2,1,0:T(8,128)S(1)}, u32[]{:S(2)}, u32[]{:S(2)}) collective-permute-start(f32[9,16,128]{2,1,0:T(8,128)S(1)} %get-tuple-element.17), channel_id=1, source_target_pairs={{0,48},{24,72},{48,96},{72,120},{96,144},{120,168},{144,192},{168,... | collective-permute-start | bytes 221192 | tf_op jit(solution)/shard_map/ppermute | solution.py:410
  40.3 2.0 %all-gather.1 = f32[18,32,128]{2,1,0:T(8,128)S(1)} all-gather(f32[9,32,128]{2,1,0:T(8,128)S(1)} %get-tuple-element.16.own), channel_id=3, replica_groups=mesh['gx0'=4,'gx1'=4,'gx2'=2,'gy'=3,'gz0'=4,'gz1'=2] {'gx2'}, dimensions={0}, use_global_device_ids=true | all-gather | bytes 442368 | tf_op jit(solution)/shard_map/all_gather | solution.py:474
  42.4 0.0 collective-permute-done.2.far
  42.4 0.0 collective-permute-done.1.cross
  42.4 3.4 %shard_map.62 = (f32[288,128]{1,0:T(8,128)S(1)}, f32[64,128]{1,0:T(8,128)S(1)}) custom-call(f32[9,32,128]{2,1,0:T(8,128)S(1)} %get-tuple-element.16.own, f32[2,9,32,128]{3,2,1,0:T(8,128)S(1)} %bitcast.8, f32[9,32,128]{2,1,0:T(8,128)S(1)} %collective-permute-done.1.cross, f32[9,16,128]{2,1,0:T(8,128)S(1)} %collective-permute-done.2.far), custom_call_target="tpu_custom_call" | custom-call | tf_op jit(solution)/shard_map/pallas_call | solution.py:425
  45.8 22.2 %all_to_all.16 = f32[64,1,128]{2,1,0:T(1,128)S(1)} all-to-all(f32[64,1,128]{2,1,0:T(1,128)S(1)} %bitcast.11), channel_id=1, replica_groups=mesh['gx0'=4,'gx1'=4,'gx2'=2,'gy'=3,'gz0'=4,'gz1'=2] {'gx0','gz0','gz1',..., dimensions={0} | all-to-all | bytes 65536 | tf_op jit(solution)/shard_map/all_to_all | solution.py:447
  68.0 12.8 %all_to_all.17.parts = f32[12,1,128]{2,1,0:T(1,128)S(1)} all-to-all(f32[12,1,128]{2,1,0:T(1,128)S(1)} %shard_map.63), channel_id=1, replica_groups=mesh['gx0'=4,'gx1'=4,'gx2'=2,'gy'=3,'gz0'=4,'gz1'=2] {'gy','gx1'}, dimensions={0} | all-to-all | bytes 12288 | tf_op jit(solution)/shard_map/all_to_all | solution.py:447
  80.7 0.8 shard_map.64
  (3 shorter events, 0.1 us)
Async XLA Ops:
  1.9 7.1 %collective-permute-start = (f32[16,128]{1,0:T(8,128)S(1)}, f32[16,128]{1,0:T(8,128)S(1)}, u32[]{:S(2)}, u32[]{:S(2)}) collective-permute-start(f32[16,128]{1,0:T(8,128)S(1)} %get-tuple-element.13), channel_id=1, source_target_pairs={{1,2},{3,4},{5,6},{2,1},{4,3},{6,5},{9,10},{11,12},{13,14},{10,9},... | collective-permute-start | bytes 24584 | tf_op jit(solution)/shard_map/ppermute | solution.py:415
  29.7 12.7 %collective-permute-start.1 = (f32[9,32,128]{2,1,0:T(8,128)S(1)}, f32[9,32,128]{2,1,0:T(8,128)S(1)}, u32[]{:S(2)}, u32[]{:S(2)}) collective-permute-start(f32[9,32,128]{2,1,0:T(8,128)S(1)} %get-tuple-element.16.own), channel_id=1, source_target_pairs={{24,48},{72,96},{120,144},{168,192},{216,240},{264,288},{312,336},... | collective-permute-start | bytes 442376 | tf_op jit(solution)/shard_map/ppermute | solution.py:415
  37.2 5.1 %collective-permute-start.2 = (f32[9,16,128]{2,1,0:T(8,128)S(1)}, f32[9,16,128]{2,1,0:T(8,128)S(1)}, u32[]{:S(2)}, u32[]{:S(2)}) collective-permute-start(f32[9,16,128]{2,1,0:T(8,128)S(1)} %get-tuple-element.17), channel_id=1, source_target_pairs={{0,48},{24,72},{48,96},{72,120},{96,144},{120,168},{144,192},{168,... | collective-permute-start | bytes 221192 | tf_op jit(solution)/shard_map/ppermute | solution.py:410

commit v8 on v6

--- a/solution.py
+++ b/solution.py
@@ -350,36 +350,82 @@
     )
 
 
-def total_of(parts):
+def two_sum(a, b):
+    total = a + b
+    part = total - a
+    return total, (a - (total - part)) + (b - part)
+
+
+def two_product(a, b):
+    total = a * b
+    a_high, b_high = a * 4097.0, b * 4097.0
+    a_high, b_high = a_high - (a_high - a), b_high - (b_high - b)
+    a_low, b_low = a - a_high, b - b_high
+    rest = ((a_high * b_high - total) + a_high * b_low + a_low * b_high) + a_low * b_low
+    return total, rest
+
+
+def added(a, b):
+    total, rest = two_sum(a[0], b[0])
+    return total, rest + (a[1] + b[1])
+
+
+def determinant(a, b, c):
+    p, p_rest = two_product(a[0], b[0])
+    q, q_rest = two_product(c[0], c[0])
+    p_rest = p_rest + (a[0] * b[1] + a[1] * b[0])
+    q_rest = q_rest + 2.0 * (c[0] * c[1])
+    total, rest = two_sum(p, -q)
+    return total + (rest + (p_rest - q_rest))
+
+
+def total_of(parts, corrected):
     if parts.ndim == 2:
-        return jnp.sum(parts[...], axis=0, keepdims=True)
-    rows = [parts[k] for k in range(parts.shape[0])]
+        count = parts.shape[0]
+        rows = [parts[k : k + 8, :] for k in range(0, count, 8)]
+    else:
+        rows = [parts[k] for k in range(parts.shape[0])]
+    rows = [(row, pltpu.roll(row, 64, 1) if corrected else jnp.zeros_like(row)) for row in rows]
     while len(rows) > 1:
-        rows = [sum(rows[k : k + 2][1:], rows[k]) for k in range(0, len(rows), 2)]
-    return rows[0]
+        ahead = [added(rows[k], rows[k + 1]) for k in range(0, len(rows) - 1, 2)]
+        rows = ahead + rows[len(rows) - len(rows) % 2 :]
+    total = rows[0]
+    while total[0].shape[0] > 1:
+        half = total[0].shape[0] // 2
+        total = added(
+            (total[0][:half], total[1][:half]), (total[0][half:], total[1][half:])
+        )
+    return total
 
 
 def relay(parts, sums_out):
-    sums = total_of(parts)
+    value, rest = total_of(parts, False)
+    lane = iota((1, 128), 1)
+    sums = jnp.where(lane < 64, value, pltpu.roll(rest, 64, 1))
     if sums_out.ndim == 3:
         sums = sums[None]
     sums_out[...] = jnp.broadcast_to(sums, sums_out.shape)
 
 
 def combine(fields, parts, acceleration_out, residual_out):
-    sums = total_of(parts)
+    sums = total_of(parts, True)
+    c = [tuple(pltpu.roll(part, (128 - k) % 128, 1) if k else part for part in sums) for k in range(4)]
+    upper, lower = determinant(c[0], c[2], c[1]), determinant(c[1], c[3], c[2])
+    lane = iota((1, 128), 1)
+    used = (lane < 12) & (lane % 4 == 0)
+    c0, c1 = (jnp.where(used, c[k][0], 1.0) for k in range(2))
+    lower = jnp.where(used, lower, 1.0)
+    alphas = c0 / c1
+    betas = upper / (c1 * c1)
+    alphas_2 = (c1 * upper) / (c0 * lower)
     for d in range(3):
-        c0, c1, c2, c3 = (sums[:, 4 * d + k : 4 * d + k + 1] for k in range(4))
-        alpha = c0 / c1
-        norm = c0 - 2.0 * alpha * c1 + alpha * alpha * c2
-        beta = norm / c0
-        grow = 1.0 + beta
-        alpha_2 = norm / (grow * grow * c1 - 2.0 * alpha * grow * c2 + alpha * alpha * c3)
+        alpha, beta, alpha_2 = (x[:, 4 * d : 4 * d + 1] for x in (alphas, betas, alphas_2))
         v0, v1, v2 = (fields[96 * f + 32 * d : 96 * f + 32 * d + 32, :] for f in range(3))
-        direction = (v0 - alpha * v1) + beta * v0
-        image = grow * v1 - alpha * v2
+        first = v0 - alpha * v1
+        direction = first + beta * v0
+        image = (v1 + beta * v1) - alpha * v2
         acceleration_out[32 * d : 32 * d + 32, :] = alpha * v0 + alpha_2 * direction
-        residual_out[32 * d : 32 * d + 32, :] = (v0 - alpha * v1) - alpha_2 * image
+        residual_out[32 * d : 32 * d + 32, :] = first - alpha_2 * image
 
 
 def moved(value, axes, by):

time: 81.5 us -> 81.7 us (level)
  no operation moved by 1% of the time
where the time goes in v8:
time: 81.7 us; the launch traced here: 81.3 us
  blocking collectives  64 us (78%)
  starting transfers between devices  11.3 us (14%)
  Pallas kernels  5.38 us (7%)
    all_to_all x2, blocking collectives, exchange(): parts = lax.all_to_all(value.reshape(-1, 1, 128), axes, 0, 0)  34.9 us
    all_to_all x1, blocking collectives, on_device(): lax.all_to_all(slots, 'gy', 0, 0)  20.7 us
    ppermute x2, starting transfers between devices, swapped(): return lax.ppermute(value, axes, links + [(b, a) for a, b in links])  8.18 us
    all_gather x1, blocking collectives, on_device(): lax.all_gather(message, GZ[1])  6.39 us
    pallas_call x5, Pallas kernels, call(): pl.pallas_call(body, out_shape=tuple((place(o) for o in outs)), in_specs=...  4.08 us
    ppermute x1, starting transfers between devices, moved(): return lax.ppermute(value, axes, pairs)  3.1 us
    all_gather x1, blocking collectives, on_device(): pair = lax.all_gather(own, GX[2])  2.02 us
  transfers between devices with their start and end apart: 3, of which 0 were waited for; matrix products, arithmetic and copies ran while one was open for 0% of the time, Pallas kernels for 0%

profile of v8, /device:TPU:1, one launch (start us, length us, event | category | flops | bytes accessed | tf_op | source)
XLA Modules:
  0.0 81.3 jit_solution(10725159565852453567)
XLA Ops:
  0.6 1.3 %shard_map.59 = (f32[4,32,128]{2,1,0:T(8,128)S(1)}, f32[16,128]{1,0:T(8,128)S(1)}) custom-call(f32[6,12,192]{2,1,0:T(8,128)} %energy.1, f32[2,4,64]{2,1,0:T(4,128)} %density.1, s32[2,4,64]{2,1,0:T(4,128)} %region.1, f32[3]{0:T(128)} %gamma.1), custom_call_target="tpu_custom_call" | custom-call | tf_op jit(solution)/shard_map/pallas_call | solution.py:475
  1.9 0.7 collective-permute-start
  2.6 6.4 %all-gather = f32[32,128]{1,0:T(8,128)S(1)} all-gather(f32[16,128]{1,0:T(8,128)S(1)} %get-tuple-element.13), channel_id=2, replica_groups=mesh['gx0'=4,'gx1'=4,'gx2'=2,'gy'=3,'gz0'=4,'gz1'=2] {'gz1'}, dimensions={0}, use_global_device_ids=true | all-gather | bytes 24576 | tf_op jit(solution)/shard_map/all_gather | solution.py:486
  9.0 0.0 collective-permute-done.odd
  9.0 20.7 %all_to_all.15.slots = f32[3,96,128]{2,1,0:T(8,128)S(1)} all-to-all(f32[3,96,128]{2,1,0:T(8,128)S(1)} %get-tuple-element.15), channel_id=1, replica_groups=mesh['gx0'=4,'gx1'=4,'gx2'=2,'gy'=3,'gz0'=4,'gz1'=2] {'gy'}, dimensions={0} | all-to-all | bytes 294912 | tf_op jit(solution)/shard_map/all_to_all | solution.py:493
  29.7 7.5 %collective-permute-start.1 = (f32[9,32,128]{2,1,0:T(8,128)S(1)}, f32[9,32,128]{2,1,0:T(8,128)S(1)}, u32[]{:S(2)}, u32[]{:S(2)}) collective-permute-start(f32[9,32,128]{2,1,0:T(8,128)S(1)} %get-tuple-element.16.own), channel_id=1, source_target_pairs={{24,48},{72,96},{120,144},{168,192},{216,240},{264,288},{312,336},... | collective-permute-start | bytes 442376 | tf_op jit(solution)/shard_map/ppermute | solution.py:438
  37.2 3.1 %collective-permute-start.2 = (f32[9,16,128]{2,1,0:T(8,128)S(1)}, f32[9,16,128]{2,1,0:T(8,128)S(1)}, u32[]{:S(2)}, u32[]{:S(2)}) collective-permute-start(f32[9,16,128]{2,1,0:T(8,128)S(1)} %get-tuple-element.17), channel_id=1, source_target_pairs={{0,48},{24,72},{48,96},{72,120},{96,144},{120,168},{144,192},{168,... | collective-permute-start | bytes 221192 | tf_op jit(solution)/shard_map/ppermute | solution.py:433
  40.3 2.0 %all-gather.1 = f32[18,32,128]{2,1,0:T(8,128)S(1)} all-gather(f32[9,32,128]{2,1,0:T(8,128)S(1)} %get-tuple-element.16.own), channel_id=3, replica_groups=mesh['gx0'=4,'gx1'=4,'gx2'=2,'gy'=3,'gz0'=4,'gz1'=2] {'gx2'}, dimensions={0}, use_global_device_ids=true | all-gather | bytes 442368 | tf_op jit(solution)/shard_map/all_gather | solution.py:497
  42.4 0.0 collective-permute-done.2.far
  42.4 0.0 collective-permute-done.1.cross
  42.4 3.0 %shard_map.62 = (f32[288,128]{1,0:T(8,128)S(1)}, f32[64,128]{1,0:T(8,128)S(1)}) custom-call(f32[9,32,128]{2,1,0:T(8,128)S(1)} %get-tuple-element.16.own, f32[2,9,32,128]{3,2,1,0:T(8,128)S(1)} %bitcast.8, f32[9,32,128]{2,1,0:T(8,128)S(1)} %collective-permute-done.1.cross, f32[9,16,128]{2,1,0:T(8,128)S(1)} %collective-permute-done.2.far), custom_call_target="tpu_custom_call" | custom-call | tf_op jit(solution)/shard_map/pallas_call | solution.py:448
  45.4 22.2 %all_to_all.16 = f32[64,1,128]{2,1,0:T(1,128)S(1)} all-to-all(f32[64,1,128]{2,1,0:T(1,128)S(1)} %bitcast.11), channel_id=1, replica_groups=mesh['gx0'=4,'gx1'=4,'gx2'=2,'gy'=3,'gz0'=4,'gz1'=2] {'gx0','gz0','gz1',..., dimensions={0} | all-to-all | bytes 65536 | tf_op jit(solution)/shard_map/all_to_all | solution.py:470
  67.6 0.1 shard_map.63
  67.7 12.8 %all_to_all.17.parts = f32[12,1,128]{2,1,0:T(1,128)S(1)} all-to-all(f32[12,1,128]{2,1,0:T(1,128)S(1)} %shard_map.63), channel_id=1, replica_groups=mesh['gx0'=4,'gx1'=4,'gx2'=2,'gy'=3,'gz0'=4,'gz1'=2] {'gy','gx1'}, dimensions={0} | all-to-all | bytes 12288 | tf_op jit(solution)/shard_map/all_to_all | solution.py:470
  80.4 0.9 %shard_map.64 = (f32[96,128]{1,0:T(8,128)}, f32[96,128]{1,0:T(8,128)}) custom-call(f32[288,128]{1,0:T(8,128)S(1)} %get-tuple-element.18.fields, f32[12,1,128]{2,1,0:T(1,128)S(1)} %all_to_all.17.parts), custom_call_target="tpu_custom_call" | custom-call | tf_op jit(solution)/shard_map/pallas_call | solution.py:448
  (2 shorter events, 0.0 us)
Async XLA Ops:
  1.9 7.1 %collective-permute-start = (f32[16,128]{1,0:T(8,128)S(1)}, f32[16,128]{1,0:T(8,128)S(1)}, u32[]{:S(2)}, u32[]{:S(2)}) collective-permute-start(f32[16,128]{1,0:T(8,128)S(1)} %get-tuple-element.13), channel_id=1, source_target_pairs={{1,2},{3,4},{5,6},{2,1},{4,3},{6,5},{9,10},{11,12},{13,14},{10,9},... | collective-permute-start | bytes 24584 | tf_op jit(solution)/shard_map/ppermute | solution.py:438
  29.7 12.7 %collective-permute-start.1 = (f32[9,32,128]{2,1,0:T(8,128)S(1)}, f32[9,32,128]{2,1,0:T(8,128)S(1)}, u32[]{:S(2)}, u32[]{:S(2)}) collective-permute-start(f32[9,32,128]{2,1,0:T(8,128)S(1)} %get-tuple-element.16.own), channel_id=1, source_target_pairs={{24,48},{72,96},{120,144},{168,192},{216,240},{264,288},{312,336},... | collective-permute-start | bytes 442376 | tf_op jit(solution)/shard_map/ppermute | solution.py:438
  37.2 5.1 %collective-permute-start.2 = (f32[9,16,128]{2,1,0:T(8,128)S(1)}, f32[9,16,128]{2,1,0:T(8,128)S(1)}, u32[]{:S(2)}, u32[]{:S(2)}) collective-permute-start(f32[9,16,128]{2,1,0:T(8,128)S(1)} %get-tuple-element.17), channel_id=1, source_target_pairs={{0,48},{24,72},{48,96},{72,120},{96,144},{120,168},{144,192},{168,... | collective-permute-start | bytes 221192 | tf_op jit(solution)/shard_map/ppermute | solution.py:433

commit v9 on v8

--- a/solution.py
+++ b/solution.py
@@ -454,7 +454,7 @@
     )(*kept)
 
 
-FIRST, SECOND = ("gx0", *GZ, "gx2"), ("gy", "gx1")
+FIRST, SECOND = ("gy", "gx1", "gx2"), ("gx0", *GZ)
 
 
 def members(axes):

time: 81.7 us -> 81.4 us (level)
  no operation moved by 1% of the time
where the time goes in v9:
time: 81.4 us; the launch traced here: 81 us
  blocking collectives  63.7 us (78%)
  starting transfers between devices  11.3 us (14%)
  Pallas kernels  5.37 us (7%)
    all_to_all x2, blocking collectives, exchange(): parts = lax.all_to_all(value.reshape(-1, 1, 128), axes, 0, 0)  34.6 us
    all_to_all x1, blocking collectives, on_device(): lax.all_to_all(slots, 'gy', 0, 0)  20.7 us
    ppermute x2, starting transfers between devices, swapped(): return lax.ppermute(value, axes, links + [(b, a) for a, b in links])  8.18 us
    all_gather x1, blocking collectives, on_device(): lax.all_gather(message, GZ[1])  6.39 us
    pallas_call x5, Pallas kernels, call(): pl.pallas_call(body, out_shape=tuple((place(o) for o in outs)), in_specs=...  4.08 us
    ppermute x1, starting transfers between devices, moved(): return lax.ppermute(value, axes, pairs)  3.1 us
    all_gather x1, blocking collectives, on_device(): pair = lax.all_gather(own, GX[2])  2.02 us
  transfers between devices with their start and end apart: 3, of which 0 were waited for; matrix products, arithmetic and copies ran while one was open for 0% of the time, Pallas kernels for 0%

profile of v9, /device:TPU:1, one launch (start us, length us, event | category | flops | bytes accessed | tf_op | source)
XLA Modules:
  0.0 81.0 jit_solution(6468445771834554563)
XLA Ops:
  0.6 1.3 %shard_map.59 = (f32[4,32,128]{2,1,0:T(8,128)S(1)}, f32[16,128]{1,0:T(8,128)S(1)}) custom-call(f32[6,12,192]{2,1,0:T(8,128)} %energy.1, f32[2,4,64]{2,1,0:T(4,128)} %density.1, s32[2,4,64]{2,1,0:T(4,128)} %region.1, f32[3]{0:T(128)} %gamma.1), custom_call_target="tpu_custom_call" | custom-call | tf_op jit(solution)/shard_map/pallas_call | solution.py:475
  1.9 0.7 collective-permute-start
  2.6 6.4 %all-gather = f32[32,128]{1,0:T(8,128)S(1)} all-gather(f32[16,128]{1,0:T(8,128)S(1)} %get-tuple-element.13), channel_id=2, replica_groups=mesh['gx0'=4,'gx1'=4,'gx2'=2,'gy'=3,'gz0'=4,'gz1'=2] {'gz1'}, dimensions={0}, use_global_device_ids=true | all-gather | bytes 24576 | tf_op jit(solution)/shard_map/all_gather | solution.py:486
  9.0 0.0 collective-permute-done.odd
  9.0 20.7 %all_to_all.15.slots = f32[3,96,128]{2,1,0:T(8,128)S(1)} all-to-all(f32[3,96,128]{2,1,0:T(8,128)S(1)} %get-tuple-element.15), channel_id=1, replica_groups=mesh['gx0'=4,'gx1'=4,'gx2'=2,'gy'=3,'gz0'=4,'gz1'=2] {'gy'}, dimensions={0} | all-to-all | bytes 294912 | tf_op jit(solution)/shard_map/all_to_all | solution.py:493
  29.7 7.5 %collective-permute-start.1 = (f32[9,32,128]{2,1,0:T(8,128)S(1)}, f32[9,32,128]{2,1,0:T(8,128)S(1)}, u32[]{:S(2)}, u32[]{:S(2)}) collective-permute-start(f32[9,32,128]{2,1,0:T(8,128)S(1)} %get-tuple-element.16.own), channel_id=1, source_target_pairs={{24,48},{72,96},{120,144},{168,192},{216,240},{264,288},{312,336},... | collective-permute-start | bytes 442376 | tf_op jit(solution)/shard_map/ppermute | solution.py:438
  37.2 3.1 %collective-permute-start.2 = (f32[9,16,128]{2,1,0:T(8,128)S(1)}, f32[9,16,128]{2,1,0:T(8,128)S(1)}, u32[]{:S(2)}, u32[]{:S(2)}) collective-permute-start(f32[9,16,128]{2,1,0:T(8,128)S(1)} %get-tuple-element.17), channel_id=1, source_target_pairs={{0,48},{24,72},{48,96},{72,120},{96,144},{120,168},{144,192},{168,... | collective-permute-start | bytes 221192 | tf_op jit(solution)/shard_map/ppermute | solution.py:433
  40.3 2.0 %all-gather.1 = f32[18,32,128]{2,1,0:T(8,128)S(1)} all-gather(f32[9,32,128]{2,1,0:T(8,128)S(1)} %get-tuple-element.16.own), channel_id=3, replica_groups=mesh['gx0'=4,'gx1'=4,'gx2'=2,'gy'=3,'gz0'=4,'gz1'=2] {'gx2'}, dimensions={0}, use_global_device_ids=true | all-gather | bytes 442368 | tf_op jit(solution)/shard_map/all_gather | solution.py:497
  42.4 0.0 collective-permute-done.2.far
  42.4 0.0 collective-permute-done.1.cross
  42.4 3.0 %shard_map.62 = (f32[288,128]{1,0:T(8,128)S(1)}, f32[24,128]{1,0:T(8,128)S(1)}) custom-call(f32[9,32,128]{2,1,0:T(8,128)S(1)} %get-tuple-element.16.own, f32[2,9,32,128]{3,2,1,0:T(8,128)S(1)} %bitcast.12, f32[9,32,128]{2,1,0:T(8,128)S(1)} %collective-permute-done.1.cross, f32[9,16,128]{2,1,0:T(8,128)S(1)} %collective-permute-done.2.far), custom_call_target="tpu_custom_call" | custom-call | tf_op jit(solution)/shard_map/pallas_call | solution.py:448
  45.4 15.4 %all_to_all.16 = f32[24,1,128]{2,1,0:T(1,128)S(1)} all-to-all(f32[24,1,128]{2,1,0:T(1,128)S(1)} %bitcast.17), channel_id=1, replica_groups=mesh['gx0'=4,'gx1'=4,'gx2'=2,'gy'=3,'gz0'=4,'gz1'=2] {'gy','gx1','gx2'}, dimensions={0} | all-to-all | bytes 24576 | tf_op jit(solution)/shard_map/all_to_all | solution.py:470
  60.8 0.1 shard_map.63
  60.9 19.2 %all_to_all.17 = f32[32,1,128]{2,1,0:T(1,128)S(1)} all-to-all(f32[32,1,128]{2,1,0:T(1,128)S(1)} %bitcast.14), channel_id=1, replica_groups=mesh['gx0'=4,'gx1'=4,'gx2'=2,'gy'=3,'gz0'=4,'gz1'=2] {'gx0','gz0','gz1'}, dimensions={0} | all-to-all | bytes 32768 | tf_op jit(solution)/shard_map/all_to_all | solution.py:470
  80.1 0.9 %shard_map.64 = (f32[96,128]{1,0:T(8,128)}, f32[96,128]{1,0:T(8,128)}) custom-call(f32[288,128]{1,0:T(8,128)S(1)} %get-tuple-element.18.fields, f32[32,128]{1,0:T(8,128)S(1)} %bitcast.13), custom_call_target="tpu_custom_call" | custom-call | tf_op jit(solution)/shard_map/pallas_call | solution.py:448
  (2 shorter events, 0.0 us)
Async XLA Ops:
  1.9 7.1 %collective-permute-start = (f32[16,128]{1,0:T(8,128)S(1)}, f32[16,128]{1,0:T(8,128)S(1)}, u32[]{:S(2)}, u32[]{:S(2)}) collective-permute-start(f32[16,128]{1,0:T(8,128)S(1)} %get-tuple-element.13), channel_id=1, source_target_pairs={{1,2},{3,4},{5,6},{2,1},{4,3},{6,5},{9,10},{11,12},{13,14},{10,9},... | collective-permute-start | bytes 24584 | tf_op jit(solution)/shard_map/ppermute | solution.py:438
  29.7 12.7 %collective-permute-start.1 = (f32[9,32,128]{2,1,0:T(8,128)S(1)}, f32[9,32,128]{2,1,0:T(8,128)S(1)}, u32[]{:S(2)}, u32[]{:S(2)}) collective-permute-start(f32[9,32,128]{2,1,0:T(8,128)S(1)} %get-tuple-element.16.own), channel_id=1, source_target_pairs={{24,48},{72,96},{120,144},{168,192},{216,240},{264,288},{312,336},... | collective-permute-start | bytes 442376 | tf_op jit(solution)/shard_map/ppermute | solution.py:438
  37.2 5.1 %collective-permute-start.2 = (f32[9,16,128]{2,1,0:T(8,128)S(1)}, f32[9,16,128]{2,1,0:T(8,128)S(1)}, u32[]{:S(2)}, u32[]{:S(2)}) collective-permute-start(f32[9,16,128]{2,1,0:T(8,128)S(1)} %get-tuple-element.17), channel_id=1, source_target_pairs={{0,48},{24,72},{48,96},{72,120},{96,144},{120,168},{144,192},{168,... | collective-permute-start | bytes 221192 | tf_op jit(solution)/shard_map/ppermute | solution.py:433

commit v10 on v8

--- a/solution.py
+++ b/solution.py
@@ -13,7 +13,7 @@
 PAIRS = 14
 ROOT = math.sqrt(0.15)
 EDGE_W, MID_W = 5.0 / 18.0, 8.0 / 18.0
-UNROLL = (3, 5, 3)
+UNROLL = (3, 1, 3)
 GX = ("gx0", "gx1", "gx2")
 GZ = ("gz0", "gz1")
 

time: 81.7 us -> 82.3 us (level)
  no operation moved by 1% of the time
where the time goes in v10:
time: 82.3 us; the launch traced here: 82 us
  blocking collectives  64 us (78%)
  starting transfers between devices  11.3 us (14%)
  Pallas kernels  6.03 us (7%)
    all_to_all x2, blocking collectives, exchange(): parts = lax.all_to_all(value.reshape(-1, 1, 128), axes, 0, 0)  34.9 us
    all_to_all x1, blocking collectives, on_device(): lax.all_to_all(slots, 'gy', 0, 0)  20.7 us
    ppermute x2, starting transfers between devices, swapped(): return lax.ppermute(value, axes, links + [(b, a) for a, b in links])  8.18 us
    all_gather x1, blocking collectives, on_device(): lax.all_gather(message, GZ[1])  6.39 us
    pallas_call x5, Pallas kernels, call(): pl.pallas_call(body, out_shape=tuple((place(o) for o in outs)), in_specs=...  4.73 us
    ppermute x1, starting transfers between devices, moved(): return lax.ppermute(value, axes, pairs)  3.1 us
    all_gather x1, blocking collectives, on_device(): pair = lax.all_gather(own, GX[2])  2.02 us
  transfers between devices with their start and end apart: 3, of which 0 were waited for; matrix products, arithmetic and copies ran while one was open for 0% of the time, Pallas kernels for 0%

profile of v10, /device:TPU:1, one launch (start us, length us, event | category | flops | bytes accessed | tf_op | source)
XLA Modules:
  0.0 82.0 jit_solution(17471261263039598684)
XLA Ops:
  0.6 1.3 %shard_map.59 = (f32[4,32,128]{2,1,0:T(8,128)S(1)}, f32[16,128]{1,0:T(8,128)S(1)}) custom-call(f32[6,12,192]{2,1,0:T(8,128)} %energy.1, f32[2,4,64]{2,1,0:T(4,128)} %density.1, s32[2,4,64]{2,1,0:T(4,128)} %region.1, f32[3]{0:T(128)} %gamma.1), custom_call_target="tpu_custom_call" | custom-call | tf_op jit(solution)/shard_map/pallas_call | solution.py:475
  1.9 0.7 collective-permute-start
  2.6 6.4 %all-gather = f32[32,128]{1,0:T(8,128)S(1)} all-gather(f32[16,128]{1,0:T(8,128)S(1)} %get-tuple-element.13), channel_id=2, replica_groups=mesh['gx0'=4,'gx1'=4,'gx2'=2,'gy'=3,'gz0'=4,'gz1'=2] {'gz1'}, dimensions={0}, use_global_device_ids=true | all-gather | bytes 24576 | tf_op jit(solution)/shard_map/all_gather | solution.py:486
  9.0 0.0 collective-permute-done.odd
  9.0 20.7 %all_to_all.15.slots = f32[3,96,128]{2,1,0:T(8,128)S(1)} all-to-all(f32[3,96,128]{2,1,0:T(8,128)S(1)} %get-tuple-element.15), channel_id=1, replica_groups=mesh['gx0'=4,'gx1'=4,'gx2'=2,'gy'=3,'gz0'=4,'gz1'=2] {'gy'}, dimensions={0} | all-to-all | bytes 294912 | tf_op jit(solution)/shard_map/all_to_all | solution.py:493
  29.7 7.5 %collective-permute-start.1 = (f32[9,32,128]{2,1,0:T(8,128)S(1)}, f32[9,32,128]{2,1,0:T(8,128)S(1)}, u32[]{:S(2)}, u32[]{:S(2)}) collective-permute-start(f32[9,32,128]{2,1,0:T(8,128)S(1)} %get-tuple-element.16.own), channel_id=1, source_target_pairs={{24,48},{72,96},{120,144},{168,192},{216,240},{264,288},{312,336},... | collective-permute-start | bytes 442376 | tf_op jit(solution)/shard_map/ppermute | solution.py:438
  37.2 3.1 %collective-permute-start.2 = (f32[9,16,128]{2,1,0:T(8,128)S(1)}, f32[9,16,128]{2,1,0:T(8,128)S(1)}, u32[]{:S(2)}, u32[]{:S(2)}) collective-permute-start(f32[9,16,128]{2,1,0:T(8,128)S(1)} %get-tuple-element.17), channel_id=1, source_target_pairs={{0,48},{24,72},{48,96},{72,120},{96,144},{120,168},{144,192},{168,... | collective-permute-start | bytes 221192 | tf_op jit(solution)/shard_map/ppermute | solution.py:433
  40.3 2.0 %all-gather.1 = f32[18,32,128]{2,1,0:T(8,128)S(1)} all-gather(f32[9,32,128]{2,1,0:T(8,128)S(1)} %get-tuple-element.16.own), channel_id=3, replica_groups=mesh['gx0'=4,'gx1'=4,'gx2'=2,'gy'=3,'gz0'=4,'gz1'=2] {'gx2'}, dimensions={0}, use_global_device_ids=true | all-gather | bytes 442368 | tf_op jit(solution)/shard_map/all_gather | solution.py:497
  42.4 0.0 collective-permute-done.2.far
  42.4 0.0 collective-permute-done.1.cross
  42.4 3.7 %shard_map.62 = (f32[288,128]{1,0:T(8,128)S(1)}, f32[64,128]{1,0:T(8,128)S(1)}) custom-call(f32[9,32,128]{2,1,0:T(8,128)S(1)} %get-tuple-element.16.own, f32[2,9,32,128]{3,2,1,0:T(8,128)S(1)} %bitcast.8, f32[9,32,128]{2,1,0:T(8,128)S(1)} %collective-permute-done.1.cross, f32[9,16,128]{2,1,0:T(8,128)S(1)} %collective-permute-done.2.far), custom_call_target="tpu_custom_call" | custom-call | tf_op jit(solution)/shard_map/pallas_call | solution.py:448
  46.1 22.2 %all_to_all.16 = f32[64,1,128]{2,1,0:T(1,128)S(1)} all-to-all(f32[64,1,128]{2,1,0:T(1,128)S(1)} %bitcast.11), channel_id=1, replica_groups=mesh['gx0'=4,'gx1'=4,'gx2'=2,'gy'=3,'gz0'=4,'gz1'=2] {'gx0','gz0','gz1',..., dimensions={0} | all-to-all | bytes 65536 | tf_op jit(solution)/shard_map/all_to_all | solution.py:470
  68.2 0.1 shard_map.63
  68.3 12.8 %all_to_all.17.parts = f32[12,1,128]{2,1,0:T(1,128)S(1)} all-to-all(f32[12,1,128]{2,1,0:T(1,128)S(1)} %shard_map.63), channel_id=1, replica_groups=mesh['gx0'=4,'gx1'=4,'gx2'=2,'gy'=3,'gz0'=4,'gz1'=2] {'gy','gx1'}, dimensions={0} | all-to-all | bytes 12288 | tf_op jit(solution)/shard_map/all_to_all | solution.py:470
  81.1 0.9 %shard_map.64 = (f32[96,128]{1,0:T(8,128)}, f32[96,128]{1,0:T(8,128)}) custom-call(f32[288,128]{1,0:T(8,128)S(1)} %get-tuple-element.18.fields, f32[12,1,128]{2,1,0:T(1,128)S(1)} %all_to_all.17.parts), custom_call_target="tpu_custom_call" | custom-call | tf_op jit(solution)/shard_map/pallas_call | solution.py:448
  (2 shorter events, 0.0 us)
Async XLA Ops:
  1.9 7.1 %collective-permute-start = (f32[16,128]{1,0:T(8,128)S(1)}, f32[16,128]{1,0:T(8,128)S(1)}, u32[]{:S(2)}, u32[]{:S(2)}) collective-permute-start(f32[16,128]{1,0:T(8,128)S(1)} %get-tuple-element.13), channel_id=1, source_target_pairs={{1,2},{3,4},{5,6},{2,1},{4,3},{6,5},{9,10},{11,12},{13,14},{10,9},... | collective-permute-start | bytes 24584 | tf_op jit(solution)/shard_map/ppermute | solution.py:438
  29.7 12.7 %collective-permute-start.1 = (f32[9,32,128]{2,1,0:T(8,128)S(1)}, f32[9,32,128]{2,1,0:T(8,128)S(1)}, u32[]{:S(2)}, u32[]{:S(2)}) collective-permute-start(f32[9,32,128]{2,1,0:T(8,128)S(1)} %get-tuple-element.16.own), channel_id=1, source_target_pairs={{24,48},{72,96},{120,144},{168,192},{216,240},{264,288},{312,336},... | collective-permute-start | bytes 442376 | tf_op jit(solution)/shard_map/ppermute | solution.py:438
  37.2 5.1 %collective-permute-start.2 = (f32[9,16,128]{2,1,0:T(8,128)S(1)}, f32[9,16,128]{2,1,0:T(8,128)S(1)}, u32[]{:S(2)}, u32[]{:S(2)}) collective-permute-start(f32[9,16,128]{2,1,0:T(8,128)S(1)} %get-tuple-element.17), channel_id=1, source_target_pairs={{0,48},{24,72},{48,96},{72,120},{96,144},{120,168},{144,192},{168,... | collective-permute-start | bytes 221192 | tf_op jit(solution)/shard_map/ppermute | solution.py:433

commit v11 on v9

--- a/solution.py
+++ b/solution.py
@@ -454,7 +454,7 @@
     )(*kept)
 
 
-FIRST, SECOND = ("gy", "gx1", "gx2"), ("gx0", *GZ)
+FIRST, SECOND = ("gy", "gx1"), ("gx0", *GZ, "gx2")
 
 
 def members(axes):

time: 81.4 us -> 83.1 us (1.021)
  blocking collectives: 63.7 us -> 65.4 us
    all_to_all x2, blocking collectives: 34.6 us -> 36.4 us  [exchange(): parts = lax.all_to_all(value.reshape(-1, 1, 128), axes, 0, 0)]
where the time goes in v11:
time: 83.1 us; the launch traced here: 82.8 us
  blocking collectives  65.4 us (79%)
  starting transfers between devices  11.3 us (14%)
  Pallas kernels  5.38 us (6%)
    all_to_all x2, blocking collectives, exchange(): parts = lax.all_to_all(value.reshape(-1, 1, 128), axes, 0, 0)  36.4 us
    all_to_all x1, blocking collectives, on_device(): lax.all_to_all(slots, 'gy', 0, 0)  20.7 us
    ppermute x2, starting transfers between devices, swapped(): return lax.ppermute(value, axes, links + [(b, a) for a, b in links])  8.18 us
    all_gather x1, blocking collectives, on_device(): lax.all_gather(message, GZ[1])  6.39 us
    pallas_call x5, Pallas kernels, call(): pl.pallas_call(body, out_shape=tuple((place(o) for o in outs)), in_specs=...  4.08 us
    ppermute x1, starting transfers between devices, moved(): return lax.ppermute(value, axes, pairs)  3.1 us
    all_gather x1, blocking collectives, on_device(): pair = lax.all_gather(own, GX[2])  2.02 us
  transfers between devices with their start and end apart: 3, of which 0 were waited for; matrix products, arithmetic and copies ran while one was open for 0% of the time, Pallas kernels for 0%

profile of v11, /device:TPU:1, one launch (start us, length us, event | category | flops | bytes accessed | tf_op | source)
XLA Modules:
  0.0 82.8 jit_solution(2740480995197118143)
XLA Ops:
  0.6 1.3 %shard_map.59 = (f32[4,32,128]{2,1,0:T(8,128)S(1)}, f32[16,128]{1,0:T(8,128)S(1)}) custom-call(f32[6,12,192]{2,1,0:T(8,128)} %energy.1, f32[2,4,64]{2,1,0:T(4,128)} %density.1, s32[2,4,64]{2,1,0:T(4,128)} %region.1, f32[3]{0:T(128)} %gamma.1), custom_call_target="tpu_custom_call" | custom-call | tf_op jit(solution)/shard_map/pallas_call | solution.py:475
  1.9 0.7 collective-permute-start
  2.6 6.4 %all-gather = f32[32,128]{1,0:T(8,128)S(1)} all-gather(f32[16,128]{1,0:T(8,128)S(1)} %get-tuple-element.13), channel_id=2, replica_groups=mesh['gx0'=4,'gx1'=4,'gx2'=2,'gy'=3,'gz0'=4,'gz1'=2] {'gz1'}, dimensions={0}, use_global_device_ids=true | all-gather | bytes 24576 | tf_op jit(solution)/shard_map/all_gather | solution.py:486
  9.0 0.0 collective-permute-done.odd
  9.0 20.7 %all_to_all.15.slots = f32[3,96,128]{2,1,0:T(8,128)S(1)} all-to-all(f32[3,96,128]{2,1,0:T(8,128)S(1)} %get-tuple-element.15), channel_id=1, replica_groups=mesh['gx0'=4,'gx1'=4,'gx2'=2,'gy'=3,'gz0'=4,'gz1'=2] {'gy'}, dimensions={0} | all-to-all | bytes 294912 | tf_op jit(solution)/shard_map/all_to_all | solution.py:493
  29.7 7.5 %collective-permute-start.1 = (f32[9,32,128]{2,1,0:T(8,128)S(1)}, f32[9,32,128]{2,1,0:T(8,128)S(1)}, u32[]{:S(2)}, u32[]{:S(2)}) collective-permute-start(f32[9,32,128]{2,1,0:T(8,128)S(1)} %get-tuple-element.16.own), channel_id=1, source_target_pairs={{24,48},{72,96},{120,144},{168,192},{216,240},{264,288},{312,336},... | collective-permute-start | bytes 442376 | tf_op jit(solution)/shard_map/ppermute | solution.py:438
  37.2 3.1 %collective-permute-start.2 = (f32[9,16,128]{2,1,0:T(8,128)S(1)}, f32[9,16,128]{2,1,0:T(8,128)S(1)}, u32[]{:S(2)}, u32[]{:S(2)}) collective-permute-start(f32[9,16,128]{2,1,0:T(8,128)S(1)} %get-tuple-element.17), channel_id=1, source_target_pairs={{0,48},{24,72},{48,96},{72,120},{96,144},{120,168},{144,192},{168,... | collective-permute-start | bytes 221192 | tf_op jit(solution)/shard_map/ppermute | solution.py:433
  40.3 2.0 %all-gather.1 = f32[18,32,128]{2,1,0:T(8,128)S(1)} all-gather(f32[9,32,128]{2,1,0:T(8,128)S(1)} %get-tuple-element.16.own), channel_id=3, replica_groups=mesh['gx0'=4,'gx1'=4,'gx2'=2,'gy'=3,'gz0'=4,'gz1'=2] {'gx2'}, dimensions={0}, use_global_device_ids=true | all-gather | bytes 442368 | tf_op jit(solution)/shard_map/all_gather | solution.py:497
  42.4 0.0 collective-permute-done.2.far
  42.4 0.0 collective-permute-done.1.cross
  42.4 3.0 %shard_map.62 = (f32[288,128]{1,0:T(8,128)S(1)}, f32[12,1,128]{2,1,0:T(1,128)S(1)}) custom-call(f32[9,32,128]{2,1,0:T(8,128)S(1)} %get-tuple-element.16.own, f32[2,9,32,128]{3,2,1,0:T(8,128)S(1)} %bitcast.8, f32[9,32,128]{2,1,0:T(8,128)S(1)} %collective-permute-done.1.cross, f32[9,16,128]{2,1,0:T(8,128)S(1)} %collective-permute-done.2.far), custom_call_target="tpu_custom_call" | custom-call | tf_op jit(solution)/shard_map/pallas_call | solution.py:448
  45.4 14.5 %all_to_all.16.parts = f32[12,1,128]{2,1,0:T(1,128)S(1)} all-to-all(f32[12,1,128]{2,1,0:T(1,128)S(1)} %get-tuple-element.19), channel_id=1, replica_groups=mesh['gx0'=4,'gx1'=4,'gx2'=2,'gy'=3,'gz0'=4,'gz1'=2] {'gy','gx1'}, dimensions={0} | all-to-all | bytes 12288 | tf_op jit(solution)/shard_map/all_to_all | solution.py:470
  59.9 0.1 shard_map.63
  59.9 21.9 %all_to_all.17 = f32[64,1,128]{2,1,0:T(1,128)S(1)} all-to-all(f32[64,1,128]{2,1,0:T(1,128)S(1)} %bitcast.9), channel_id=1, replica_groups=mesh['gx0'=4,'gx1'=4,'gx2'=2,'gy'=3,'gz0'=4,'gz1'=2] {'gx0','gz0','gz1',..., dimensions={0} | all-to-all | bytes 65536 | tf_op jit(solution)/shard_map/all_to_all | solution.py:470
  81.8 0.9 %shard_map.64 = (f32[96,128]{1,0:T(8,128)}, f32[96,128]{1,0:T(8,128)}) custom-call(f32[288,128]{1,0:T(8,128)S(1)} %get-tuple-element.18.fields, f32[64,128]{1,0:T(8,128)S(1)} %bitcast.10), custom_call_target="tpu_custom_call" | custom-call | tf_op jit(solution)/shard_map/pallas_call | solution.py:448
  (2 shorter events, 0.0 us)
Async XLA Ops:
  1.9 7.1 %collective-permute-start = (f32[16,128]{1,0:T(8,128)S(1)}, f32[16,128]{1,0:T(8,128)S(1)}, u32[]{:S(2)}, u32[]{:S(2)}) collective-permute-start(f32[16,128]{1,0:T(8,128)S(1)} %get-tuple-element.13), channel_id=1, source_target_pairs={{1,2},{3,4},{5,6},{2,1},{4,3},{6,5},{9,10},{11,12},{13,14},{10,9},... | collective-permute-start | bytes 24584 | tf_op jit(solution)/shard_map/ppermute | solution.py:438
  29.7 12.7 %collective-permute-start.1 = (f32[9,32,128]{2,1,0:T(8,128)S(1)}, f32[9,32,128]{2,1,0:T(8,128)S(1)}, u32[]{:S(2)}, u32[]{:S(2)}) collective-permute-start(f32[9,32,128]{2,1,0:T(8,128)S(1)} %get-tuple-element.16.own), channel_id=1, source_target_pairs={{24,48},{72,96},{120,144},{168,192},{216,240},{264,288},{312,336},... | collective-permute-start | bytes 442376 | tf_op jit(solution)/shard_map/ppermute | solution.py:438
  37.2 5.1 %collective-permute-start.2 = (f32[9,16,128]{2,1,0:T(8,128)S(1)}, f32[9,16,128]{2,1,0:T(8,128)S(1)}, u32[]{:S(2)}, u32[]{:S(2)}) collective-permute-start(f32[9,16,128]{2,1,0:T(8,128)S(1)} %get-tuple-element.17), channel_id=1, source_target_pairs={{0,48},{24,72},{48,96},{72,120},{96,144},{120,168},{144,192},{168,... | collective-permute-start | bytes 221192 | tf_op jit(solution)/shard_map/ppermute | solution.py:433

commit v12 on v10

--- a/solution.py
+++ b/solution.py
@@ -13,7 +13,7 @@
 PAIRS = 14
 ROOT = math.sqrt(0.15)
 EDGE_W, MID_W = 5.0 / 18.0, 8.0 / 18.0
-UNROLL = (3, 1, 3)
+UNROLL = (9, 5, 3)
 GX = ("gx0", "gx1", "gx2")
 GZ = ("gz0", "gz1")
 

time: 82.3 us -> 86.7 us (1.053)
  Pallas kernels: 6.03 us -> 10.4 us
    pallas_call x5, Pallas kernels: 4.73 us -> 9.08 us  [call(): pl.pallas_call(body, out_shape=tuple((place(o) for o in outs)), in_specs=...]
where the time goes in v12:
time: 86.7 us; the launch traced here: 86.3 us
  blocking collectives  64 us (74%)
  starting transfers between devices  11.3 us (13%)
  Pallas kernels  10.4 us (12%)
    all_to_all x2, blocking collectives, exchange(): parts = lax.all_to_all(value.reshape(-1, 1, 128), axes, 0, 0)  34.9 us
    all_to_all x1, blocking collectives, on_device(): lax.all_to_all(slots, 'gy', 0, 0)  20.7 us
    pallas_call x5, Pallas kernels, call(): pl.pallas_call(body, out_shape=tuple((place(o) for o in outs)), in_specs=...  9.08 us
    ppermute x2, starting transfers between devices, swapped(): return lax.ppermute(value, axes, links + [(b, a) for a, b in links])  8.18 us
    all_gather x1, blocking collectives, on_device(): lax.all_gather(message, GZ[1])  6.39 us
    ppermute x1, starting transfers between devices, moved(): return lax.ppermute(value, axes, pairs)  3.1 us
    all_gather x1, blocking collectives, on_device(): pair = lax.all_gather(own, GX[2])  2.02 us
  transfers between devices with their start and end apart: 3, of which 0 were waited for; matrix products, arithmetic and copies ran while one was open for 0% of the time, Pallas kernels for 0%

profile of v12, /device:TPU:1, one launch (start us, length us, event | category | flops | bytes accessed | tf_op | source)
XLA Modules:
  0.0 86.3 jit_solution(10140866306052013599)
XLA Ops:
  0.6 1.3 %shard_map.59 = (f32[4,32,128]{2,1,0:T(8,128)S(1)}, f32[16,128]{1,0:T(8,128)S(1)}) custom-call(f32[6,12,192]{2,1,0:T(8,128)} %energy.1, f32[2,4,64]{2,1,0:T(4,128)} %density.1, s32[2,4,64]{2,1,0:T(4,128)} %region.1, f32[3]{0:T(128)} %gamma.1), custom_call_target="tpu_custom_call" | custom-call | tf_op jit(solution)/shard_map/pallas_call | solution.py:475
  1.9 0.7 collective-permute-start
  2.6 6.4 %all-gather = f32[32,128]{1,0:T(8,128)S(1)} all-gather(f32[16,128]{1,0:T(8,128)S(1)} %get-tuple-element.13), channel_id=2, replica_groups=mesh['gx0'=4,'gx1'=4,'gx2'=2,'gy'=3,'gz0'=4,'gz1'=2] {'gz1'}, dimensions={0}, use_global_device_ids=true | all-gather | bytes 24576 | tf_op jit(solution)/shard_map/all_gather | solution.py:486
  9.0 0.0 collective-permute-done.odd
  9.0 20.7 %all_to_all.15.slots = f32[3,96,128]{2,1,0:T(8,128)S(1)} all-to-all(f32[3,96,128]{2,1,0:T(8,128)S(1)} %get-tuple-element.15), channel_id=1, replica_groups=mesh['gx0'=4,'gx1'=4,'gx2'=2,'gy'=3,'gz0'=4,'gz1'=2] {'gy'}, dimensions={0} | all-to-all | bytes 294912 | tf_op jit(solution)/shard_map/all_to_all | solution.py:493
  29.7 7.5 %collective-permute-start.1 = (f32[9,32,128]{2,1,0:T(8,128)S(1)}, f32[9,32,128]{2,1,0:T(8,128)S(1)}, u32[]{:S(2)}, u32[]{:S(2)}) collective-permute-start(f32[9,32,128]{2,1,0:T(8,128)S(1)} %get-tuple-element.16.own), channel_id=1, source_target_pairs={{24,48},{72,96},{120,144},{168,192},{216,240},{264,288},{312,336},... | collective-permute-start | bytes 442376 | tf_op jit(solution)/shard_map/ppermute | solution.py:438
  37.2 3.1 %collective-permute-start.2 = (f32[9,16,128]{2,1,0:T(8,128)S(1)}, f32[9,16,128]{2,1,0:T(8,128)S(1)}, u32[]{:S(2)}, u32[]{:S(2)}) collective-permute-start(f32[9,16,128]{2,1,0:T(8,128)S(1)} %get-tuple-element.17), channel_id=1, source_target_pairs={{0,48},{24,72},{48,96},{72,120},{96,144},{120,168},{144,192},{168,... | collective-permute-start | bytes 221192 | tf_op jit(solution)/shard_map/ppermute | solution.py:433
  40.3 2.0 %all-gather.1 = f32[18,32,128]{2,1,0:T(8,128)S(1)} all-gather(f32[9,32,128]{2,1,0:T(8,128)S(1)} %get-tuple-element.16.own), channel_id=3, replica_groups=mesh['gx0'=4,'gx1'=4,'gx2'=2,'gy'=3,'gz0'=4,'gz1'=2] {'gx2'}, dimensions={0}, use_global_device_ids=true | all-gather | bytes 442368 | tf_op jit(solution)/shard_map/all_gather | solution.py:497
  42.4 0.0 collective-permute-done.2.far
  42.4 0.0 collective-permute-done.1.cross
  42.4 8.0 %shard_map.62 = (f32[288,128]{1,0:T(8,128)S(1)}, f32[64,128]{1,0:T(8,128)S(1)}) custom-call(f32[9,32,128]{2,1,0:T(8,128)S(1)} %get-tuple-element.16.own, f32[2,9,32,128]{3,2,1,0:T(8,128)S(1)} %bitcast.8, f32[9,32,128]{2,1,0:T(8,128)S(1)} %collective-permute-done.1.cross, f32[9,16,128]{2,1,0:T(8,128)S(1)} %collective-permute-done.2.far), custom_call_target="tpu_custom_call" | custom-call | tf_op jit(solution)/shard_map/pallas_call | solution.py:448
  50.4 22.2 %all_to_all.16 = f32[64,1,128]{2,1,0:T(1,128)S(1)} all-to-all(f32[64,1,128]{2,1,0:T(1,128)S(1)} %bitcast.11), channel_id=1, replica_groups=mesh['gx0'=4,'gx1'=4,'gx2'=2,'gy'=3,'gz0'=4,'gz1'=2] {'gx0','gz0','gz1',..., dimensions={0} | all-to-all | bytes 65536 | tf_op jit(solution)/shard_map/all_to_all | solution.py:470
  72.6 0.1 shard_map.63
  72.7 12.8 %all_to_all.17.parts = f32[12,1,128]{2,1,0:T(1,128)S(1)} all-to-all(f32[12,1,128]{2,1,0:T(1,128)S(1)} %shard_map.63), channel_id=1, replica_groups=mesh['gx0'=4,'gx1'=4,'gx2'=2,'gy'=3,'gz0'=4,'gz1'=2] {'gy','gx1'}, dimensions={0} | all-to-all | bytes 12288 | tf_op jit(solution)/shard_map/all_to_all | solution.py:470
  85.4 0.9 %shard_map.64 = (f32[96,128]{1,0:T(8,128)}, f32[96,128]{1,0:T(8,128)}) custom-call(f32[288,128]{1,0:T(8,128)S(1)} %get-tuple-element.18.fields, f32[12,1,128]{2,1,0:T(1,128)S(1)} %all_to_all.17.parts), custom_call_target="tpu_custom_call" | custom-call | tf_op jit(solution)/shard_map/pallas_call | solution.py:448
  (2 shorter events, 0.0 us)
Async XLA Ops:
  1.9 7.1 %collective-permute-start = (f32[16,128]{1,0:T(8,128)S(1)}, f32[16,128]{1,0:T(8,128)S(1)}, u32[]{:S(2)}, u32[]{:S(2)}) collective-permute-start(f32[16,128]{1,0:T(8,128)S(1)} %get-tuple-element.13), channel_id=1, source_target_pairs={{1,2},{3,4},{5,6},{2,1},{4,3},{6,5},{9,10},{11,12},{13,14},{10,9},... | collective-permute-start | bytes 24584 | tf_op jit(solution)/shard_map/ppermute | solution.py:438
  29.7 12.7 %collective-permute-start.1 = (f32[9,32,128]{2,1,0:T(8,128)S(1)}, f32[9,32,128]{2,1,0:T(8,128)S(1)}, u32[]{:S(2)}, u32[]{:S(2)}) collective-permute-start(f32[9,32,128]{2,1,0:T(8,128)S(1)} %get-tuple-element.16.own), channel_id=1, source_target_pairs={{24,48},{72,96},{120,144},{168,192},{216,240},{264,288},{312,336},... | collective-permute-start | bytes 442376 | tf_op jit(solution)/shard_map/ppermute | solution.py:438
  37.2 5.1 %collective-permute-start.2 = (f32[9,16,128]{2,1,0:T(8,128)S(1)}, f32[9,16,128]{2,1,0:T(8,128)S(1)}, u32[]{:S(2)}, u32[]{:S(2)}) collective-permute-start(f32[9,16,128]{2,1,0:T(8,128)S(1)} %get-tuple-element.17), channel_id=1, source_target_pairs={{0,48},{24,72},{48,96},{72,120},{96,144},{120,168},{144,192},{168,... | collective-permute-start | bytes 221192 | tf_op jit(solution)/shard_map/ppermute | solution.py:433
